TPU v7x, 32 devices: a whole 2x2x4 slice. The times are simulated.
32 devices in a mesh: row: 8 (over z, x), col: 4 (over y, core).
Axes of the slice: x: 2, y: 2, z: 4, core: 2. Of those that a mesh axis runs over, the one named last changes fastest.
Arguments:
- object_slices: float32 [2, 4, 2048, 1024], P(None, None, 'row', 'col'), may hold values from -1 to 1
- positions: int32 [8, 4, 2, 2], P('row', 'col'), may hold values from 0 to 128
- intensities: float32 [8, 4, 2, 256, 256], P('row', 'col'), may hold values from 0 to 0.8
- probe: float32 [2, 256, 256], replicated, may hold values from -6 to 6
- propagator: float32 [256, 256], replicated, may hold values from -3.140625 to 3.140625
Outputs:
- gradient: float32 [2, 4, 2048, 1024], P(None, None, 'row', 'col')
- updated: float32 [2, 4, 2048, 1024], P(None, None, 'row', 'col')
Inputs may be any that keep to these rules, and one draw needn't show every extreme that they name: `positions`: each probe window lies inside its tile widened by 64 pixels on every side.
All inputs are finite; a program needn't handle non-finite values.
Results may differ from a plain program's by a relative error of at most 0.0003.
Values sent between devices are 32-bit elements; how exact they have to be, the bound alone decides.
A program may use at most 128 MiB of HBM per device.

v0:
```python
import jax
import jax.numpy as jnp
from jax import lax
from jax.sharding import PartitionSpec as P

HALO = 64


descent_rate = 0.5


def passed_along(block, axis, distance):
    devices = range(lax.axis_size(axis))
    route = [((i - distance) % len(devices), i) for i in devices]
    return lax.ppermute(block, axis, route)


def with_halo(cells, sides, width):
    for axis, dim in sides:
        count = lax.axis_size(axis)
        head = lax.slice_in_dim(cells, 0, width, axis=dim)
        tail = lax.slice_in_dim(cells, cells.shape[dim] - width, cells.shape[dim], axis=dim)
        cells = jnp.concatenate(
            [
                lax.ppermute(tail, axis, [(i, (i + 1) % count) for i in range(count)]),
                cells,
                lax.ppermute(head, axis, [((i + 1) % count, i) for i in range(count)]),
            ],
            axis=dim,
        )
    return cells


def tables(width):
    counter = jnp.arange(width, dtype=jnp.int32)
    product = counter[:, None] * counter[None, :] % width
    angles = product.astype(jnp.float32) * (2.0 * jnp.pi / width)
    norming = 1.0 / jnp.sqrt(jnp.float32(width))
    return (jnp.cos(angles) * norming, jnp.sin(angles) * norming)


def apply_left(matrix, field):
    return jnp.einsum("ab,kbc->kac", matrix, field, precision=lax.Precision.HIGHEST)


def apply_right(field, matrix):
    return jnp.einsum("kab,bc->kac", field, matrix, precision=lax.Precision.HIGHEST)


def fourier(real_part, imag_part, cosines, sines, direction):
    half_re = apply_left(cosines, real_part) - direction * apply_left(sines, imag_part)
    half_im = apply_left(cosines, imag_part) + direction * apply_left(sines, real_part)
    full_re = apply_right(half_re, cosines) - direction * apply_right(half_im, sines)
    full_im = apply_right(half_im, cosines) + direction * apply_right(half_re, sines)
    return (full_re, full_im)


def complex_product(left_re, left_im, right_re, right_im):
    return (left_re * right_re - left_im * right_im, left_re * right_im + left_im * right_re)


def probe_gradients(windows, probe, propagator, measured):
    width = probe.shape[-1]
    layers = windows.shape[2]
    count = windows.shape[0]
    cosines, sines = tables(width)
    phase_re = jnp.cos(propagator)
    phase_im = jnp.sin(propagator)
    wave_re = jnp.broadcast_to(probe[0], (count, width, width))
    wave_im = jnp.broadcast_to(probe[1], (count, width, width))
    stored = []
    for layer in range(layers):
        stored.append((wave_re, wave_im))
        exit_re, exit_im = complex_product(
            wave_re, wave_im, windows[:, 0, layer], windows[:, 1, layer]
        )
        if layer < layers - 1:
            freq_re, freq_im = fourier(exit_re, exit_im, cosines, sines, -1.0)
            freq_re, freq_im = complex_product(freq_re, freq_im, phase_re, phase_im)
            wave_re, wave_im = fourier(freq_re, freq_im, cosines, sines, 1.0)
    far_re, far_im = fourier(exit_re, exit_im, cosines, sines, -1.0)
    misfit = far_re * far_re + far_im * far_im - measured
    back_re, back_im = fourier(misfit * far_re, misfit * far_im, cosines, sines, 1.0)
    real_terms = [None] * layers
    imag_terms = [None] * layers
    for layer in range(layers - 1, -1, -1):
        wave_re, wave_im = stored[layer]
        real_terms[layer] = wave_re * back_re + wave_im * back_im
        imag_terms[layer] = wave_re * back_im - wave_im * back_re
        if layer > 0:
            slab_re = windows[:, 0, layer]
            slab_im = windows[:, 1, layer]
            back_re, back_im = (
                slab_re * back_re + slab_im * back_im,
                slab_re * back_im - slab_im * back_re,
            )
            freq_re, freq_im = fourier(back_re, back_im, cosines, sines, -1.0)
            freq_re, freq_im = complex_product(freq_re, freq_im, phase_re, -phase_im)
            back_re, back_im = fourier(freq_re, freq_im, cosines, sines, 1.0)
    real_stack = jnp.stack(real_terms, axis=1)
    imag_stack = jnp.stack(imag_terms, axis=1)
    return jnp.stack([real_stack, imag_stack], axis=1)


def fold_rows(summed):
    extent = summed.shape[2]
    inner = extent - 2 * HALO
    from_below = passed_along(summed[:, :, :HALO], "row", -1)
    from_above = passed_along(summed[:, :, extent - HALO :], "row", 1)
    middle = summed[:, :, HALO : extent - HALO]
    middle = middle.at[:, :, inner - HALO :].add(from_below)
    return middle.at[:, :, :HALO].add(from_above)


def fold_cols(summed):
    extent = summed.shape[3]
    inner = extent - 2 * HALO
    from_right = passed_along(summed[:, :, :, :HALO], "col", -1)
    from_left = passed_along(summed[:, :, :, extent - HALO :], "col", 1)
    middle = summed[:, :, :, HALO : extent - HALO]
    middle = middle.at[:, :, :, inner - HALO :].add(from_right)
    return middle.at[:, :, :, :HALO].add(from_left)


def on_device(object_slices, positions, intensities, probe, propagator):
    extended = with_halo(object_slices, (("row", 2), ("col", 3)), HALO)
    width = probe.shape[-1]
    layers = object_slices.shape[1]
    offsets = positions[0, 0]
    window_shape = (2, layers, width, width)
    anchor = jnp.zeros((), jnp.int32)

    def cut_window(offset):
        return lax.dynamic_slice(extended, (anchor, anchor, offset[0], offset[1]), window_shape)

    windows = jax.vmap(cut_window)(offsets)
    terms = probe_gradients(windows, probe, propagator, intensities[0, 0])

    def add_one(index, running):
        offset = offsets[index]
        start = (anchor, anchor, offset[0], offset[1])
        current = lax.dynamic_slice(running, start, window_shape)
        return lax.dynamic_update_slice(running, current + terms[index], start)

    summed = lax.fori_loop(0, terms.shape[0], add_one, jnp.zeros_like(extended))
    gradient = fold_cols(fold_rows(summed))
    return (gradient, object_slices - descent_rate * gradient)


def solution(mesh):
    return jax.shard_map(
        on_device,
        mesh=mesh,
        in_specs=(
            P(None, None, "row", "col"),
            P("row", "col", None, None),
            P("row", "col", None, None, None),
            P(),
            P(),
        ),
        out_specs=(P(None, None, "row", "col"), P(None, None, "row", "col")),
        check_vma=False,
    )
```

profile of v0, /device:TPU:1, one launch (start us, length us, event | category | flops | bytes accessed | tf_op | source)
XLA Modules:
  0.0 438.9 jit_solution(10680784427912786373)
XLA Ops:
  0.6 2.3 fusion.819
  2.9 2.0 collective-permute-start
  4.9 3.0 collective-permute-start.1
  8.0 1.9 copy.261
  9.9 17.2 %collective-permute-done = f32[2,4,64,256]{3,2,1,0:T(8,128)} collective-permute-done((f32[2,4,64,256]{3,2,1,0:T(8,128)}, f32[2,4,64,256]{3,2,1,0:T(8,128)}, u32[]{:S(2)}, u32[]{:S(2)}) %collective-permute-start) | collective-permute-done | bytes 524320 | tf_op jit(solution)/shard_map/ppermute | solution.py:25
  27.1 2.4 copy.260
  30.8 3.0 pad_maximum_fusion.4
  33.8 2.7 collective-permute-start.2
  38.7 14.6 %collective-permute-done.2 = f32[2,4,384,64]{2,3,1,0:T(8,128)} collective-permute-done((f32[2,4,384,64]{2,3,1,0:T(8,128)}, f32[2,4,384,64]{2,3,1,0:T(8,128)}, u32[]{:S(2)}, u32[]{:S(2)}) %collective-permute-start.2) | collective-permute-done | bytes 786464 | tf_op jit(solution)/shard_map/ppermute | solution.py:25
  54.8 4.6 %pad_maximum_fusion = f32[2,4,384,384]{2,3,1,0:T(8,128)} fusion(f32[2,4,384,64]{2,3,1,0:T(8,128)} %collective-permute-done.3, f32[2,4,64,256]{2,3,1,0:T(8,128)} %copy.262, f32[2,4,256,256]{2,3,1,0:T(8,128)S(1)} %copy.261, f32[2,4,64,256]{2,3,1,0:T(8,128)} %copy.260, f32[2,4,384,64]{2,3,1,0:T(8,128)} %collective-permute-done.2), kind=kLoop, calls=%fused_computation.5 | loop fusion | flops 4718592 | bytes 9437184 | tf_op jit(solution)/shard_map/concatenate | solution.py:23
  59.4 18.5 %while.19 = (s32[]{:T(128)}, f32[2,4,384,384]{2,3,1,0:T(8,128)}, s32[2,4]{1,0:T(2,128)S(1)}, f32[2,2,4,256,256]{4,3,0,2,1:T(8,128)}, s32[]{:T(128)}) while((s32[]{:T(128)}, f32[2,4,384,384]{2,3,1,0:T(8,128)}, s32[2,4]{1,0:T(2,128)S(1)}, f32[2,2,4,256,256]{4,3,0,2,1:T(8,128)}, s32[]{:T(128)}) %tuple.98), condition=%wide.while_cond.4, body=%wide.while_body.4.sunk | while | flops 2 | bytes 12583545 | solution.py:134
  60.0 3.6 constant_dynamic-slice_fusion.8
  65.4 3.1 bitcast_dynamic-update-slice_fusion.2
  69.1 3.8 constant_dynamic-slice_fusion.8
  74.8 3.1 bitcast_dynamic-update-slice_fusion.2
  78.0 3.2 fusion.242
  81.2 3.1 fusion.238
  84.3 3.1 fusion.55
  89.2 1.9 fusion.53
  93.0 2.0 fusion.51
  104.4 2.2 fusion.232
  115.9 2.0 fusion.47
  127.1 2.1 fusion.214
  140.3 2.3 fusion.61
  151.8 2.0 fusion.204
  163.2 2.1 fusion.32
  170.8 1.9 fusion.58
  176.3 2.2 fusion.31
  187.8 2.1 fusion.186
  189.8 1.9 fusion.182
  191.8 1.9 fusion.25
  193.7 1.9 fusion.24
  199.3 2.1 convolution_add_fusion.6
  201.4 2.0 add_bitcast_fusion
  210.8 2.2 fusion.21
  224.2 2.1 fusion.16
  231.9 2.0 add_bitcast_fusion.1
  235.8 2.0 fusion.158
  247.0 2.3 fusion.10
  258.7 2.0 fusion.152
  262.6 2.0 add_bitcast_fusion.2
  272.0 2.1 fusion.5
  283.4 2.3 fusion.1
  295.3 2.4 pad_maximum_fusion.1
  297.8 2.5 broadcast_in_dim.6
  300.3 58.3 %while.18 = (s32[]{:T(128)}, f32[2,4,384,384]{3,2,1,0:T(8,128)}, s32[2,2]{1,0:T(2,128)S(1)}, f32[2,2,4,256,256]{4,3,0,2,1:T(8,128)}, s32[]{:T(128)}, /*index=5*/s32[]{:T(128)}, s32[]{:T(128)}) while((s32[]{:T(128)}, f32[2,4,384,384]{3,2,1,0:T(8,128)}, s32[2,2]{1,0:T(2,128)S(1)}, f32[2,2,4,256,256]{4,3,0,2,1:T(8,128)}, s32[]{:T(128)}, ...), condition=%wide.region_1.2_spmd, body=%wide.region_0.1_spmd.sunk | while | flops 524296 | bytes 10485957 | solution.py:145
  305.0 3.1 bitcast_add_fusion.2
  308.1 20.6 %dynamic_update_slice.8 = f32[2,4,384,384]{3,2,1,0:T(8,128)} dynamic-update-slice(f32[2,4,384,384]{3,2,1,0:T(8,128)} %get-tuple-element.306, f32[2,4,256,256]{3,2,1,0:T(8,128)S(1)} %bitcast_add_fusion.2, s32[]{:T(128)} %constant.153.clone.1..sunk, s32[]{:T(128)} %constant.153.clone.1..sunk, s32[]{:T(128)S(6)} %select_n.625, s32[]{:T(128)S(6)} %select_n.626) | dynamic-update-slice | bytes 4194308 | tf_op jit(solution)/shard_map/while/body/eval_jaxpr/dynamic_update_slice | solution.py:143
  333.3 3.2 bitcast_add_fusion.2
  336.4 22.2 %dynamic_update_slice.8 = f32[2,4,384,384]{3,2,1,0:T(8,128)} dynamic-update-slice(f32[2,4,384,384]{3,2,1,0:T(8,128)} %get-tuple-element.306, f32[2,4,256,256]{3,2,1,0:T(8,128)S(1)} %bitcast_add_fusion.2, s32[]{:T(128)} %constant.153.clone.1..sunk, s32[]{:T(128)} %constant.153.clone.1..sunk, s32[]{:T(128)S(6)} %select_n.625, s32[]{:T(128)S(6)} %select_n.626) | dynamic-update-slice | bytes 4194308 | tf_op jit(solution)/shard_map/while/body/eval_jaxpr/dynamic_update_slice | solution.py:143
  360.1 7.4 %collective-permute-start.4 = (f32[2,4,64,384]{3,2,1,0:T(8,128)S(1)}, f32[2,4,64,384]{3,2,1,0:T(8,128)S(1)}, u32[]{:S(2)}, u32[]{:S(2)}) collective-permute-start(f32[2,4,64,384]{3,2,1,0:T(8,128)S(1)} %get-tuple-element.193), channel_id=1, source_target_pairs={{4,0},{8,4},{12,8},{16,12},{20,16},{24,20},{28,24},{0,28},{5,1},{9... | collective-permute-start | bytes 2359304 | tf_op jit(solution)/shard_map/ppermute | solution.py:15
  367.5 2.1 slice.222
  369.6 27.2 %collective-permute-done.4 = f32[2,4,64,384]{3,2,1,0:T(8,128)S(1)} collective-permute-done((f32[2,4,64,384]{3,2,1,0:T(8,128)S(1)}, f32[2,4,64,384]{3,2,1,0:T(8,128)S(1)}, u32[]{:S(2)}, u32[]{:S(2)}) %collective-permute-start.4) | collective-permute-done | bytes 786464 | tf_op jit(solution)/shard_map/ppermute | solution.py:15
  399.9 2.4 copy.385
  403.4 2.4 copy.387
  405.8 2.0 collective-permute-start.7
  407.8 1.9 slice.252
  409.7 5.2 %collective-permute-done.6 = f32[2,4,256,64]{2,3,1,0:T(8,128)} collective-permute-done((f32[2,4,256,64]{2,3,1,0:T(8,128)}, f32[2,4,256,64]{2,3,1,0:T(8,128)}, u32[]{:S(2)}, u32[]{:S(2)}) %collective-permute-start.6) | collective-permute-done | bytes 524320 | tf_op jit(solution)/shard_map/ppermute | solution.py:15
  414.9 2.4 copy.386
  417.3 2.3 slice_add_fusion.1
  419.6 6.5 %scatter-add.16 = f32[2,4,256,256]{3,2,1,0:T(8,128)} dynamic-update-slice(f32[2,4,256,256]{3,2,1,0:T(8,128)} %slice.252, f32[2,4,256,64]{3,2,1,0:T(8,128)} %slice_add_fusion.1, s32[]{:T(128)} %constant.153.clone.1, s32[]{:T(128)} %constant.153.clone.1, s32[]{:T(128)} %constant.153.clone.1, s32[]{:T(128)} %constant.161.clone.1) | dynamic-update-slice | bytes 1048580 | tf_op jit(solution)/shard_map/scatter-add | solution.py:121
  426.0 2.5 copy.388
  430.2 4.5 %scatter-add.19 = f32[2,4,256,256]{3,2,1,0:T(8,128)S(1)} dynamic-update-slice(f32[2,4,256,256]{3,2,1,0:T(8,128)S(1)} %copy-done, f32[2,4,256,64]{3,2,1,0:T(8,128)S(1)} %slice_add_fusion, s32[]{:T(128)} %constant.153.clone.1, s32[]{:T(128)} %constant.153.clone.1, s32[]{:T(128)} %constant.153.clone.1, s32[]{:T(128)} %constant.153.clone.1) | dynamic-update-slice | bytes 1048580 | tf_op jit(solution)/shard_map/scatter-add | solution.py:122
  434.8 3.9 multiply_subtract_fusion
  (128 shorter events, 173.8 us)
Async XLA Ops:
  2.9 24.2 %collective-permute-start = (f32[2,4,64,256]{3,2,1,0:T(8,128)}, f32[2,4,64,256]{3,2,1,0:T(8,128)}, u32[]{:S(2)}, u32[]{:S(2)}) collective-permute-start(f32[2,4,64,256]{3,2,1,0:T(8,128)} %get-tuple-element.204), channel_id=1, source_target_pairs={{0,4},{4,8},{8,12},{12,16},{16,20},{20,24},{24,28},{28,0},{1,5},{5... | collective-permute-start | bytes 1572872 | tf_op jit(solution)/shard_map/ppermute | solution.py:25
  4.9 24.5 %collective-permute-start.1 = (f32[2,4,64,256]{3,2,1,0:T(8,128)}, f32[2,4,64,256]{3,2,1,0:T(8,128)S(1)}, u32[]{:S(2)}, u32[]{:S(2)}) collective-permute-start(f32[2,4,64,256]{3,2,1,0:T(8,128)} %get-tuple-element.205), channel_id=1, source_target_pairs={{4,0},{8,4},{12,8},{16,12},{20,16},{24,20},{28,24},{0,28},{5,1},{9... | collective-permute-start | bytes 1572872 | tf_op jit(solution)/shard_map/ppermute | solution.py:27
  30.8 5.7 %copy-start.4 = (f32[256,256]{1,0:T(8,128)S(1)}, f32[256,256]{1,0:T(8,128)}, u32[]{:S(2)}) copy-start(f32[256,256]{1,0:T(8,128)} %param.19) | copy-start | bytes 786436
  30.8 6.7 %copy-start.5 = (s32[1,1,2,2]{3,2,1,0:T(2,128)S(1)}, s32[1,1,2,2]{3,2,1,0:T(2,128)}, u32[]{:S(2)}) copy-start(s32[1,1,2,2]{3,2,1,0:T(2,128)} %param.16) | copy-start | bytes 52
  33.8 19.5 %collective-permute-start.2 = (f32[2,4,384,64]{2,3,1,0:T(8,128)}, f32[2,4,384,64]{2,3,1,0:T(8,128)}, u32[]{:S(2)}, u32[]{:S(2)}) collective-permute-start(f32[2,4,384,64]{2,3,1,0:T(8,128)} %get-tuple-element.194), channel_id=1, source_target_pairs={{0,1},{1,2},{2,3},{3,0},{4,5},{5,6},{6,7},{7,4},{8,9},{9,10},{10,1... | collective-permute-start | bytes 2359304 | tf_op jit(solution)/shard_map/ppermute | solution.py:25
  36.5 18.3 %collective-permute-start.3 = (f32[2,4,384,64]{2,3,1,0:T(8,128)}, f32[2,4,384,64]{2,3,1,0:T(8,128)}, u32[]{:S(2)}, u32[]{:S(2)}) collective-permute-start(f32[2,4,384,64]{2,3,1,0:T(8,128)} %get-tuple-element.195), channel_id=1, source_target_pairs={{1,0},{2,1},{3,2},{0,3},{5,4},{6,5},{7,6},{4,7},{9,8},{10,9},{11,1... | collective-permute-start | bytes 2359304 | tf_op jit(solution)/shard_map/ppermute | solution.py:27
  78.0 11.2 %copy-start.3 = (f32[2,2,4,256,256]{4,3,0,2,1:T(8,128)S(1)}, f32[2,2,4,256,256]{4,3,0,2,1:T(8,128)}, u32[]{:S(2)}) copy-start(f32[2,2,4,256,256]{4,3,0,2,1:T(8,128)} %get-tuple-element.137) | copy-start | bytes 12582916
  180.4 7.4 %copy-start.2 = (f32[1,1,2,256,256]{4,3,2,1,0:T(8,128)S(1)}, f32[1,1,2,256,256]{4,3,2,1,0:T(8,128)}, u32[]{:S(2)}) copy-start(f32[1,1,2,256,256]{4,3,2,1,0:T(8,128)} %param.17) | copy-start | bytes 1572868
  360.1 36.7 %collective-permute-start.4 = (f32[2,4,64,384]{3,2,1,0:T(8,128)S(1)}, f32[2,4,64,384]{3,2,1,0:T(8,128)S(1)}, u32[]{:S(2)}, u32[]{:S(2)}) collective-permute-start(f32[2,4,64,384]{3,2,1,0:T(8,128)S(1)} %get-tuple-element.193), channel_id=1, source_target_pairs={{4,0},{8,4},{12,8},{16,12},{20,16},{24,20},{28,24},{0,28},{5,1},{9... | collective-permute-start | bytes 2359304 | tf_op jit(solution)/shard_map/ppermute | solution.py:15
  367.5 30.5 %collective-permute-start.5 = (f32[2,4,64,384]{3,2,1,0:T(8,128)S(1)}, f32[2,4,64,384]{3,2,1,0:T(8,128)S(1)}, u32[]{:S(2)}, u32[]{:S(2)}) collective-permute-start(f32[2,4,64,384]{3,2,1,0:T(8,128)S(1)} %get-tuple-element.192), channel_id=1, source_target_pairs={{28,0},{0,4},{4,8},{8,12},{12,16},{16,20},{20,24},{24,28},{29,1},{... | collective-permute-start | bytes 2359304 | tf_op jit(solution)/shard_map/ppermute | solution.py:15
  402.2 12.7 %collective-permute-start.6 = (f32[2,4,256,64]{2,3,1,0:T(8,128)}, f32[2,4,256,64]{2,3,1,0:T(8,128)}, u32[]{:S(2)}, u32[]{:S(2)}) collective-permute-start(f32[2,4,256,64]{2,3,1,0:T(8,128)} %copy.385), channel_id=1, source_target_pairs={{1,0},{2,1},{3,2},{0,3},{5,4},{6,5},{7,6},{4,7},{9,8},{10,9},{11,1... | collective-permute-start | bytes 1572872 | tf_op jit(solution)/shard_map/ppermute | solution.py:15
  405.8 20.2 %collective-permute-start.7 = (f32[2,4,256,64]{2,3,1,0:T(8,128)}, f32[2,4,256,64]{2,3,1,0:T(8,128)}, u32[]{:S(2)}, u32[]{:S(2)}) collective-permute-start(f32[2,4,256,64]{2,3,1,0:T(8,128)} %copy.387), channel_id=1, source_target_pairs={{3,0},{0,1},{1,2},{2,3},{7,4},{4,5},{5,6},{6,7},{11,8},{8,9},{9,10... | collective-permute-start | bytes 1572872 | tf_op jit(solution)/shard_map/ppermute | solution.py:15
  426.0 4.2 copy-start
  434.8 4.0 copy-start.1
where the time goes:
time: 447 us; the launch traced here: 439 us
  matrix products  216 us (48%)
  local copies, waits for them, and re-layouts  103 us (23%)
  waiting for transfers between devices  65.7 us (15%)
  other arithmetic  26.3 us (6%)
  starting transfers between devices  18.3 us (4%)
  loops' own time  8.13 us (2%)
    dot_general x56, matrix products, apply_left(): jnp.einsum('ab,kbc->kac', matrix, field, precision=lax.Precision.HIGHEST)  110 us
    dot_general x56, matrix products, apply_right(): jnp.einsum('kab,bc->kac', field, matrix, precision=lax.Precision.HIGHEST)  106 us
    dynamic_update_slice x2, local copies, waits for them, and re-layouts, add_one(): return lax.dynamic_update_slice(running, current + terms[index], start)  42.8 us
    ppermute x4, waiting for transfers between devices, passed_along(): return lax.ppermute(block, axis, route)  32.4 us
    ppermute x2, waiting for transfers between devices, with_halo(): lax.ppermute(tail, axis, [(i, (i + 1) % count) for i in range(count)])  31.8 us
    gather x10, local copies, waits for them, and re-layouts  18.4 us
    ppermute x4, starting transfers between devices, passed_along(): return lax.ppermute(block, axis, route)  10.6 us
  transfers between devices with their start and end apart: 8, of which 5 were waited for; matrix products, arithmetic and copies ran while one was open for 6% of the time, Pallas kernels for 0%

commit v1 on v0

v1 whole, which is shorter than its diff:
```python
import jax
import jax.numpy as jnp
import numpy as np
from jax import lax
from jax.experimental import pallas as pl
from jax.experimental.pallas import tpu as pltpu
from jax.sharding import PartitionSpec as P

HALO = 64


descent_rate = 0.5


def split(value):
    high = value.astype(jnp.bfloat16)
    low = (value - high.astype(jnp.float32)).astype(jnp.bfloat16)
    return high, low


def half_tables(width):
    half = width // 2
    place = np.arange(half)
    found = []
    for odd in (0, 1):
        angle = 2.0 * np.pi * (np.outer(2 * place + odd, place) % width) / width
        re = np.cos(angle) / np.sqrt(width)
        im = -np.sin(angle) / np.sqrt(width)
        found.append(np.block([[re, -im], [im, re]]).astype(np.float32))
    even, odd = found
    four = np.stack([even, odd, even.T, odd.T])
    high = four.astype(jnp.bfloat16)
    low = (four - high.astype(np.float32)).astype(jnp.bfloat16)
    lefts = np.concatenate([high, high, low], axis=2)
    rights = np.concatenate([np.swapaxes(high, 1, 2), np.swapaxes(high, 1, 2), np.swapaxes(low, 1, 2)], axis=1)
    return lefts, rights


def dot_left(matrix, value):
    high, low = split(value)
    return jnp.dot(matrix, jnp.concatenate([high, low, high], 0), preferred_element_type=jnp.float32)


def dot_right(value, matrix):
    high, low = split(value)
    return jnp.dot(jnp.concatenate([high, low, high], 1), matrix, preferred_element_type=jnp.float32)


def cut(value, dim):
    half = value.shape[dim] // 2
    return (lax.slice_in_dim(value, 0, half, axis=dim), lax.slice_in_dim(value, half, 2 * half, axis=dim))


def joined(first, second, dim):
    return jnp.concatenate([first, second], dim)


def forward_axis(re, im, dim, dot, even_matrix, odd_matrix):
    r0, r1 = cut(re, dim)
    i0, i1 = cut(im, dim)
    even_re, even_im = cut(dot(joined(r0 + r1, i0 + i1, dim), even_matrix), dim)
    odd_re, odd_im = cut(dot(joined(r0 - r1, i0 - i1, dim), odd_matrix), dim)
    return joined(even_re, odd_re, dim), joined(even_im, odd_im, dim)


def inverse_axis(re, im, dim, dot, even_matrix, odd_matrix):
    r0, r1 = cut(re, dim)
    i0, i1 = cut(im, dim)
    p_re, p_im = cut(dot(joined(r0, i0, dim), even_matrix), dim)
    q_re, q_im = cut(dot(joined(r1, i1, dim), odd_matrix), dim)
    return joined(p_re + q_re, p_re - q_re, dim), joined(p_im + q_im, p_im - q_im, dim)


def left_dot(value, matrix):
    return dot_left(matrix, value)


def forward(re, im, lefts, rights):
    re, im = forward_axis(re, im, 0, left_dot, lefts[0], lefts[1])
    return forward_axis(re, im, 1, dot_right, rights[0], rights[1])


def inverse(re, im, lefts, rights):
    re, im = inverse_axis(re, im, 1, dot_right, rights[2], rights[3])
    return inverse_axis(re, im, 0, left_dot, lefts[2], lefts[3])


def by_parity(array, dim):
    return jnp.concatenate(
        [
            lax.slice_in_dim(array, 0, array.shape[dim], stride=2, axis=dim),
            lax.slice_in_dim(array, 1, array.shape[dim], stride=2, axis=dim),
        ],
        axis=dim,
    )


def complex_product(left_re, left_im, right_re, right_im):
    return (left_re * right_re - left_im * right_im, left_re * right_im + left_im * right_re)


def slid(whole, shift, axis, span):
    turned = pltpu.roll(whole, lax.rem(span - shift, span), axis)
    kept = lax.broadcasted_iota(jnp.int32, whole[:-1].shape, axis) < span - shift
    return jnp.where(kept, turned[:-1], turned[1:])


def spread(whole, shift, axis, span):
    turned = pltpu.roll(whole, lax.rem(shift, span), axis)
    zero = jnp.zeros_like(turned[:1])
    first = jnp.concatenate([zero, turned], 0)
    other = jnp.concatenate([turned, zero], 0)
    moved = lax.broadcasted_iota(jnp.int32, first.shape, axis) < shift
    return jnp.where(moved, first, other)


def row_place(oy, rows, width):
    base = jnp.minimum(oy - lax.rem(oy, 8), rows - width - 8)
    return pl.ds(pl.multiple_of(base, 8), width + 8), oy - base


def lane_blocks(value):
    return jnp.stack([value[:, at : at + 128] for at in range(0, value.shape[1], 128)])


def lane_joined(blocks):
    return jnp.concatenate([blocks[i] for i in range(blocks.shape[0])], 1)


def take_window(whole, shift, ox):
    rows, lanes = whole.shape
    whole = slid(whole.reshape(rows // 8, 8, lanes), shift, 1, 8).reshape(rows - 8, lanes)
    return lane_joined(slid(lane_blocks(whole), ox, 2, 128))


def widened(term, shift, ox):
    term = lane_joined(spread(lane_blocks(term), ox, 2, 128))
    rows, lanes = term.shape
    return spread(term.reshape(rows // 8, 8, lanes), shift, 1, 8).reshape(rows + 8, lanes)


def step_kernel(offsets, ext, measured, probe, phase, lefts, rights, out, windows, waves):
    count = measured.shape[0]
    width = measured.shape[-1]
    layers = ext.shape[1]
    last = layers - 1
    out[...] = jnp.zeros_like(out)
    for k in range(count):
        waves[k, 0] = probe[...]

    def cut_layer(k, layer):
        rows, shift = row_place(offsets[k, 0], ext.shape[2], width)
        for c in range(2):
            windows[k, layer, c] = take_window(ext[c, layer, rows, :], shift, offsets[k, 1])

    def leave(k, layer):
        return complex_product(
            waves[k, layer, 0], waves[k, layer, 1], windows[k, layer, 0], windows[k, layer, 1]
        )

    def onward(layer, carry):
        for k in range(count):
            cut_layer(k, layer)
            re, im = forward(*leave(k, layer), lefts, rights)
            re, im = complex_product(re, im, phase[0], phase[1])
            re, im = inverse(re, im, lefts, rights)
            waves[k, layer + 1, 0] = re
            waves[k, layer + 1, 1] = im
        return carry

    lax.fori_loop(0, last, onward, 0)

    def record(k, layer, back_re, back_im):
        wave_re, wave_im = waves[k, layer, 0], waves[k, layer, 1]
        rows, shift = row_place(offsets[k, 0], ext.shape[2], width)
        re_term = wave_re * back_re + wave_im * back_im
        im_term = wave_re * back_im - wave_im * back_re
        out[0, layer, rows, :] += widened(re_term, shift, offsets[k, 1])
        out[1, layer, rows, :] += widened(im_term, shift, offsets[k, 1])

    for k in range(count):
        cut_layer(k, last)
        far_re, far_im = forward(*leave(k, last), lefts, rights)
        misfit = far_re * far_re + far_im * far_im - measured[k]
        back_re, back_im = inverse(misfit * far_re, misfit * far_im, lefts, rights)
        record(k, last, back_re, back_im)
        waves[k, last, 0] = back_re
        waves[k, last, 1] = back_im

    def backward(step, carry):
        layer = last - step
        for k in range(count):
            back_re, back_im = waves[k, layer, 0], waves[k, layer, 1]
            slab_re, slab_im = windows[k, layer, 0], windows[k, layer, 1]
            re, im = complex_product(back_re, back_im, slab_re, -slab_im)
            re, im = forward(re, im, lefts, rights)
            re, im = complex_product(re, im, phase[0], -phase[1])
            re, im = inverse(re, im, lefts, rights)
            record(k, layer - 1, re, im)
            waves[k, layer - 1, 0] = re
            waves[k, layer - 1, 1] = im
        return carry

    lax.fori_loop(0, last, backward, 0)


def window_sums(extended, offsets, measured, probe, propagator):
    count = measured.shape[0]
    width = measured.shape[-1]
    layers = extended.shape[1]
    lefts, rights = half_tables(width)
    ordered = by_parity(by_parity(propagator, 0), 1)
    phase = jnp.stack([jnp.cos(ordered), jnp.sin(ordered)])
    measured = by_parity(by_parity(measured, 1), 2)
    vmem = pl.BlockSpec(memory_space=pltpu.VMEM)
    return pl.pallas_call(
        step_kernel,
        out_shape=jax.ShapeDtypeStruct(extended.shape, jnp.float32),
        in_specs=[pl.BlockSpec(memory_space=pltpu.SMEM)] + [vmem] * 6,
        out_specs=vmem,
        scratch_shapes=[
            pltpu.VMEM((count, layers, 2, width, width), jnp.float32),
            pltpu.VMEM((count, layers, 2, width, width), jnp.float32),
        ],
        compiler_params=pltpu.CompilerParams(vmem_limit_bytes=50 * 2**20),
    )(offsets, extended, measured, probe, phase, jnp.asarray(lefts), jnp.asarray(rights))


def passed_along(block, axis, distance):
    devices = range(lax.axis_size(axis))
    route = [((i - distance) % len(devices), i) for i in devices]
    return lax.ppermute(block, axis, route)


def with_halo(cells, sides, width):
    for axis, dim in sides:
        count = lax.axis_size(axis)
        head = lax.slice_in_dim(cells, 0, width, axis=dim)
        tail = lax.slice_in_dim(cells, cells.shape[dim] - width, cells.shape[dim], axis=dim)
        cells = jnp.concatenate(
            [
                lax.ppermute(tail, axis, [(i, (i + 1) % count) for i in range(count)]),
                cells,
                lax.ppermute(head, axis, [((i + 1) % count, i) for i in range(count)]),
            ],
            axis=dim,
        )
    return cells


def fold_rows(summed):
    extent = summed.shape[2]
    inner = extent - 2 * HALO
    from_below = passed_along(summed[:, :, :HALO], "row", -1)
    from_above = passed_along(summed[:, :, extent - HALO :], "row", 1)
    middle = summed[:, :, HALO : extent - HALO]
    middle = middle.at[:, :, inner - HALO :].add(from_below)
    return middle.at[:, :, :HALO].add(from_above)


def fold_cols(summed):
    extent = summed.shape[3]
    inner = extent - 2 * HALO
    from_right = passed_along(summed[:, :, :, :HALO], "col", -1)
    from_left = passed_along(summed[:, :, :, extent - HALO :], "col", 1)
    middle = summed[:, :, :, HALO : extent - HALO]
    middle = middle.at[:, :, :, inner - HALO :].add(from_right)
    return middle.at[:, :, :, :HALO].add(from_left)


def on_device(object_slices, positions, intensities, probe, propagator):
    extended = with_halo(object_slices, (("row", 2), ("col", 3)), HALO)
    summed = window_sums(extended, positions[0, 0], intensities[0, 0], probe, propagator)
    gradient = fold_cols(fold_rows(summed))
    return (gradient, object_slices - descent_rate * gradient)


def solution(mesh):
    return jax.shard_map(
        on_device,
        mesh=mesh,
        in_specs=(
            P(None, None, "row", "col"),
            P("row", "col", None, None),
            P("row", "col", None, None, None),
            P(),
            P(),
        ),
        out_specs=(P(None, None, "row", "col"), P(None, None, "row", "col")),
        check_vma=False,
    )
```

time: 447 us -> 181 us (0.40); the launches traced: 439 us -> 180 us
  matrix products: 216 us -> 0 us
  local copies, waits for them, and re-layouts: 103 us -> 63.8 us
  Pallas kernels: 0 us -> 26.3 us
  other arithmetic: 26.3 us -> 15.8 us
  loops' own time: 8.13 us -> 0 us
  waiting for transfers between devices: 65.7 us -> 60.2 us
  starting transfers between devices: 18.3 us -> 13.4 us
    dot_general x112 -> x0, matrix products: 216 us -> none  [the longest x56 110 us: apply_left(): jnp.einsum('ab,kbc->kac', matrix, field, precision=lax.Precision.HIGHEST)]
    dynamic_update_slice x2 -> x0, local copies, waits for them, and re-layouts: 42.8 us -> none  [add_one(): return lax.dynamic_update_slice(running, current + terms[index], start)]
    slice x2 -> x10, local copies, waits for them, and re-layouts: 1.17 us -> 31.6 us  [the longest x4 14.4 us: by_parity(): lax.slice_in_dim(array, 0, array.shape[dim], stride=2, axis=dim)]
    pallas_call x0 -> x1, Pallas kernels: none -> 26.3 us  [window_sums(): pl.pallas_call(step_kernel, out_shape=jax.ShapeDtypeStruct(extended.shape...]
    gather x10 -> x0, local copies, waits for them, and re-layouts: 18.4 us -> none
    ppermute x2, waiting for transfers between devices: 31.8 us -> 18.7 us  [with_halo(): lax.ppermute(tail, axis, [(i, (i + 1) % count) for i in range(count)])]
    another operation x2 -> x0, loops' own time: 8.13 us -> none  [the longest x1 7.97 us: on_device(): summed = lax.fori_loop(0, terms.shape[0], add_one, jnp.zeros_like(extended))]
    ppermute x4, waiting for transfers between devices: 32.4 us -> 39.7 us  [passed_along(): return lax.ppermute(block, axis, route)]
  transfers between devices with their start and end apart: 8 -> 8, of which waited for: 5 -> 4; matrix products, arithmetic and copies ran while one was open for 6% -> 26% of each run, Pallas kernels for 0% -> 0%
where the time goes in v1:
time: 181 us; the launch traced here: 180 us
  local copies, waits for them, and re-layouts  63.8 us (35%)
  waiting for transfers between devices  60.2 us (33%)
  Pallas kernels  26.3 us (15%)
  other arithmetic  15.8 us (9%)
  starting transfers between devices  13.4 us (7%)
    ppermute x4, waiting for transfers between devices, passed_along(): return lax.ppermute(block, axis, route)  39.7 us
    pallas_call x1, Pallas kernels, window_sums(): pl.pallas_call(step_kernel, out_shape=jax.ShapeDtypeStruct(extended.shape...  26.3 us
    ppermute x2, waiting for transfers between devices, with_halo(): lax.ppermute(tail, axis, [(i, (i + 1) % count) for i in range(count)])  18.7 us
    slice x4, local copies, waits for them, and re-layouts, by_parity(): lax.slice_in_dim(array, 0, array.shape[dim], stride=2, axis=dim)  14.4 us
    slice x4, local copies, waits for them, and re-layouts, by_parity(): lax.slice_in_dim(array, 1, array.shape[dim], stride=2, axis=dim)  14.4 us
    scatter-add x1, local copies, waits for them, and re-layouts, fold_cols(): middle = middle.at[:, :, :, inner - HALO:].add(from_right)  6.46 us
    concatenate x1, other arithmetic, with_halo(): jnp.concatenate([lax.ppermute(tail, axis, [(i, (i + 1) % count) for i in...  6.32 us
    ppermute x4, starting transfers between devices, passed_along(): return lax.ppermute(block, axis, route)  5.24 us
  transfers between devices with their start and end apart: 8, of which 4 were waited for; matrix products, arithmetic and copies ran while one was open for 26% of the time, Pallas kernels for 0%

profile of v1, /device:TPU:1, one launch (start us, length us, event | category | flops | bytes accessed | tf_op | source)
XLA Modules:
  0.0 180.3 jit_solution(11423636333208392038)
XLA Ops:
  0.6 0.0 copy-start.7
  0.6 1.4 fusion.7
  2.1 2.1 %collective-permute-start = (f32[2,4,64,256]{3,2,1,0:T(8,128)S(1)}, f32[2,4,64,256]{3,2,1,0:T(8,128)S(1)}, u32[]{:S(2)}, u32[]{:S(2)}) collective-permute-start(f32[2,4,64,256]{3,2,1,0:T(8,128)S(1)} %get-tuple-element.57), channel_id=1, source_target_pairs={{0,4},{4,8},{8,12},{12,16},{16,20},{20,24},{24,28},{28,0},{1,5},{5... | collective-permute-start | bytes 1572872 | tf_op jit(solution)/shard_map/ppermute | solution.py:242
  4.2 3.1 %collective-permute-start.1 = (f32[2,4,64,256]{3,2,1,0:T(8,128)S(1)}, f32[2,4,64,256]{3,2,1,0:T(8,128)S(1)}, u32[]{:S(2)}, u32[]{:S(2)}) collective-permute-start(f32[2,4,64,256]{3,2,1,0:T(8,128)S(1)} %get-tuple-element.56), channel_id=1, source_target_pairs={{4,0},{8,4},{12,8},{16,12},{20,16},{24,20},{28,24},{0,28},{5,1},{9... | collective-permute-start | bytes 1572872 | tf_op jit(solution)/shard_map/ppermute | solution.py:244
  7.3 18.7 %collective-permute-done = f32[2,4,64,256]{3,2,1,0:T(8,128)S(1)} collective-permute-done((f32[2,4,64,256]{3,2,1,0:T(8,128)S(1)}, f32[2,4,64,256]{3,2,1,0:T(8,128)S(1)}, u32[]{:S(2)}, u32[]{:S(2)}) %collective-permute-start) | collective-permute-done | bytes 524320 | tf_op jit(solution)/shard_map/ppermute | solution.py:242
  26.0 0.0 copy-done.7
  26.1 0.1 constant_dynamic-update-slice_fusion.1
  26.2 1.7 collective-permute-done.1
  28.0 0.0 copy-start.4
  28.0 0.5 fusion.6
  28.5 1.1 copy-done.4
  29.6 1.3 copy.10
  30.9 0.0 copy-start.8
  30.9 1.8 %collective-permute-start.3 = (f32[2,4,384,64]{2,3,1,0:T(8,128)}, f32[2,4,384,64]{2,3,1,0:T(8,128)S(1)}, u32[]{:S(2)}, u32[]{:S(2)}) collective-permute-start(f32[2,4,384,64]{2,3,1,0:T(8,128)} %copy.10), channel_id=1, source_target_pairs={{1,0},{2,1},{3,2},{0,3},{5,4},{6,5},{7,6},{4,7},{9,8},{10,9},{11,1... | collective-permute-start | bytes 2359304 | tf_op jit(solution)/shard_map/ppermute | solution.py:244
  32.8 1.3 copy.9
  34.1 1.1 collective-permute-start.2
  35.2 1.0 slice.181
  36.2 1.0 slice.180
  37.3 4.5 %slice.183 = f32[256,128]{1,0:T(8,128)S(1)} slice(f32[256,256]{1,0:T(8,128)S(1)} %pad_maximum_fusion.4), slice={[0:256:1], [1:256:2]} | slice | bytes 262144 | tf_op jit(solution)/shard_map/slice | solution.py:92
  41.8 4.5 %slice.182 = f32[256,128]{1,0:T(8,128)S(1)} slice(f32[256,256]{1,0:T(8,128)S(1)} %pad_maximum_fusion.4), slice={[0:256:1], [0:256:2]} | slice | bytes 262144 | tf_op jit(solution)/shard_map/slice | solution.py:91
  46.3 0.0 copy-done.8
  46.3 0.1 slice.177
  46.4 0.1 slice.176
  46.6 8.8 %slice.179 = f32[2,256,128]{2,1,0:T(8,128)S(1)} slice(f32[2,256,256]{2,1,0:T(8,128)S(1)} %pad_maximum_fusion.1), slice={[0:2:1], [0:256:1], [1:256:2]} | slice | bytes 524288 | tf_op jit(solution)/shard_map/slice | solution.py:92
  55.4 8.8 %slice.178 = f32[2,256,128]{2,1,0:T(8,128)S(1)} slice(f32[2,256,256]{2,1,0:T(8,128)S(1)} %pad_maximum_fusion.1), slice={[0:2:1], [0:256:1], [0:256:2]} | slice | bytes 524288 | tf_op jit(solution)/shard_map/slice | solution.py:91
  64.2 1.1 fusion.3
  65.4 0.1 pad_maximum_fusion.2
  65.5 0.0 collective-permute-done.3
  65.5 0.5 copy.12
  66.0 0.0 collective-permute-done.2
  66.0 2.8 %copy.11 = f32[2,4,384,64]{3,2,1,0:T(8,128)} copy(f32[2,4,384,64]{2,3,1,0:T(8,128)} %collective-permute-done.2) | data formatting | bytes 1572864 | tf_op jit(solution)/shard_map/ppermute | solution.py:242
  68.7 0.0 copy-start
  68.7 6.3 %pad_maximum_fusion.ext = f32[2,4,384,384]{3,2,1,0:T(8,128)} fusion(f32[2,4,384,64]{3,2,1,0:T(8,128)S(1)} %copy.12, f32[2,4,384,256]{3,2,1,0:T(8,128)} %copy-done.4, f32[2,4,384,64]{3,2,1,0:T(8,128)} %copy.11), kind=kLoop, calls=%fused_computation | loop fusion | flops 2359296 | bytes 9437184 | tf_op jit(solution)/shard_map/concatenate | solution.py:240
  75.0 0.0 copy-done
  75.0 0.0 copy-done.1
  75.0 0.0 copy-done.2
  75.1 26.3 %shard_map.86 = f32[2,4,384,384]{3,2,1,0:T(8,128)} custom-call(s32[2,2]{1,0:T(2,128)S(1)} %bitcast.4, f32[2,4,384,384]{3,2,1,0:T(8,128)} %pad_maximum_fusion.ext, f32[2,256,256]{2,1,0:T(8,128)S(1)} %get-tuple-element.60.measured, f32[2,256,256]{2,1,0:T(8,128)S(1)} %copy-done.1, f32[2,256,256]{2,1,0:T(8,128)S(1)} %get-tuple-element.61.phase, ...), custom_call_target="tpu_custom_call" | custom-call | tf_op jit(solution)/shard_map/pallas_call | solution.py:216
  101.3 1.6 fusion.4
  103.0 3.5 %collective-permute-start.4 = (f32[2,4,64,384]{3,2,1,0:T(8,128)S(1)}, f32[2,4,64,384]{3,2,1,0:T(8,128)S(1)}, u32[]{:S(2)}, u32[]{:S(2)}) collective-permute-start(f32[2,4,64,384]{3,2,1,0:T(8,128)S(1)} %get-tuple-element.51), channel_id=1, source_target_pairs={{4,0},{8,4},{12,8},{16,12},{20,16},{24,20},{28,24},{0,28},{5,1},{9... | collective-permute-start | bytes 2359304 | tf_op jit(solution)/shard_map/ppermute | solution.py:232
  106.5 0.0 collective-permute-start.5
  106.5 33.0 %collective-permute-done.4 = f32[2,4,64,384]{3,2,1,0:T(8,128)S(1)} collective-permute-done((f32[2,4,64,384]{3,2,1,0:T(8,128)S(1)}, f32[2,4,64,384]{3,2,1,0:T(8,128)S(1)}, u32[]{:S(2)}, u32[]{:S(2)}) %collective-permute-start.4) | collective-permute-done | bytes 786464 | tf_op jit(solution)/shard_map/ppermute | solution.py:232
  139.4 0.0 copy-done.3
  139.4 0.0 slice-done
  139.4 0.1 fusion.1
  139.5 0.0 collective-permute-done.5
  139.5 0.2 fusion
  139.7 1.6 fusion.5
  141.4 2.4 %copy.13 = f32[2,4,256,64]{2,3,1,0:T(8,128)} copy(f32[2,4,256,64]{3,2,1,0:T(8,128)} %get-tuple-element.53) | data formatting | bytes 1048576 | tf_op jit(solution)/shard_map/slice | solution.py:264
  143.7 0.4 collective-permute-start.6
  144.1 2.3 %copy.15 = f32[2,4,256,64]{2,3,1,0:T(8,128)} copy(f32[2,4,256,64]{3,2,1,0:T(8,128)} %get-tuple-element.52) | data formatting | bytes 1048576 | tf_op jit(solution)/shard_map/slice | solution.py:265
  146.4 1.4 collective-permute-start.7
  147.8 1.9 %slice.201 = f32[2,4,256,256]{3,2,1,0:T(8,128)} slice(f32[2,4,256,384]{3,2,1,0:T(8,128)S(1)} %fusion), slice={[0:2], [0:4], [0:256], [64:320]} | slice | bytes 4194304 | tf_op jit(solution)/shard_map/slice | solution.py:266
  149.7 6.8 %collective-permute-done.6 = f32[2,4,256,64]{2,3,1,0:T(8,128)} collective-permute-done((f32[2,4,256,64]{2,3,1,0:T(8,128)}, f32[2,4,256,64]{2,3,1,0:T(8,128)}, u32[]{:S(2)}, u32[]{:S(2)}) %collective-permute-start.6) | collective-permute-done | bytes 524320 | tf_op jit(solution)/shard_map/ppermute | solution.py:232
  156.5 2.4 %copy.14 = f32[2,4,256,64]{3,2,1,0:T(8,128)} copy(f32[2,4,256,64]{2,3,1,0:T(8,128)} %collective-permute-done.6) | data formatting | bytes 1048576 | tf_op jit(solution)/shard_map/ppermute | solution.py:232
  158.9 2.3 %slice_add_fusion.1 = f32[2,4,256,64]{3,2,1,0:T(8,128)} fusion(f32[2,4,256,64]{3,2,1,0:T(8,128)} %copy.14, f32[2,4,256,384]{3,2,1,0:T(8,128)S(1)} %fusion), kind=kLoop, calls=%fused_computation.3 | loop fusion | flops 131072 | bytes 1572864 | tf_op jit(solution)/shard_map/add | solution.py:267
  161.2 6.5 %scatter-add.16 = f32[2,4,256,256]{3,2,1,0:T(8,128)} dynamic-update-slice(f32[2,4,256,256]{3,2,1,0:T(8,128)} %slice.201, f32[2,4,256,64]{3,2,1,0:T(8,128)} %slice_add_fusion.1, s32[]{:T(128)} %constant.109.clone.1, s32[]{:T(128)} %constant.109.clone.1, s32[]{:T(128)} %constant.109.clone.1, s32[]{:T(128)} %constant.110.clone.1) | dynamic-update-slice | bytes 1048580 | tf_op jit(solution)/shard_map/scatter-add | solution.py:267
  167.6 0.0 collective-permute-done.7
  167.6 2.5 %copy.16 = f32[2,4,256,64]{3,2,1,0:T(8,128)} copy(f32[2,4,256,64]{2,3,1,0:T(8,128)} %collective-permute-done.7) | data formatting | bytes 1048576 | tf_op jit(solution)/shard_map/ppermute | solution.py:232
  170.1 1.6 slice_add_fusion
  171.8 0.0 copy-done.5
  171.8 4.5 %scatter-add.19 = f32[2,4,256,256]{3,2,1,0:T(8,128)S(1)} dynamic-update-slice(f32[2,4,256,256]{3,2,1,0:T(8,128)S(1)} %copy-done.5, f32[2,4,256,64]{3,2,1,0:T(8,128)S(1)} %slice_add_fusion, s32[]{:T(128)} %constant.109.clone.1, s32[]{:T(128)} %constant.109.clone.1, s32[]{:T(128)} %constant.109.clone.1, s32[]{:T(128)} %constant.109.clone.1) | dynamic-update-slice | bytes 1048580 | tf_op jit(solution)/shard_map/scatter-add | solution.py:268
  176.3 0.0 copy-start.6
  176.3 3.9 %multiply_subtract_fusion = f32[2,4,256,256]{3,2,1,0:T(8,128)} fusion(f32[2,4,256,256]{3,2,1,0:T(8,128)} %param.15, f32[2,4,256,256]{3,2,1,0:T(8,128)S(1)} %scatter-add.19), kind=kLoop, calls=%fused_computation.1 | loop fusion | flops 1048576 | bytes 6291456 | tf_op jit(solution)/shard_map/sub | solution.py:275
  180.3 0.0 copy-done.6
  (9 shorter events, 0.1 us)
Async XLA Ops:
  0.6 25.4 %copy-start.7 = (f32[2,4,256,256]{3,2,1,0:T(8,128)S(1)}, f32[2,4,256,256]{3,2,1,0:T(8,128)}, u32[]{:S(2)}) copy-start(f32[2,4,256,256]{3,2,1,0:T(8,128)} %param.15) | copy-start | bytes 6291460
  2.1 23.9 %collective-permute-start = (f32[2,4,64,256]{3,2,1,0:T(8,128)S(1)}, f32[2,4,64,256]{3,2,1,0:T(8,128)S(1)}, u32[]{:S(2)}, u32[]{:S(2)}) collective-permute-start(f32[2,4,64,256]{3,2,1,0:T(8,128)S(1)} %get-tuple-element.57), channel_id=1, source_target_pairs={{0,4},{4,8},{8,12},{12,16},{16,20},{20,24},{24,28},{28,0},{1,5},{5... | collective-permute-start | bytes 1572872 | tf_op jit(solution)/shard_map/ppermute | solution.py:242
  4.2 23.8 %collective-permute-start.1 = (f32[2,4,64,256]{3,2,1,0:T(8,128)S(1)}, f32[2,4,64,256]{3,2,1,0:T(8,128)S(1)}, u32[]{:S(2)}, u32[]{:S(2)}) collective-permute-start(f32[2,4,64,256]{3,2,1,0:T(8,128)S(1)} %get-tuple-element.56), channel_id=1, source_target_pairs={{4,0},{8,4},{12,8},{16,12},{20,16},{24,20},{28,24},{0,28},{5,1},{9... | collective-permute-start | bytes 1572872 | tf_op jit(solution)/shard_map/ppermute | solution.py:244
  28.0 1.6 copy-start.4
  30.9 15.3 %copy-start.8 = (f32[1,1,2,256,256]{4,3,2,1,0:T(8,128)S(1)}, f32[1,1,2,256,256]{4,3,2,1,0:T(8,128)}, u32[]{:S(2)}) copy-start(f32[1,1,2,256,256]{4,3,2,1,0:T(8,128)} %param.17) | copy-start | bytes 1572868
  30.9 34.5 %collective-permute-start.3 = (f32[2,4,384,64]{2,3,1,0:T(8,128)}, f32[2,4,384,64]{2,3,1,0:T(8,128)S(1)}, u32[]{:S(2)}, u32[]{:S(2)}) collective-permute-start(f32[2,4,384,64]{2,3,1,0:T(8,128)} %copy.10), channel_id=1, source_target_pairs={{1,0},{2,1},{3,2},{0,3},{5,4},{6,5},{7,6},{4,7},{9,8},{10,9},{11,1... | collective-permute-start | bytes 2359304 | tf_op jit(solution)/shard_map/ppermute | solution.py:244
  34.1 31.9 %collective-permute-start.2 = (f32[2,4,384,64]{2,3,1,0:T(8,128)}, f32[2,4,384,64]{2,3,1,0:T(8,128)}, u32[]{:S(2)}, u32[]{:S(2)}) collective-permute-start(f32[2,4,384,64]{2,3,1,0:T(8,128)} %copy.9), channel_id=1, source_target_pairs={{0,1},{1,2},{2,3},{3,0},{4,5},{5,6},{6,7},{7,4},{8,9},{9,10},{10,1... | collective-permute-start | bytes 2359304 | tf_op jit(solution)/shard_map/ppermute | solution.py:242
  68.7 6.3 %copy-start = (bf16[4,256,768]{2,1,0:T(8,128)(2,1)S(1)}, bf16[4,256,768]{2,1,0:T(8,128)(2,1)}, u32[]{:S(2)}) copy-start(bf16[4,256,768]{2,1,0:T(8,128)(2,1)} %constant.112.clone.lefts) | copy-start | bytes 4718596
  68.7 6.3 %copy-start.1 = (f32[2,256,256]{2,1,0:T(8,128)S(1)}, f32[2,256,256]{2,1,0:T(8,128)}, u32[]{:S(2)}) copy-start(f32[2,256,256]{2,1,0:T(8,128)} %probe.1) | copy-start | bytes 1572868
  68.7 6.3 %copy-start.2 = (s32[1,1,2,2]{3,2,1,0:T(2,128)S(1)}, s32[1,1,2,2]{3,2,1,0:T(2,128)}, u32[]{:S(2)}) copy-start(s32[1,1,2,2]{3,2,1,0:T(2,128)} %param.16) | copy-start | bytes 52
  101.3 38.1 %copy-start.3 = (f32[2,4,384,384]{3,2,1,0:T(8,128)S(1)}, f32[2,4,384,384]{3,2,1,0:T(8,128)}, u32[]{:S(2)}) copy-start(f32[2,4,384,384]{3,2,1,0:T(8,128)} %shard_map.86) | copy-start | bytes 14155780
  103.0 36.5 %collective-permute-start.4 = (f32[2,4,64,384]{3,2,1,0:T(8,128)S(1)}, f32[2,4,64,384]{3,2,1,0:T(8,128)S(1)}, u32[]{:S(2)}, u32[]{:S(2)}) collective-permute-start(f32[2,4,64,384]{3,2,1,0:T(8,128)S(1)} %get-tuple-element.51), channel_id=1, source_target_pairs={{4,0},{8,4},{12,8},{16,12},{20,16},{24,20},{28,24},{0,28},{5,1},{9... | collective-permute-start | bytes 2359304 | tf_op jit(solution)/shard_map/ppermute | solution.py:232
  106.4 33.0 %slice-start = ((f32[2,4,384,384]{3,2,1,0:T(8,128)}), f32[2,4,256,384]{3,2,1,0:T(8,128)S(1)}, s32[]{:S(2)}) async-start(f32[2,4,384,384]{3,2,1,0:T(8,128)} %shard_map.86), calls=%async_computation | async-start | bytes 6291456 | tf_op jit(solution)/shard_map/slice | solution.py:256
  106.5 33.1 %collective-permute-start.5 = (f32[2,4,64,384]{3,2,1,0:T(8,128)S(1)}, f32[2,4,64,384]{3,2,1,0:T(8,128)S(1)}, u32[]{:S(2)}, u32[]{:S(2)}) collective-permute-start(f32[2,4,64,384]{3,2,1,0:T(8,128)S(1)} %get-tuple-element.50), channel_id=1, source_target_pairs={{28,0},{0,4},{4,8},{8,12},{12,16},{16,20},{20,24},{24,28},{29,1},{... | collective-permute-start | bytes 2359304 | tf_op jit(solution)/shard_map/ppermute | solution.py:232
  143.7 12.8 %collective-permute-start.6 = (f32[2,4,256,64]{2,3,1,0:T(8,128)}, f32[2,4,256,64]{2,3,1,0:T(8,128)}, u32[]{:S(2)}, u32[]{:S(2)}) collective-permute-start(f32[2,4,256,64]{2,3,1,0:T(8,128)} %copy.13), channel_id=1, source_target_pairs={{1,0},{2,1},{3,2},{0,3},{5,4},{6,5},{7,6},{4,7},{9,8},{10,9},{11,1... | collective-permute-start | bytes 1572872 | tf_op jit(solution)/shard_map/ppermute | solution.py:232
  146.4 21.2 %collective-permute-start.7 = (f32[2,4,256,64]{2,3,1,0:T(8,128)}, f32[2,4,256,64]{2,3,1,0:T(8,128)}, u32[]{:S(2)}, u32[]{:S(2)}) collective-permute-start(f32[2,4,256,64]{2,3,1,0:T(8,128)} %copy.15), channel_id=1, source_target_pairs={{3,0},{0,1},{1,2},{2,3},{7,4},{4,5},{5,6},{6,7},{11,8},{8,9},{9,10... | collective-permute-start | bytes 1572872 | tf_op jit(solution)/shard_map/ppermute | solution.py:232
  167.6 4.2 %copy-start.5 = (f32[2,4,256,256]{3,2,1,0:T(8,128)S(1)}, f32[2,4,256,256]{3,2,1,0:T(8,128)}, u32[]{:S(2)}) copy-start(f32[2,4,256,256]{3,2,1,0:T(8,128)} %scatter-add.16) | copy-start | bytes 6291460
  176.3 4.0 %copy-start.6 = (f32[2,4,256,256]{3,2,1,0:T(8,128)}, f32[2,4,256,256]{3,2,1,0:T(8,128)S(1)}, u32[]{:S(2)}) copy-start(f32[2,4,256,256]{3,2,1,0:T(8,128)S(1)} %scatter-add.19) | copy-start | bytes 6291460

commit v2 on v1

v2 whole, which is shorter than its diff:
```python
import jax
import jax.numpy as jnp
import numpy as np
from jax import lax
from jax.experimental import pallas as pl
from jax.experimental.pallas import tpu as pltpu
from jax.sharding import PartitionSpec as P

HALO = 64


descent_rate = 0.5


def passed_along(block, axis, distance):
    devices = range(lax.axis_size(axis))
    route = [((i - distance) % len(devices), i) for i in devices]
    return lax.ppermute(block, axis, route)


def split(value):
    high = value.astype(jnp.bfloat16)
    low = (value - high.astype(jnp.float32)).astype(jnp.bfloat16)
    return high, low


def half_tables(width):
    half = width // 2
    place = np.arange(half)
    found = []
    for odd in (0, 1):
        angle = 2.0 * np.pi * (np.outer(2 * place + odd, place) % width) / width
        re = np.cos(angle) / np.sqrt(width)
        im = -np.sin(angle) / np.sqrt(width)
        found.append(np.block([[re, -im], [im, re]]).astype(np.float32))
    even, odd = found
    order = np.eye(width, dtype=np.float32)[np.concatenate([2 * place, 2 * place + 1])]
    six = np.stack([even, odd, even.T, odd.T, order, order.T])
    high = six.astype(jnp.bfloat16)
    low = (six - high.astype(np.float32)).astype(jnp.bfloat16)
    return np.stack([high, low])


def dot_left(pair, value):
    high, low = split(value)
    matrix = jnp.concatenate([pair[0], pair[0], pair[1]], 1)
    return jnp.dot(matrix, jnp.concatenate([high, low, high], 0), preferred_element_type=jnp.float32)


def dot_right(value, pair):
    high, low = split(value)
    matrix = jnp.concatenate([pair[0], pair[0], pair[1]], 0)
    return jnp.dot(jnp.concatenate([high, low, high], 1), matrix, preferred_element_type=jnp.float32)


def cut(value, dim):
    half = value.shape[dim] // 2
    return (lax.slice_in_dim(value, 0, half, axis=dim), lax.slice_in_dim(value, half, 2 * half, axis=dim))


def joined(first, second, dim):
    return jnp.concatenate([first, second], dim)


def forward_axis(re, im, dim, dot, even_matrix, odd_matrix):
    r0, r1 = cut(re, dim)
    i0, i1 = cut(im, dim)
    even_re, even_im = cut(dot(joined(r0 + r1, i0 + i1, dim), even_matrix), dim)
    odd_re, odd_im = cut(dot(joined(r0 - r1, i0 - i1, dim), odd_matrix), dim)
    return joined(even_re, odd_re, dim), joined(even_im, odd_im, dim)


def inverse_axis(re, im, dim, dot, even_matrix, odd_matrix):
    r0, r1 = cut(re, dim)
    i0, i1 = cut(im, dim)
    p_re, p_im = cut(dot(joined(r0, i0, dim), even_matrix), dim)
    q_re, q_im = cut(dot(joined(r1, i1, dim), odd_matrix), dim)
    return joined(p_re + q_re, p_re - q_re, dim), joined(p_im + q_im, p_im - q_im, dim)


def left_dot(value, pair):
    return dot_left(pair, value)


def forward(re, im, pairs):
    re, im = forward_axis(re, im, 0, left_dot, pairs(0), pairs(1))
    return forward_axis(re, im, 1, dot_right, pairs(2), pairs(3))


def inverse(re, im, pairs):
    re, im = inverse_axis(re, im, 1, dot_right, pairs(0), pairs(1))
    return inverse_axis(re, im, 0, left_dot, pairs(2), pairs(3))


def by_parity(value, pairs):
    return dot_right(dot_left(pairs(4), value), pairs(5))


def complex_product(left_re, left_im, right_re, right_im):
    return (left_re * right_re - left_im * right_im, left_re * right_im + left_im * right_re)


def slid(whole, shift, axis, span):
    turned = pltpu.roll(whole, lax.rem(span - shift, span), axis)
    kept = lax.broadcasted_iota(jnp.int32, whole[:-1].shape, axis) < span - shift
    return jnp.where(kept, turned[:-1], turned[1:])


def spread(whole, shift, axis, span):
    turned = pltpu.roll(whole, lax.rem(shift, span), axis)
    zero = jnp.zeros_like(turned[:1])
    first = jnp.concatenate([zero, turned], 0)
    other = jnp.concatenate([turned, zero], 0)
    moved = lax.broadcasted_iota(jnp.int32, first.shape, axis) < shift
    return jnp.where(moved, first, other)


def row_place(oy, rows, width):
    base = jnp.minimum(oy - lax.rem(oy, 8), rows - width - 8)
    return pl.ds(pl.multiple_of(base, 8), width + 8), oy - base


def lane_place(ox, lanes=128):
    early = ox < HALO
    return jnp.where(early, 2, 0), jnp.where(early, ox + lanes - HALO, ox - HALO)


def swapped(value):
    return pltpu.roll(value, HALO, value.ndim - 1)


def lower_lanes(value):
    return lax.broadcasted_iota(jnp.int32, value.shape, value.ndim - 1) < HALO


def step_kernel(
    offsets, core, edges, right, left, right_ends, left_ends, measured, probe, phase, tables,
    out, out_edges, to_right, to_left, to_right_ends, to_left_ends,
    ext, total, windows, waves, ordered, phases,
):
    count = measured.shape[0]
    width = measured.shape[-1]
    layers = core.shape[1]
    last = layers - 1
    tall = core.shape[2]
    wide = core.shape[3] // 128
    rounds = wide + 1
    whole = tall + 2 * HALO
    pieces = ((0, HALO, True, 0), (HALO, tall, False, 0), (HALO + tall, HALO, True, HALO))

    def pairs(index):
        return tables[0, index], tables[1, index]

    def gather(layer, carry):
        for start, size, is_edge, at in pieces:
            rows, own = pl.ds(start, size), pl.ds(at, size)
            for c in range(2):
                source = edges if is_edge else core
                for j in range(wide):
                    ext[c, layer, j, rows, :] = source[c, layer, own, pl.ds(j * 128, 128)]
            r = (right_ends if is_edge else right)[layer, own, :]
            l = (left_ends if is_edge else left)[layer, own, :]
            low = lower_lanes(r)
            ext[0, layer, wide, rows, :] = jnp.where(low, r, swapped(l))
            ext[1, layer, wide, rows, :] = jnp.where(low, swapped(r), l)
        return carry

    lax.fori_loop(0, layers, gather, 0)
    total[...] = jnp.zeros_like(total)
    for c in range(2):
        phases[c] = by_parity(phase[c], pairs)
    for k in range(count):
        waves[k, 0] = probe[...]
        ordered[k] = by_parity(measured[k], pairs)

    def cut_layer(k, layer):
        rows, shift = row_place(offsets[k, 0], whole, width)
        first, turn = lane_place(offsets[k, 1])
        for c in range(2):
            blocks = jnp.stack(
                [ext[c, layer, lax.rem(first + j, rounds), rows, :] for j in range(rounds)]
            )
            blocks = slid(blocks, turn, 2, 128)
            for j in range(wide):
                part = blocks[j].reshape((width + 8) // 8, 8, 128)
                windows[k, layer, c, :, j * 128 : j * 128 + 128] = slid(part, shift, 1, 8).reshape(width, 128)

    def leave(k, layer):
        return complex_product(
            waves[k, layer, 0], waves[k, layer, 1], windows[k, layer, 0], windows[k, layer, 1]
        )

    def onward(layer, carry):
        for k in range(count):
            cut_layer(k, layer)
            re, im = forward(*leave(k, layer), pairs)
            re, im = complex_product(re, im, phases[0], phases[1])
            re, im = inverse(re, im, pairs)
            waves[k, layer + 1, 0] = re
            waves[k, layer + 1, 1] = im
        return carry

    lax.fori_loop(0, last, onward, 0)

    def record(k, layer, back_re, back_im):
        wave_re, wave_im = waves[k, layer, 0], waves[k, layer, 1]
        rows, shift = row_place(offsets[k, 0], whole, width)
        first, turn = lane_place(offsets[k, 1])
        terms = (wave_re * back_re + wave_im * back_im, wave_re * back_im - wave_im * back_re)
        for c in range(2):
            blocks = jnp.stack([terms[c][:, j * 128 : j * 128 + 128] for j in range(wide)])
            blocks = spread(blocks, turn, 2, 128)
            for j in range(rounds):
                part = spread(blocks[j].reshape(width // 8, 8, 128), shift, 1, 8)
                total[c, layer, lax.rem(first + j, rounds), rows, :] += part.reshape(width + 8, 128)

    for k in range(count):
        cut_layer(k, last)
        far_re, far_im = forward(*leave(k, last), pairs)
        misfit = far_re * far_re + far_im * far_im - ordered[k]
        back_re, back_im = inverse(misfit * far_re, misfit * far_im, pairs)
        record(k, last, back_re, back_im)
        waves[k, last, 0] = back_re
        waves[k, last, 1] = back_im

    def backward(step, carry):
        layer = last - step
        for k in range(count):
            back_re, back_im = waves[k, layer, 0], waves[k, layer, 1]
            slab_re, slab_im = windows[k, layer, 0], windows[k, layer, 1]
            re, im = complex_product(back_re, back_im, slab_re, -slab_im)
            re, im = forward(re, im, pairs)
            re, im = complex_product(re, im, phases[0], -phases[1])
            re, im = inverse(re, im, pairs)
            record(k, layer - 1, re, im)
            waves[k, layer - 1, 0] = re
            waves[k, layer - 1, 1] = im
        return carry

    lax.fori_loop(0, last, backward, 0)

    def hand_out(layer, carry):
        for start, size, is_edge, at in pieces:
            rows, own = pl.ds(start, size), pl.ds(at, size)
            for c in range(2):
                target = out_edges if is_edge else out
                for j in range(wide):
                    target[c, layer, own, pl.ds(j * 128, 128)] = total[c, layer, j, rows, :]
            re, im = total[0, layer, wide, rows, :], total[1, layer, wide, rows, :]
            low = lower_lanes(re)
            (to_right_ends if is_edge else to_right)[layer, own, :] = jnp.where(low, re, swapped(im))
            (to_left_ends if is_edge else to_left)[layer, own, :] = jnp.where(low, swapped(re), im)
        return carry

    lax.fori_loop(0, layers, hand_out, 0)


def packed(cells):
    wide = cells.shape[-1]
    head = jnp.concatenate([cells[0, ..., :HALO], cells[1, ..., :HALO]], -1)
    tail = jnp.concatenate([cells[0, ..., wide - HALO :], cells[1, ..., wide - HALO :]], -1)
    return head, tail


def like(array):
    return jax.ShapeDtypeStruct(array.shape, array.dtype)


def absorb(parts, cells, from_left, from_right):
    wide = cells.shape[-1]
    l, r = from_left[...], from_right[...]
    low = lower_lanes(l)
    zero = jnp.zeros_like(l)
    added = (
        (jnp.where(low, l, zero), jnp.where(low, zero, swapped(r))),
        (jnp.where(low, swapped(l), zero), jnp.where(low, zero, r)),
    )
    for c in range(2):
        parts[c, :, :, 0:128] = cells[c, :, :, 0:128] + added[c][0]
        for at in range(128, wide - 128, 128):
            parts[c, :, :, at : at + 128] = cells[c, :, :, at : at + 128]
        parts[c, :, :, wide - 128 : wide] = cells[c, :, :, wide - 128 : wide] + added[c][1]


def edges_kernel(edges, from_left, from_right, up, down):
    size = edges.shape[2] // 2
    top, bottom = pl.ds(0, size), pl.ds(size, size)
    absorb(up, edges.at[:, :, top, :], from_left.at[:, top, :], from_right.at[:, top, :])
    absorb(down, edges.at[:, :, bottom, :], from_left.at[:, bottom, :], from_right.at[:, bottom, :])


def final_kernel(cells, from_left, from_right, from_above, from_below, objects, gradient, updated):
    tall = cells.shape[2]
    absorb(gradient, cells, from_left, from_right)
    gradient[:, :, 0:HALO, :] += from_above[...]
    gradient[:, :, tall - HALO : tall, :] += from_below[...]
    updated[...] = objects[...] - descent_rate * gradient[...]


def on_device(object_slices, positions, intensities, probe, propagator):
    measured = intensities[0, 0]
    count, width = measured.shape[0], measured.shape[-1]
    layers, tall, broad = object_slices.shape[1:]
    wide = broad // 128
    tables = jnp.asarray(half_tables(width))
    phase = jnp.stack([jnp.cos(propagator), jnp.sin(propagator)])
    above = passed_along(object_slices[:, :, tall - HALO :], "row", 1)
    below = passed_along(object_slices[:, :, :HALO], "row", -1)
    head, tail = packed(object_slices)
    right = passed_along(head, "col", -1)
    left = passed_along(tail, "col", 1)
    edges = jnp.concatenate([above, below], 2)
    head, tail = packed(edges)
    right_ends = passed_along(head, "col", -1)
    left_ends = passed_along(tail, "col", 1)
    vmem = pl.BlockSpec(memory_space=pltpu.VMEM)
    limit = pltpu.CompilerParams(vmem_limit_bytes=58 * 2**20)
    cells, edges, to_right, to_left, to_right_ends, to_left_ends = pl.pallas_call(
        step_kernel,
        out_shape=[like(v) for v in (object_slices, edges, right, left, right_ends, left_ends)],
        in_specs=[pl.BlockSpec(memory_space=pltpu.SMEM)] + [vmem] * 10,
        out_specs=[vmem] * 6,
        scratch_shapes=[
            pltpu.VMEM((2, layers, wide + 1, tall + 2 * HALO, 128), jnp.float32),
            pltpu.VMEM((2, layers, wide + 1, tall + 2 * HALO, 128), jnp.float32),
            pltpu.VMEM((count, layers, 2, width, width), jnp.float32),
            pltpu.VMEM((count, layers, 2, width, width), jnp.float32),
            pltpu.VMEM((count, width, width), jnp.float32),
            pltpu.VMEM((2, width, width), jnp.float32),
        ],
        compiler_params=limit,
    )(
        positions[0, 0], object_slices, edges, right, left, right_ends, left_ends,
        measured, probe, phase, tables,
    )
    left_ends = passed_along(to_right_ends, "col", 1)
    right_ends = passed_along(to_left_ends, "col", -1)
    left = passed_along(to_right, "col", 1)
    right = passed_along(to_left, "col", -1)
    up, down = pl.pallas_call(
        edges_kernel,
        out_shape=[like(above), like(below)],
        in_specs=[vmem] * 3,
        out_specs=[vmem] * 2,
        compiler_params=limit,
    )(edges, left_ends, right_ends)
    from_above = passed_along(down, "row", 1)
    from_below = passed_along(up, "row", -1)
    return tuple(
        pl.pallas_call(
            final_kernel,
            out_shape=[like(cells), like(cells)],
            in_specs=[vmem] * 6,
            out_specs=[vmem] * 2,
            compiler_params=limit,
        )(cells, left, right, from_above, from_below, object_slices)
    )


def solution(mesh):
    return jax.shard_map(
        on_device,
        mesh=mesh,
        in_specs=(
            P(None, None, "row", "col"),
            P("row", "col", None, None),
            P("row", "col", None, None, None),
            P(),
            P(),
        ),
        out_specs=(P(None, None, "row", "col"), P(None, None, "row", "col")),
        check_vma=False,
    )
```

time: 181 us -> 115 us (0.64)
  local copies, waits for them, and re-layouts: 63.8 us -> 5.24 us
  other arithmetic: 15.8 us -> 1.54 us
  Pallas kernels: 26.3 us -> 37.5 us
  waiting for transfers between devices: 60.2 us -> 51.7 us
  starting transfers between devices: 13.4 us -> 17.5 us
    slice x19 -> x1, local copies, waits for them, and re-layouts: 43.4 us -> 1.42 us  [on_device(): below = passed_along(object_slices[:, :, :HALO], 'row', -1)]
    ppermute x4 -> x0, waiting for transfers between devices: 20.5 us -> none  [the longest x2 18.7 us: with_halo(): lax.ppermute(tail, axis, [(i, (i + 1) % count) for i in range(count)])]
    ppermute x4 -> x12, starting transfers between devices: 5.24 us -> 17.5 us  [passed_along(): return lax.ppermute(block, axis, route)]
    ppermute x4 -> x12, waiting for transfers between devices: 39.7 us -> 51.7 us  [passed_along(): return lax.ppermute(block, axis, route)]
    pallas_call x1 -> x3, Pallas kernels: 26.3 us -> 37.5 us  [the longest x1 29.8 us: on_device(): pl.pallas_call(step_kernel, out_shape=[like(v) for v in (object_slices, e...]
    scatter-add x2 -> x0, local copies, waits for them, and re-layouts: 11 us -> none  [the longest x1 6.46 us: fold_cols(): middle = middle.at[:, :, :, inner - HALO:].add(from_right)]
    ppermute x4 -> x0, starting transfers between devices: 8.12 us -> none  [the longest x2 4.91 us: with_halo(): lax.ppermute(head, axis, [((i + 1) % count, i) for i in range(count)])]
    ppermute x4 -> x0, local copies, waits for them, and re-layouts: 8.07 us -> none  [the longest x2 4.85 us: passed_along(): return lax.ppermute(block, axis, route)]
  transfers between devices with their start and end apart: 8 -> 12, of which waited for: 4 -> 9; matrix products, arithmetic and copies ran while one was open for 26% -> 3% of each run, Pallas kernels for 0% -> 2%
where the time goes in v2:
time: 115 us; the launch traced here: 114 us
  waiting for transfers between devices  51.7 us (45%)
  Pallas kernels  37.5 us (33%)
  starting transfers between devices  17.5 us (15%)
  local copies, waits for them, and re-layouts  5.24 us (5%)
  other arithmetic  1.54 us (1%)
    ppermute x12, waiting for transfers between devices, passed_along(): return lax.ppermute(block, axis, route)  51.7 us
    pallas_call x1, Pallas kernels, on_device(): pl.pallas_call(step_kernel, out_shape=[like(v) for v in (object_slices, e...  29.8 us
    ppermute x12, starting transfers between devices, passed_along(): return lax.ppermute(block, axis, route)  17.5 us
    pallas_call x1, Pallas kernels, on_device(): pl.pallas_call(final_kernel, out_shape=[like(cells), like(cells)], in_spe...  5.29 us
    pallas_call x1, Pallas kernels, on_device(): pl.pallas_call(edges_kernel, out_shape=[like(above), like(below)], in_spe...  2.47 us
  transfers between devices with their start and end apart: 12, of which 9 were waited for; matrix products, arithmetic and copies ran while one was open for 3% of the time, Pallas kernels for 2%

profile of v2, /device:TPU:1, one launch (start us, length us, event | category | flops | bytes accessed | tf_op | source)
XLA Modules:
  0.0 114.2 jit_solution(8561858637083422547)
XLA Ops:
  0.6 0.0 copy-start
  0.6 1.4 %fusion = (f32[2,4,64,256]{3,2,1,0:T(8,128)S(1)}, f32[2,4,64,256]{3,2,1,0:T(8,128)S(1)}) fusion(f32[2,4,256,256]{3,2,1,0:T(8,128)} %objects.1), kind=kLoop, calls=%fused_computation.17 | loop fusion | bytes 2097152 | tf_op jit(solution)/shard_map/slice | solution.py:308
  2.1 5.1 %collective-permute-start.1 = (f32[2,4,64,256]{3,2,1,0:T(8,128)S(1)}, f32[2,4,64,256]{3,2,1,0:T(8,128)S(1)}, u32[]{:S(2)}, u32[]{:S(2)}) collective-permute-start(f32[2,4,64,256]{3,2,1,0:T(8,128)S(1)} %get-tuple-element.22), channel_id=1, source_target_pairs={{4,0},{8,4},{12,8},{16,12},{20,16},{24,20},{28,24},{0,28},{5,1},{9... | collective-permute-start | bytes 1572872 | tf_op jit(solution)/shard_map/ppermute | solution.py:18
  7.2 0.0 collective-permute-start
  7.2 0.0 copy-done
  7.2 0.3 slice_bitcast_fusion.1
  7.5 0.2 pad_maximum_fusion
  7.8 1.0 collective-permute-start.2
  8.8 0.2 pad_maximum_fusion.1
  9.0 1.2 %collective-permute-start.3 = (f32[4,256,128]{2,1,0:T(8,128)S(1)}, f32[4,256,128]{2,1,0:T(8,128)S(1)}, u32[]{:S(2)}, u32[]{:S(2)}) collective-permute-start(f32[4,256,128]{2,1,0:T(8,128)S(1)} %pad_maximum_fusion.1), channel_id=1, source_target_pairs={{3,0},{0,1},{1,2},{2,3},{7,4},{4,5},{5,6},{6,7},{11,8},{8,9},{9,10... | collective-permute-start | bytes 1572872 | tf_op jit(solution)/shard_map/ppermute | solution.py:18
  10.2 17.8 %collective-permute-done = f32[2,4,64,256]{3,2,1,0:T(8,128)S(1)} collective-permute-done((f32[2,4,64,256]{3,2,1,0:T(8,128)S(1)}, f32[2,4,64,256]{3,2,1,0:T(8,128)S(1)}, u32[]{:S(2)}, u32[]{:S(2)}) %collective-permute-start) | collective-permute-done | bytes 524320 | tf_op jit(solution)/shard_map/ppermute | solution.py:18
  28.0 0.0 collective-permute-done.1
  28.0 0.0 copy-start.1
  28.0 0.0 copy-start.8
  28.0 0.2 slice_bitcast_fusion.5
  28.3 0.1 pad_maximum_fusion.3
  28.4 0.5 collective-permute-start.4
  28.9 0.1 pad_maximum_fusion.4
  29.1 1.3 %collective-permute-start.5 = (f32[4,128,128]{2,1,0:T(8,128)S(1)}, f32[4,128,128]{2,1,0:T(8,128)S(1)}, u32[]{:S(2)}, u32[]{:S(2)}) collective-permute-start(f32[4,128,128]{2,1,0:T(8,128)S(1)} %pad_maximum_fusion.4), channel_id=1, source_target_pairs={{3,0},{0,1},{1,2},{2,3},{7,4},{4,5},{5,6},{6,7},{11,8},{8,9},{9,10... | collective-permute-start | bytes 786440 | tf_op jit(solution)/shard_map/ppermute | solution.py:18
  30.4 0.0 copy-done.8
  30.4 0.9 cosine_bitcast_fusion
  31.3 0.0 copy-done.1
  31.4 0.9 pad_maximum_fusion.2.phase
  32.2 0.0 collective-permute-done.2.right
  32.2 0.0 copy-start.2
  32.2 0.0 collective-permute-done.3.left
  32.2 0.0 copy-start.3
  32.2 4.0 %collective-permute-done.4.right_ends = f32[4,128,128]{2,1,0:T(8,128)S(1)} collective-permute-done((f32[4,128,128]{2,1,0:T(8,128)S(1)}, f32[4,128,128]{2,1,0:T(8,128)S(1)}, u32[]{:S(2)}, u32[]{:S(2)}) %collective-permute-start.4) | collective-permute-done | bytes 262176 | tf_op jit(solution)/shard_map/ppermute | solution.py:18
  36.2 0.0 copy-start.9
  36.2 0.2 collective-permute-done.5.left_ends
  36.4 0.0 copy-start.10
  36.4 0.0 copy-done.2
  36.5 0.0 copy-done.3
  36.5 0.5 copy-done.9
  36.9 0.2 copy-done.10
  37.2 29.8 %shard_map.77 = (f32[2,4,256,256]{3,2,1,0:T(8,128)}, f32[2,4,128,256]{3,2,1,0:T(8,128)}, f32[4,256,128]{2,1,0:T(8,128)}, f32[4,256,128]{2,1,0:T(8,128)}, f32[4,128,128]{2,1,0:T(8,128)}, /*index=5*/f32[4,128,128]{2,1,0:T(8,128)}) custom-call(s32[2,2]{1,0:T(2,128)} %bitcast.23, f32[2,4,256,256]{3,2,1,0:T(8,128)} %objects.1, f32[2,4,128,256]{3,2,1,0:T(8,128)} %copy-done.1, ...), custom_call_target="tpu_custom_call" | custom-call | tf_op jit(solution)/shard_map/pallas_call | solution.py:318
  66.9 2.4 %collective-permute-start.8 = (f32[4,128,128]{2,1,0:T(8,128)}, f32[4,128,128]{2,1,0:T(8,128)S(1)}, u32[]{:S(2)}, u32[]{:S(2)}) collective-permute-start(f32[4,128,128]{2,1,0:T(8,128)} %get-tuple-element.14), channel_id=1, source_target_pairs={{3,0},{0,1},{1,2},{2,3},{7,4},{4,5},{5,6},{6,7},{11,8},{8,9},{9,10... | collective-permute-start | bytes 786440 | tf_op jit(solution)/shard_map/ppermute | solution.py:18
  69.3 0.0 collective-permute-start.9
  69.3 1.7 %collective-permute-start.6 = (f32[4,256,128]{2,1,0:T(8,128)}, f32[4,256,128]{2,1,0:T(8,128)S(1)}, u32[]{:S(2)}, u32[]{:S(2)}) collective-permute-start(f32[4,256,128]{2,1,0:T(8,128)} %get-tuple-element.11), channel_id=1, source_target_pairs={{3,0},{0,1},{1,2},{2,3},{7,4},{4,5},{5,6},{6,7},{11,8},{8,9},{9,10... | collective-permute-start | bytes 1572872 | tf_op jit(solution)/shard_map/ppermute | solution.py:18
  71.1 0.0 collective-permute-start.7
  71.1 3.9 %collective-permute-done.8.from_left = f32[4,128,128]{2,1,0:T(8,128)S(1)} collective-permute-done((f32[4,128,128]{2,1,0:T(8,128)}, f32[4,128,128]{2,1,0:T(8,128)S(1)}, u32[]{:S(2)}, u32[]{:S(2)}) %collective-permute-start.8) | collective-permute-done | bytes 262176 | tf_op jit(solution)/shard_map/ppermute | solution.py:18
  75.0 0.0 copy-start.11
  75.0 3.5 %collective-permute-done.9.from_right = f32[4,128,128]{2,1,0:T(8,128)S(1)} collective-permute-done((f32[4,128,128]{2,1,0:T(8,128)}, f32[4,128,128]{2,1,0:T(8,128)S(1)}, u32[]{:S(2)}, u32[]{:S(2)}) %collective-permute-start.9) | collective-permute-done | bytes 262176 | tf_op jit(solution)/shard_map/ppermute | solution.py:18
  78.4 0.0 copy-start.12
  78.5 0.0 copy-done.11
  78.5 0.7 copy-done.12
  79.2 2.5 %shard_map.78 = (f32[2,4,64,256]{3,2,1,0:T(8,128)}, f32[2,4,64,256]{3,2,1,0:T(8,128)}) custom-call(f32[2,4,128,256]{3,2,1,0:T(8,128)} %get-tuple-element.13.edges, f32[4,128,128]{2,1,0:T(8,128)} %copy-done.11, f32[4,128,128]{2,1,0:T(8,128)} %copy-done.12), custom_call_target="tpu_custom_call" | custom-call | tf_op jit(solution)/shard_map/pallas_call | solution.py:340
  81.6 2.2 %collective-permute-start.10 = (f32[2,4,64,256]{3,2,1,0:T(8,128)}, f32[2,4,64,256]{3,2,1,0:T(8,128)S(1)}, u32[]{:S(2)}, u32[]{:S(2)}) collective-permute-start(f32[2,4,64,256]{3,2,1,0:T(8,128)} %get-tuple-element.16), channel_id=1, source_target_pairs={{28,0},{0,4},{4,8},{8,12},{12,16},{16,20},{20,24},{24,28},{29,1},{... | collective-permute-start | bytes 1572872 | tf_op jit(solution)/shard_map/ppermute | solution.py:18
  83.9 1.9 %collective-permute-start.11 = (f32[2,4,64,256]{3,2,1,0:T(8,128)}, f32[2,4,64,256]{3,2,1,0:T(8,128)S(1)}, u32[]{:S(2)}, u32[]{:S(2)}) collective-permute-start(f32[2,4,64,256]{3,2,1,0:T(8,128)} %get-tuple-element.17), channel_id=1, source_target_pairs={{4,0},{8,4},{12,8},{16,12},{20,16},{24,20},{28,24},{0,28},{5,1},{9... | collective-permute-start | bytes 1572872 | tf_op jit(solution)/shard_map/ppermute | solution.py:18
  85.8 0.4 collective-permute-done.6.from_left
  86.2 0.0 copy-start.4
  86.2 1.7 %collective-permute-done.7.from_right = f32[4,256,128]{2,1,0:T(8,128)S(1)} collective-permute-done((f32[4,256,128]{2,1,0:T(8,128)}, f32[4,256,128]{2,1,0:T(8,128)S(1)}, u32[]{:S(2)}, u32[]{:S(2)}) %collective-permute-start.7) | collective-permute-done | bytes 524320 | tf_op jit(solution)/shard_map/ppermute | solution.py:18
  87.9 0.0 copy-start.5
  87.9 18.1 %collective-permute-done.10.from_above = f32[2,4,64,256]{3,2,1,0:T(8,128)S(1)} collective-permute-done((f32[2,4,64,256]{3,2,1,0:T(8,128)}, f32[2,4,64,256]{3,2,1,0:T(8,128)S(1)}, u32[]{:S(2)}, u32[]{:S(2)}) %collective-permute-start.10) | collective-permute-done | bytes 524320 | tf_op jit(solution)/shard_map/ppermute | solution.py:18
  106.0 0.0 copy-start.6
  106.0 2.1 %collective-permute-done.11.from_below = f32[2,4,64,256]{3,2,1,0:T(8,128)S(1)} collective-permute-done((f32[2,4,64,256]{3,2,1,0:T(8,128)}, f32[2,4,64,256]{3,2,1,0:T(8,128)S(1)}, u32[]{:S(2)}, u32[]{:S(2)}) %collective-permute-start.11) | collective-permute-done | bytes 524320 | tf_op jit(solution)/shard_map/ppermute | solution.py:18
  108.1 0.0 copy-start.7
  108.1 0.0 copy-done.4
  108.1 0.0 copy-done.5
  108.1 0.0 copy-done.6
  108.1 0.8 copy-done.7
  108.9 5.3 %shard_map.79 = (f32[2,4,256,256]{3,2,1,0:T(8,128)}, f32[2,4,256,256]{3,2,1,0:T(8,128)}) custom-call(f32[2,4,256,256]{3,2,1,0:T(8,128)} %get-tuple-element.10.cells, f32[4,256,128]{2,1,0:T(8,128)} %copy-done.4, f32[4,256,128]{2,1,0:T(8,128)} %copy-done.5, f32[2,4,64,256]{3,2,1,0:T(8,128)} %copy-done.6, f32[2,4,64,256]{3,2,1,0:T(8,128)} %copy-done.7, ...), custom_call_target="tpu_custom_call" | custom-call | tf_op jit(solution)/shard_map/pallas_call | solution.py:350
  (2 shorter events, 0.1 us)
Async XLA Ops:
  0.6 6.6 %copy-start = (f32[2,4,256,256]{3,2,1,0:T(8,128)S(1)}, f32[2,4,256,256]{3,2,1,0:T(8,128)}, u32[]{:S(2)}) copy-start(f32[2,4,256,256]{3,2,1,0:T(8,128)} %objects.1) | copy-start | bytes 6291460
  2.1 25.9 %collective-permute-start.1 = (f32[2,4,64,256]{3,2,1,0:T(8,128)S(1)}, f32[2,4,64,256]{3,2,1,0:T(8,128)S(1)}, u32[]{:S(2)}, u32[]{:S(2)}) collective-permute-start(f32[2,4,64,256]{3,2,1,0:T(8,128)S(1)} %get-tuple-element.22), channel_id=1, source_target_pairs={{4,0},{8,4},{12,8},{16,12},{20,16},{24,20},{28,24},{0,28},{5,1},{9... | collective-permute-start | bytes 1572872 | tf_op jit(solution)/shard_map/ppermute | solution.py:18
  7.2 20.7 %collective-permute-start = (f32[2,4,64,256]{3,2,1,0:T(8,128)S(1)}, f32[2,4,64,256]{3,2,1,0:T(8,128)S(1)}, u32[]{:S(2)}, u32[]{:S(2)}) collective-permute-start(f32[2,4,64,256]{3,2,1,0:T(8,128)S(1)} %get-tuple-element.23), channel_id=1, source_target_pairs={{28,0},{0,4},{4,8},{8,12},{12,16},{16,20},{20,24},{24,28},{29,1},{... | collective-permute-start | bytes 1572872 | tf_op jit(solution)/shard_map/ppermute | solution.py:18
  7.8 24.5 %collective-permute-start.2 = (f32[4,256,128]{2,1,0:T(8,128)S(1)}, f32[4,256,128]{2,1,0:T(8,128)S(1)}, u32[]{:S(2)}, u32[]{:S(2)}) collective-permute-start(f32[4,256,128]{2,1,0:T(8,128)S(1)} %pad_maximum_fusion), channel_id=1, source_target_pairs={{1,0},{2,1},{3,2},{0,3},{5,4},{6,5},{7,6},{4,7},{9,8},{10,9},{11,1... | collective-permute-start | bytes 1572872 | tf_op jit(solution)/shard_map/ppermute | solution.py:18
  9.0 23.2 %collective-permute-start.3 = (f32[4,256,128]{2,1,0:T(8,128)S(1)}, f32[4,256,128]{2,1,0:T(8,128)S(1)}, u32[]{:S(2)}, u32[]{:S(2)}) collective-permute-start(f32[4,256,128]{2,1,0:T(8,128)S(1)} %pad_maximum_fusion.1), channel_id=1, source_target_pairs={{3,0},{0,1},{1,2},{2,3},{7,4},{4,5},{5,6},{6,7},{11,8},{8,9},{9,10... | collective-permute-start | bytes 1572872 | tf_op jit(solution)/shard_map/ppermute | solution.py:18
  28.0 3.3 %copy-start.1 = (f32[2,4,128,256]{3,2,1,0:T(8,128)}, f32[2,4,128,256]{3,2,1,0:T(8,128)S(1)}, u32[]{:S(2)}) copy-start(f32[2,4,128,256]{3,2,1,0:T(8,128)S(1)} %constant_dynamic-update-slice_fusion.edges) | copy-start | bytes 3145732
  28.0 2.4 %copy-start.8 = (f32[256,256]{1,0:T(8,128)S(1)}, f32[256,256]{1,0:T(8,128)}, u32[]{:S(2)}) copy-start(f32[256,256]{1,0:T(8,128)} %param.10) | copy-start | bytes 786436
  28.4 7.8 %collective-permute-start.4 = (f32[4,128,128]{2,1,0:T(8,128)S(1)}, f32[4,128,128]{2,1,0:T(8,128)S(1)}, u32[]{:S(2)}, u32[]{:S(2)}) collective-permute-start(f32[4,128,128]{2,1,0:T(8,128)S(1)} %pad_maximum_fusion.3), channel_id=1, source_target_pairs={{1,0},{2,1},{3,2},{0,3},{5,4},{6,5},{7,6},{4,7},{9,8},{10,9},{11,1... | collective-permute-start | bytes 786440 | tf_op jit(solution)/shard_map/ppermute | solution.py:18
  29.1 7.4 %collective-permute-start.5 = (f32[4,128,128]{2,1,0:T(8,128)S(1)}, f32[4,128,128]{2,1,0:T(8,128)S(1)}, u32[]{:S(2)}, u32[]{:S(2)}) collective-permute-start(f32[4,128,128]{2,1,0:T(8,128)S(1)} %pad_maximum_fusion.4), channel_id=1, source_target_pairs={{3,0},{0,1},{1,2},{2,3},{7,4},{4,5},{5,6},{6,7},{11,8},{8,9},{9,10... | collective-permute-start | bytes 786440 | tf_op jit(solution)/shard_map/ppermute | solution.py:18
  32.2 4.2 %copy-start.2 = (f32[4,256,128]{2,1,0:T(8,128)}, f32[4,256,128]{2,1,0:T(8,128)S(1)}, u32[]{:S(2)}) copy-start(f32[4,256,128]{2,1,0:T(8,128)S(1)} %collective-permute-done.2.right) | copy-start | bytes 1572868
  32.2 4.2 %copy-start.3 = (f32[4,256,128]{2,1,0:T(8,128)}, f32[4,256,128]{2,1,0:T(8,128)S(1)}, u32[]{:S(2)}) copy-start(f32[4,256,128]{2,1,0:T(8,128)S(1)} %collective-permute-done.3.left) | copy-start | bytes 1572868
  36.2 0.7 copy-start.9
  36.4 0.7 copy-start.10
  66.9 8.0 %collective-permute-start.8 = (f32[4,128,128]{2,1,0:T(8,128)}, f32[4,128,128]{2,1,0:T(8,128)S(1)}, u32[]{:S(2)}, u32[]{:S(2)}) collective-permute-start(f32[4,128,128]{2,1,0:T(8,128)} %get-tuple-element.14), channel_id=1, source_target_pairs={{3,0},{0,1},{1,2},{2,3},{7,4},{4,5},{5,6},{6,7},{11,8},{8,9},{9,10... | collective-permute-start | bytes 786440 | tf_op jit(solution)/shard_map/ppermute | solution.py:18
  69.3 9.1 %collective-permute-start.9 = (f32[4,128,128]{2,1,0:T(8,128)}, f32[4,128,128]{2,1,0:T(8,128)S(1)}, u32[]{:S(2)}, u32[]{:S(2)}) collective-permute-start(f32[4,128,128]{2,1,0:T(8,128)} %get-tuple-element.15), channel_id=1, source_target_pairs={{1,0},{2,1},{3,2},{0,3},{5,4},{6,5},{7,6},{4,7},{9,8},{10,9},{11,1... | collective-permute-start | bytes 786440 | tf_op jit(solution)/shard_map/ppermute | solution.py:18
  69.3 16.8 %collective-permute-start.6 = (f32[4,256,128]{2,1,0:T(8,128)}, f32[4,256,128]{2,1,0:T(8,128)S(1)}, u32[]{:S(2)}, u32[]{:S(2)}) collective-permute-start(f32[4,256,128]{2,1,0:T(8,128)} %get-tuple-element.11), channel_id=1, source_target_pairs={{3,0},{0,1},{1,2},{2,3},{7,4},{4,5},{5,6},{6,7},{11,8},{8,9},{9,10... | collective-permute-start | bytes 1572872 | tf_op jit(solution)/shard_map/ppermute | solution.py:18
  71.1 16.8 %collective-permute-start.7 = (f32[4,256,128]{2,1,0:T(8,128)}, f32[4,256,128]{2,1,0:T(8,128)S(1)}, u32[]{:S(2)}, u32[]{:S(2)}) collective-permute-start(f32[4,256,128]{2,1,0:T(8,128)} %get-tuple-element.12), channel_id=1, source_target_pairs={{1,0},{2,1},{3,2},{0,3},{5,4},{6,5},{7,6},{4,7},{9,8},{10,9},{11,1... | collective-permute-start | bytes 1572872 | tf_op jit(solution)/shard_map/ppermute | solution.py:18
  75.0 3.5 %copy-start.11 = (f32[4,128,128]{2,1,0:T(8,128)}, f32[4,128,128]{2,1,0:T(8,128)S(1)}, u32[]{:S(2)}) copy-start(f32[4,128,128]{2,1,0:T(8,128)S(1)} %collective-permute-done.8.from_left) | copy-start | bytes 786436
  78.4 0.7 copy-start.12
  81.6 24.4 %collective-permute-start.10 = (f32[2,4,64,256]{3,2,1,0:T(8,128)}, f32[2,4,64,256]{3,2,1,0:T(8,128)S(1)}, u32[]{:S(2)}, u32[]{:S(2)}) collective-permute-start(f32[2,4,64,256]{3,2,1,0:T(8,128)} %get-tuple-element.16), channel_id=1, source_target_pairs={{28,0},{0,4},{4,8},{8,12},{12,16},{16,20},{20,24},{24,28},{29,1},{... | collective-permute-start | bytes 1572872 | tf_op jit(solution)/shard_map/ppermute | solution.py:18
  83.9 24.3 %collective-permute-start.11 = (f32[2,4,64,256]{3,2,1,0:T(8,128)}, f32[2,4,64,256]{3,2,1,0:T(8,128)S(1)}, u32[]{:S(2)}, u32[]{:S(2)}) collective-permute-start(f32[2,4,64,256]{3,2,1,0:T(8,128)} %get-tuple-element.17), channel_id=1, source_target_pairs={{4,0},{8,4},{12,8},{16,12},{20,16},{24,20},{28,24},{0,28},{5,1},{9... | collective-permute-start | bytes 1572872 | tf_op jit(solution)/shard_map/ppermute | solution.py:18
  86.2 21.9 %copy-start.4 = (f32[4,256,128]{2,1,0:T(8,128)}, f32[4,256,128]{2,1,0:T(8,128)S(1)}, u32[]{:S(2)}) copy-start(f32[4,256,128]{2,1,0:T(8,128)S(1)} %collective-permute-done.6.from_left) | copy-start | bytes 1572868
  87.9 20.2 %copy-start.5 = (f32[4,256,128]{2,1,0:T(8,128)}, f32[4,256,128]{2,1,0:T(8,128)S(1)}, u32[]{:S(2)}) copy-start(f32[4,256,128]{2,1,0:T(8,128)S(1)} %collective-permute-done.7.from_right) | copy-start | bytes 1572868
  106.0 2.1 %copy-start.6 = (f32[2,4,64,256]{3,2,1,0:T(8,128)}, f32[2,4,64,256]{3,2,1,0:T(8,128)S(1)}, u32[]{:S(2)}) copy-start(f32[2,4,64,256]{3,2,1,0:T(8,128)S(1)} %collective-permute-done.10.from_above) | copy-start | bytes 1572868
  108.1 0.8 copy-start.7

commit v3 on v2

v3 whole, which is shorter than its diff:
```python
import jax
import jax.numpy as jnp
import numpy as np
from jax import lax
from jax.experimental import pallas as pl
from jax.experimental.pallas import tpu as pltpu
from jax.sharding import PartitionSpec as P

HALO = 64


descent_rate = 0.5


def passed_along(block, axis, distance):
    devices = range(lax.axis_size(axis))
    route = [((i - distance) % len(devices), i) for i in devices]
    return lax.ppermute(block, axis, route)


def split(value):
    high = value.astype(jnp.bfloat16)
    low = (value - high.astype(jnp.float32)).astype(jnp.bfloat16)
    return high, low


def half_tables(width):
    half = width // 2
    place = np.arange(half)
    found = []
    for odd in (0, 1):
        angle = 2.0 * np.pi * (np.outer(2 * place + odd, place) % width) / width
        re = np.cos(angle) / np.sqrt(width)
        im = -np.sin(angle) / np.sqrt(width)
        found.append(np.block([[re, -im], [im, re]]).astype(np.float32))
    even, odd = found
    order = np.eye(width, dtype=np.float32)[np.concatenate([2 * place, 2 * place + 1])]
    six = np.stack([even, odd, even.T, odd.T, order, order.T])
    high = six.astype(jnp.bfloat16)
    low = (six - high.astype(np.float32)).astype(jnp.bfloat16)
    return np.stack([high, low])


def dot_left(pair, value):
    high, low = split(value)
    matrix = jnp.concatenate([pair[0], pair[0], pair[1]], 1)
    return jnp.dot(matrix, jnp.concatenate([high, low, high], 0), preferred_element_type=jnp.float32)


def dot_right(value, pair):
    high, low = split(value)
    matrix = jnp.concatenate([pair[0], pair[0], pair[1]], 0)
    return jnp.dot(jnp.concatenate([high, low, high], 1), matrix, preferred_element_type=jnp.float32)


def cut(value, dim):
    half = value.shape[dim] // 2
    return (lax.slice_in_dim(value, 0, half, axis=dim), lax.slice_in_dim(value, half, 2 * half, axis=dim))


def joined(first, second, dim):
    return jnp.concatenate([first, second], dim)


def forward_axis(re, im, dim, dot, even_matrix, odd_matrix):
    r0, r1 = cut(re, dim)
    i0, i1 = cut(im, dim)
    even_re, even_im = cut(dot(joined(r0 + r1, i0 + i1, dim), even_matrix), dim)
    odd_re, odd_im = cut(dot(joined(r0 - r1, i0 - i1, dim), odd_matrix), dim)
    return joined(even_re, odd_re, dim), joined(even_im, odd_im, dim)


def inverse_axis(re, im, dim, dot, even_matrix, odd_matrix):
    r0, r1 = cut(re, dim)
    i0, i1 = cut(im, dim)
    p_re, p_im = cut(dot(joined(r0, i0, dim), even_matrix), dim)
    q_re, q_im = cut(dot(joined(r1, i1, dim), odd_matrix), dim)
    return joined(p_re + q_re, p_re - q_re, dim), joined(p_im + q_im, p_im - q_im, dim)


def left_dot(value, pair):
    return dot_left(pair, value)


def forward(re, im, pairs):
    re, im = forward_axis(re, im, 0, left_dot, pairs(0), pairs(1))
    return forward_axis(re, im, 1, dot_right, pairs(2), pairs(3))


def inverse(re, im, pairs):
    re, im = inverse_axis(re, im, 1, dot_right, pairs(0), pairs(1))
    return inverse_axis(re, im, 0, left_dot, pairs(2), pairs(3))


def by_parity(value, pairs):
    return dot_right(dot_left(pairs(4), value), pairs(5))


def complex_product(left_re, left_im, right_re, right_im):
    return (left_re * right_re - left_im * right_im, left_re * right_im + left_im * right_re)


def slid(whole, shift, axis, span):
    turned = pltpu.roll(whole, lax.rem(span - shift, span), axis)
    kept = lax.broadcasted_iota(jnp.int32, whole[:-1].shape, axis) < span - shift
    return jnp.where(kept, turned[:-1], turned[1:])


def spread(whole, shift, axis, span):
    turned = pltpu.roll(whole, lax.rem(shift, span), axis)
    zero = jnp.zeros_like(turned[:1])
    first = jnp.concatenate([zero, turned], 0)
    other = jnp.concatenate([turned, zero], 0)
    moved = lax.broadcasted_iota(jnp.int32, first.shape, axis) < shift
    return jnp.where(moved, first, other)


def row_place(oy, rows, width):
    base = jnp.minimum(oy - lax.rem(oy, 8), rows - width - 8)
    return pl.ds(pl.multiple_of(base, 8), width + 8), oy - base


def lane_place(ox, lanes=128):
    early = ox < HALO
    return jnp.where(early, 2, 0), jnp.where(early, ox + lanes - HALO, ox - HALO)


def swapped(value):
    return pltpu.roll(value, HALO, value.ndim - 1)


def lower_lanes(value):
    return lax.broadcasted_iota(jnp.int32, value.shape, value.ndim - 1) < HALO


def row_pieces(tall):
    return ((0, HALO, True, 0), (HALO, tall, False, 0), (HALO + tall, HALO, True, HALO))


def fill_ext(ext, core, edges, right, left, right_ends, left_ends):
    wide = core.shape[3] // 128

    def gather(layer, carry):
        for start, size, is_edge, at in row_pieces(core.shape[2]):
            rows, own = pl.ds(start, size), pl.ds(at, size)
            for c in range(2):
                source = edges if is_edge else core
                for j in range(wide):
                    ext[c, layer, j, rows, :] = source[c, layer, own, pl.ds(j * 128, 128)]
            r = (right_ends if is_edge else right)[layer, own, :]
            l = (left_ends if is_edge else left)[layer, own, :]
            low = lower_lanes(r)
            ext[0, layer, wide, rows, :] = jnp.where(low, r, swapped(l))
            ext[1, layer, wide, rows, :] = jnp.where(low, swapped(r), l)
        return carry

    lax.fori_loop(0, core.shape[1], gather, 0)


def cut_layer(ext, windows, offsets, k, layer):
    rounds, whole = ext.shape[2], ext.shape[3]
    width = windows.shape[-1]
    rows, shift = row_place(offsets[k, 0], whole, width)
    first, turn = lane_place(offsets[k, 1])
    for c in range(2):
        blocks = jnp.stack([ext[c, layer, lax.rem(first + j, rounds), rows, :] for j in range(rounds)])
        blocks = slid(blocks, turn, 2, 128)
        for j in range(rounds - 1):
            part = blocks[j].reshape((width + 8) // 8, 8, 128)
            windows[k, layer, c, :, j * 128 : j * 128 + 128] = slid(part, shift, 1, 8).reshape(width, 128)


def leave(waves, windows, k, layer):
    return complex_product(
        waves[k, layer, 0], waves[k, layer, 1], windows[k, layer, 0], windows[k, layer, 1]
    )


def hop(re, im, phases, sign, pairs):
    re, im = forward(re, im, pairs)
    re, im = complex_product(re, im, phases[0], sign * phases[1])
    return inverse(re, im, pairs)


def onward(ext, windows, waves, offsets, phases, pairs, steps):
    def one(layer, carry):
        for k in range(waves.shape[0]):
            cut_layer(ext, windows, offsets, k, layer)
            re, im = hop(*leave(waves, windows, k, layer), phases, 1.0, pairs)
            waves[k, layer + 1, 0] = re
            waves[k, layer + 1, 1] = im
        return carry

    lax.fori_loop(0, steps, one, 0)


def record(total, waves, offsets, k, layer, back_re, back_im):
    rounds, whole = total.shape[2], total.shape[3]
    width = waves.shape[-1]
    wave_re, wave_im = waves[k, layer, 0], waves[k, layer, 1]
    rows, shift = row_place(offsets[k, 0], whole, width)
    first, turn = lane_place(offsets[k, 1])
    terms = (wave_re * back_re + wave_im * back_im, wave_re * back_im - wave_im * back_re)
    for c in range(2):
        blocks = jnp.stack([terms[c][:, j * 128 : j * 128 + 128] for j in range(rounds - 1)])
        blocks = spread(blocks, turn, 2, 128)
        for j in range(rounds):
            part = spread(blocks[j].reshape(width // 8, 8, 128), shift, 1, 8)
            total[c, layer, lax.rem(first + j, rounds), rows, :] += part.reshape(width + 8, 128)


def returned(back, windows, k, layer):
    return complex_product(back[k, 0], back[k, 1], windows[k, layer, 0], -windows[k, layer, 1])


def backward(total, windows, waves, back, offsets, phases, pairs, start):
    def one(step, carry):
        layer = start - step
        for k in range(waves.shape[0]):
            re, im = hop(*returned(back, windows, k, layer), phases, -1.0, pairs)
            record(total, waves, offsets, k, layer - 1, re, im)
            back[k, 0] = re
            back[k, 1] = im
        return carry

    lax.fori_loop(0, start, one, 0)


def hand_out(total, out, out_edges, to_right, to_left, to_right_ends, to_left_ends):
    wide = out.shape[3] // 128

    def one(layer, carry):
        for start, size, is_edge, at in row_pieces(out.shape[2]):
            rows, own = pl.ds(start, size), pl.ds(at, size)
            for c in range(2):
                target = out_edges if is_edge else out
                for j in range(wide):
                    target[c, layer, own, pl.ds(j * 128, 128)] = total[c, layer, j, rows, :]
            re, im = total[0, layer, wide, rows, :], total[1, layer, wide, rows, :]
            low = lower_lanes(re)
            (to_right_ends if is_edge else to_right)[layer, own, :] = jnp.where(low, re, swapped(im))
            (to_left_ends if is_edge else to_left)[layer, own, :] = jnp.where(low, swapped(re), im)
        return carry

    lax.fori_loop(0, out.shape[1], one, 0)


def table_pairs(tables):
    return lambda index: (tables[0, index], tables[1, index])


def entry_kernel(measured, phase, tables, ordered, phases):
    pairs = table_pairs(tables)
    for c in range(2):
        phases[c] = by_parity(phase[c], pairs)
    for k in range(measured.shape[0]):
        ordered[k] = by_parity(measured[k], pairs)


def first_kernel(offsets, *refs):
    pieces, (probe, phases, tables, waves, windows, ext) = refs[:6], refs[6:]
    fill_ext(ext, *pieces)
    for k in range(waves.shape[0]):
        waves[k, 0] = probe[...]
    onward(ext, windows, waves, offsets, phases, table_pairs(tables), windows.shape[1])


def turn_kernel(offsets, *refs):
    pieces, (entering, ordered, phases, tables) = refs[:6], refs[6:10]
    outs, slab_back, (ext, total, waves, windows, back) = refs[10:16], refs[16], refs[17:]
    pairs = table_pairs(tables)
    last = windows.shape[1] - 1
    fill_ext(ext, *pieces)
    total[...] = jnp.zeros_like(total)
    for k in range(waves.shape[0]):
        waves[k, 0] = entering[k, entering.shape[1] - 1]
    onward(ext, windows, waves, offsets, phases, pairs, last)
    for k in range(waves.shape[0]):
        cut_layer(ext, windows, offsets, k, last)
        far_re, far_im = forward(*leave(waves, windows, k, last), pairs)
        misfit = far_re * far_re + far_im * far_im - ordered[k]
        re, im = inverse(misfit * far_re, misfit * far_im, pairs)
        record(total, waves, offsets, k, last, re, im)
        back[k, 0] = re
        back[k, 1] = im
    backward(total, windows, waves, back, offsets, phases, pairs, last)
    for k in range(waves.shape[0]):
        re, im = returned(back, windows, k, 0)
        slab_back[k, 0] = re
        slab_back[k, 1] = im
    hand_out(total, *outs)


def last_kernel(offsets, waves, windows, slab_back, phases, tables, *refs):
    outs, (total, back) = refs[:6], refs[6:]
    pairs = table_pairs(tables)
    start = windows.shape[1] - 1
    total[...] = jnp.zeros_like(total)
    for k in range(waves.shape[0]):
        re, im = hop(slab_back[k, 0], slab_back[k, 1], phases, -1.0, pairs)
        record(total, waves, offsets, k, start, re, im)
        back[k, 0] = re
        back[k, 1] = im
    backward(total, windows, waves, back, offsets, phases, pairs, start)
    hand_out(total, *outs)


def packed(cells):
    wide = cells.shape[-1]
    head = jnp.concatenate([cells[0, ..., :HALO], cells[1, ..., :HALO]], -1)
    tail = jnp.concatenate([cells[0, ..., wide - HALO :], cells[1, ..., wide - HALO :]], -1)
    return head, tail


def like(array):
    return jax.ShapeDtypeStruct(array.shape, array.dtype)


def absorb(parts, cells, from_left, from_right):
    wide = cells.shape[-1]
    l, r = from_left[...], from_right[...]
    low = lower_lanes(l)
    zero = jnp.zeros_like(l)
    added = (
        (jnp.where(low, l, zero), jnp.where(low, zero, swapped(r))),
        (jnp.where(low, swapped(l), zero), jnp.where(low, zero, r)),
    )
    for c in range(2):
        parts[c, :, :, 0:128] = cells[c, :, :, 0:128] + added[c][0]
        for at in range(128, wide - 128, 128):
            parts[c, :, :, at : at + 128] = cells[c, :, :, at : at + 128]
        parts[c, :, :, wide - 128 : wide] = cells[c, :, :, wide - 128 : wide] + added[c][1]


def edges_kernel(edges, from_left, from_right, up, down):
    size = edges.shape[2] // 2
    top, bottom = pl.ds(0, size), pl.ds(size, size)
    absorb(up, edges.at[:, :, top, :], from_left.at[:, top, :], from_right.at[:, top, :])
    absorb(down, edges.at[:, :, bottom, :], from_left.at[:, bottom, :], from_right.at[:, bottom, :])


def final_kernel(*refs):
    groups, objects, gradient, updated = refs[:-3], refs[-3], refs[-2], refs[-1]
    at = 0
    for g in range(0, len(groups), 5):
        cells, from_left, from_right, from_above, from_below = groups[g : g + 5]
        tall = cells.shape[2]
        own = gradient.at[:, at : at + cells.shape[1]]
        absorb(own, cells, from_left, from_right)
        own[:, :, 0:HALO, :] += from_above[...]
        own[:, :, tall - HALO : tall, :] += from_below[...]
        at += cells.shape[1]
    updated[...] = objects[...] - descent_rate * gradient[...]


def gathered(cells):
    tall = cells.shape[2]
    above = passed_along(cells[:, :, tall - HALO :], "row", 1)
    below = passed_along(cells[:, :, :HALO], "row", -1)
    head, tail = packed(cells)
    right = passed_along(head, "col", -1)
    left = passed_along(tail, "col", 1)
    edges = jnp.concatenate([above, below], 2)
    head, tail = packed(edges)
    return (cells, edges, right, left, passed_along(head, "col", -1), passed_along(tail, "col", 1))


def folded(cells, edges, to_right, to_left, to_right_ends, to_left_ends):
    left_ends = passed_along(to_right_ends, "col", 1)
    right_ends = passed_along(to_left_ends, "col", -1)
    left = passed_along(to_right, "col", 1)
    right = passed_along(to_left, "col", -1)
    shape = list(edges.shape)
    shape[2] //= 2
    part = jax.ShapeDtypeStruct(tuple(shape), edges.dtype)
    up, down = called(edges_kernel, [part, part], [], 0)(edges, left_ends, right_ends)
    return (cells, left, right, passed_along(down, "row", 1), passed_along(up, "row", -1))


def called(kernel, outs, scratch, hops, scalars=0):
    vmem = pl.BlockSpec(memory_space=pltpu.VMEM)
    smem = pl.BlockSpec(memory_space=pltpu.SMEM)

    def call(*operands):
        moved = sum(4 * v.size for v in outs) + sum(4 * v.size for v in operands)
        return pl.pallas_call(
            kernel,
            out_shape=outs,
            in_specs=[smem] * scalars + [vmem] * (len(operands) - scalars),
            out_specs=[vmem] * len(outs),
            scratch_shapes=[pltpu.VMEM(shape, jnp.float32) for shape in scratch],
            compiler_params=pltpu.CompilerParams(vmem_limit_bytes=56 * 2**20),
            cost_estimate=pl.CostEstimate(flops=hops * 2**31, bytes_accessed=moved, transcendentals=0),
        )(*operands)

    return call


def on_device(object_slices, positions, intensities, probe, propagator):
    measured, offsets = intensities[0, 0], positions[0, 0]
    count, width = measured.shape[0], measured.shape[-1]
    layers, tall, broad = object_slices.shape[1:]
    near = layers // 2
    rest = layers - near
    tables = jnp.asarray(half_tables(width))
    phase = jnp.stack([jnp.cos(propagator), jnp.sin(propagator)])
    ordered, phases = called(entry_kernel, [like(measured), like(phase)], [], 0)(measured, phase, tables)
    ahead = gathered(object_slices[:, :near])
    behind = gathered(object_slices[:, near:])

    def wide_sums(depth):
        return (2, depth, broad // 128 + 1, tall + 2 * HALO, 128)

    def fields(*lead):
        return (count, *lead, 2, width, width)

    def f32(shape):
        return jax.ShapeDtypeStruct(shape, jnp.float32)

    waves, windows = called(
        first_kernel, [f32(fields(near + 1)), f32(fields(near))], [wide_sums(near)], 2 * near, 1
    )(offsets, *ahead, probe, phases, tables)
    *late, slab_back = called(
        turn_kernel,
        [like(v) for v in behind] + [f32(fields())],
        [wide_sums(rest), wide_sums(rest), fields(rest), fields(rest), fields()],
        4 * rest,
        1,
    )(offsets, *behind, waves, ordered, phases, tables)
    early = called(
        last_kernel, [like(v) for v in ahead], [wide_sums(near), fields()], 2 * near, 1
    )(offsets, waves, windows, slab_back, phases, tables)
    late = folded(*late)
    early = folded(*early)
    outs = [like(object_slices), like(object_slices)]
    return tuple(called(final_kernel, outs, [], 0)(*early, *late, object_slices))


def solution(mesh):
    return jax.shard_map(
        on_device,
        mesh=mesh,
        in_specs=(
            P(None, None, "row", "col"),
            P("row", "col", None, None),
            P("row", "col", None, None, None),
            P(),
            P(),
        ),
        out_specs=(P(None, None, "row", "col"), P(None, None, "row", "col")),
        check_vma=False,
    )
```

time: 115 us -> 130 us (1.13)
  starting transfers between devices: 17.5 us -> 31.5 us
  waiting for transfers between devices: 51.7 us -> 39.7 us
  Pallas kernels: 37.5 us -> 48.6 us
  local copies, waits for them, and re-layouts: 5.24 us -> 6.96 us
    ppermute x12 -> x24, starting transfers between devices: 17.5 us -> 31.5 us  [passed_along(): return lax.ppermute(block, axis, route)]
    ppermute x12 -> x24, waiting for transfers between devices: 51.7 us -> 39.7 us  [passed_along(): return lax.ppermute(block, axis, route)]
    pallas_call x3 -> x7, Pallas kernels: 37.5 us -> 48.6 us  [call(): pl.pallas_call(kernel, out_shape=outs, in_specs=[smem] * scalars + [vmem]...]
    slice x1 -> x2, local copies, waits for them, and re-layouts: 1.42 us -> 2.89 us  [the longest x1 1.46 us: on_device(): behind = gathered(object_slices[:, near:])]
  transfers between devices with their start and end apart: 12 -> 24, of which waited for: 9 -> 8; matrix products, arithmetic and copies ran while one was open for 3% -> 4% of each run, Pallas kernels for 2% -> 22%
where the time goes in v3:
time: 130 us
  Pallas kernels  48.6 us (37%)
  waiting for transfers between devices  39.7 us (31%)
  starting transfers between devices  31.5 us (24%)
  local copies, waits for them, and re-layouts  6.96 us (5%)
  other arithmetic  1.78 us (1%)
    pallas_call x7, Pallas kernels, call(): pl.pallas_call(kernel, out_shape=outs, in_specs=[smem] * scalars + [vmem]...  48.6 us
    ppermute x24, waiting for transfers between devices, passed_along(): return lax.ppermute(block, axis, route)  39.7 us
    ppermute x24, starting transfers between devices, passed_along(): return lax.ppermute(block, axis, route)  31.5 us
  transfers between devices with their start and end apart: 24, of which 8 were waited for; matrix products, arithmetic and copies ran while one was open for 4% of the time, Pallas kernels for 22%

profile of v3, /device:TPU:1, one launch (start us, length us, event | category | flops | bytes accessed | tf_op | source)
XLA Modules:
  0.0 129.6 jit_solution(370600904250630870)
XLA Ops:
  0.6 0.0 copy-start
  0.6 1.4 %fusion = (f32[2,2,64,256]{3,2,1,0:T(8,128)S(1)}, f32[2,2,64,256]{3,2,1,0:T(8,128)S(1)}, f32[2,2,64,256]{3,2,1,0:T(8,128)S(1)}, f32[2,2,64,256]{3,2,1,0:T(8,128)S(1)}) fusion(f32[2,4,256,256]{3,2,1,0:T(8,128)} %refs_10_.1), kind=kLoop, calls=%fused_computation.31 | loop fusion | bytes 2097152 | tf_op jit(solution)/shard_map/slice | solution.py:359
  2.1 5.1 %collective-permute-start.7 = (f32[2,2,64,256]{3,2,1,0:T(8,128)S(1)}, f32[2,2,64,256]{3,2,1,0:T(8,128)S(1)}, u32[]{:S(2)}, u32[]{:S(2)}) collective-permute-start(f32[2,2,64,256]{3,2,1,0:T(8,128)S(1)} %get-tuple-element.52), channel_id=1, source_target_pairs={{4,0},{8,4},{12,8},{16,12},{20,16},{24,20},{28,24},{0,28},{5,1},{9... | collective-permute-start | bytes 786440 | tf_op jit(solution)/shard_map/ppermute | solution.py:18
  7.2 4.2 %collective-permute-start.1 = (f32[2,2,64,256]{3,2,1,0:T(8,128)S(1)}, f32[2,2,64,256]{3,2,1,0:T(8,128)S(1)}, u32[]{:S(2)}, u32[]{:S(2)}) collective-permute-start(f32[2,2,64,256]{3,2,1,0:T(8,128)S(1)} %get-tuple-element.54), channel_id=1, source_target_pairs={{4,0},{8,4},{12,8},{16,12},{20,16},{24,20},{28,24},{0,28},{5,1},{9... | collective-permute-start | bytes 786440 | tf_op jit(solution)/shard_map/ppermute | solution.py:18
  11.4 0.3 slice_bitcast_fusion.1
  11.7 0.1 pad_maximum_fusion.1
  11.9 0.0 copy-start.3
  11.9 1.6 %collective-permute-start.2 = (f32[2,256,128]{2,1,0:T(8,128)S(1)}, f32[2,256,128]{2,1,0:T(8,128)S(1)}, u32[]{:S(2)}, u32[]{:S(2)}) collective-permute-start(f32[2,256,128]{2,1,0:T(8,128)S(1)} %pad_maximum_fusion.1), channel_id=1, source_target_pairs={{1,0},{2,1},{3,2},{0,3},{5,4},{6,5},{7,6},{4,7},{9,8},{10,9},{11,1... | collective-permute-start | bytes 786440 | tf_op jit(solution)/shard_map/ppermute | solution.py:18
  13.4 1.5 %fusion.1 = (f32[2,2,256,256]{3,2,1,0:T(8,128)}, f32[2,2,256,256]{3,2,1,0:T(8,128)}) fusion(f32[2,4,256,256]{3,2,1,0:T(8,128)S(1)} %copy-done), kind=kLoop, calls=%fused_computation.32 | loop fusion | bytes 4194304 | tf_op jit(solution)/shard_map/slice | solution.py:409
  14.9 0.9 cosine_bitcast_fusion
  15.9 0.8 pad_maximum_fusion.phase
  16.7 0.1 pad_maximum_fusion.4
  16.8 0.1 pad_maximum_fusion.3
  17.0 3.8 %shard_map.77 = (f32[2,256,256]{2,1,0:T(8,128)}, f32[2,256,256]{2,1,0:T(8,128)}) custom-call(f32[2,256,256]{2,1,0:T(8,128)} %bitcast.38, f32[2,256,256]{2,1,0:T(8,128)} %pad_maximum_fusion.phase, bf16[2,6,256,256]{3,2,1,0:T(8,128)(2,1)} %constant.2.clone.tables.refs_8_.refs_9_), custom_call_target="tpu_custom_call" | custom-call | bytes 5242880 | tf_op jit(solution)/shard_map/pallas_call | solution.py:386
  20.7 0.1 pad_maximum_fusion.2
  20.9 7.1 %collective-permute-done = f32[2,2,64,256]{3,2,1,0:T(8,128)S(1)} collective-permute-done((f32[2,2,64,256]{3,2,1,0:T(8,128)S(1)}, f32[2,2,64,256]{3,2,1,0:T(8,128)S(1)}, u32[]{:S(2)}, u32[]{:S(2)}) %collective-permute-start) | collective-permute-done | bytes 262176 | tf_op jit(solution)/shard_map/ppermute | solution.py:18
  27.9 1.6 %collective-permute-start.3 = (f32[2,256,128]{2,1,0:T(8,128)S(1)}, f32[2,256,128]{2,1,0:T(8,128)S(1)}, u32[]{:S(2)}, u32[]{:S(2)}) collective-permute-start(f32[2,256,128]{2,1,0:T(8,128)S(1)} %pad_maximum_fusion.2), channel_id=1, source_target_pairs={{3,0},{0,1},{1,2},{2,3},{7,4},{4,5},{5,6},{6,7},{11,8},{8,9},{9,10... | collective-permute-start | bytes 786440 | tf_op jit(solution)/shard_map/ppermute | solution.py:18
  29.6 0.1 collective-permute-start.8
  29.7 0.1 slice_bitcast_fusion.13
  29.8 0.1 pad_maximum_fusion.6
  29.9 0.1 pad_maximum_fusion.5
  30.1 0.7 collective-permute-start.4
  30.7 0.0 collective-permute-done.7
  30.7 1.2 collective-permute-start.5
  32.0 0.1 slice_bitcast_fusion.9
  32.1 0.1 pad_maximum_fusion.8
  32.2 0.1 pad_maximum_fusion.7
  32.3 0.0 collective-permute-done.2.refs_2_
  32.4 0.5 collective-permute-start.9
  32.9 1.9 %collective-permute-done.3.refs_3_ = f32[2,256,128]{2,1,0:T(8,128)S(1)} collective-permute-done((f32[2,256,128]{2,1,0:T(8,128)S(1)}, f32[2,256,128]{2,1,0:T(8,128)S(1)}, u32[]{:S(2)}, u32[]{:S(2)}) %collective-permute-start.3) | collective-permute-done | bytes 262176 | tf_op jit(solution)/shard_map/ppermute | solution.py:18
  34.8 0.3 collective-permute-start.10
  35.1 6.2 %collective-permute-done.4.refs_4_ = f32[2,128,128]{2,1,0:T(8,128)S(1)} collective-permute-done((f32[2,128,128]{2,1,0:T(8,128)S(1)}, f32[2,128,128]{2,1,0:T(8,128)S(1)}, u32[]{:S(2)}, u32[]{:S(2)}) %collective-permute-start.4) | collective-permute-done | bytes 131104 | tf_op jit(solution)/shard_map/ppermute | solution.py:18
  41.4 0.0 collective-permute-start.11
  41.4 0.6 copy-done.22
  42.0 0.0 copy-done.24
  42.0 10.2 %shard_map.78 = (f32[2,3,2,256,256]{4,3,2,1,0:T(8,128)}, f32[2,2,2,256,256]{4,3,2,1,0:T(8,128)}) custom-call(s32[2,2]{1,0:T(2,128)} %bitcast.39, f32[2,2,256,256]{3,2,1,0:T(8,128)} %get-tuple-element.57.refs_0_, f32[2,2,128,256]{3,2,1,0:T(8,128)} %copy-done.1, f32[2,256,128]{2,1,0:T(8,128)} %copy-done.16, f32[2,256,128]{2,1,0:T(8,128)} %copy-done.20, ...), custom_call_target="tpu_custom_call" | custom-call | flops 8589934592 | bytes 11796496 | tf_op jit(solution)/shard_map/pallas_call | solution.py:386
  52.3 0.0 collective-permute-done.9.refs_3_
  52.3 0.0 collective-permute-done.11.refs_5_
  52.4 0.7 copy-done.17
  53.0 0.1 copy-done.21
  53.1 0.1 copy-done.23
  53.2 14.4 %shard_map.79 = (f32[2,2,256,256]{3,2,1,0:T(8,128)}, f32[2,2,128,256]{3,2,1,0:T(8,128)}, f32[2,256,128]{2,1,0:T(8,128)}, f32[2,256,128]{2,1,0:T(8,128)}, f32[2,1...) custom-call(s32[2,2]{1,0:T(2,128)} %bitcast.40, ...), custom_call_target="tpu_custom_call" | custom-call | flops 17179869184 | bytes 13107216 | tf_op jit(solution)/shard_map/pallas_call | solution.py:386
  67.6 0.5 collective-permute-start.20
  68.1 0.2 collective-permute-start.21
  68.3 10.9 %shard_map.80 = (f32[2,2,256,256]{3,2,1,0:T(8,128)}, f32[2,2,128,256]{3,2,1,0:T(8,128)}, f32[2,256,128]{2,1,0:T(8,128)}, f32[2,256,128]{2,1,0:T(8,128)}, f32[2,128,128]{2,1,0:T(8,128)}, /*index=5*/f32[2,128,128]{2,1,0:T(8,128)}) custom-call(s32[2,2]{1,0:T(2,128)} %bitcast.41, f32[2,3,2,256,256]{4,3,2,1,0:T(8,128)} %get-tuple-element.24.refs_6_.waves, ...), custom_call_target="tpu_custom_call" | custom-call | flops 8589934592 | bytes 12320784 | tf_op jit(solution)/shard_map/pallas_call | solution.py:386
  79.1 1.5 %collective-permute-start.12 = (f32[2,256,128]{2,1,0:T(8,128)}, f32[2,256,128]{2,1,0:T(8,128)S(1)}, u32[]{:S(2)}, u32[]{:S(2)}) collective-permute-start(f32[2,256,128]{2,1,0:T(8,128)} %get-tuple-element.29), channel_id=1, source_target_pairs={{3,0},{0,1},{1,2},{2,3},{7,4},{4,5},{5,6},{6,7},{11,8},{8,9},{9,10... | collective-permute-start | bytes 786440 | tf_op jit(solution)/shard_map/ppermute | solution.py:18
  80.7 1.7 %collective-permute-start.18 = (f32[2,256,128]{2,1,0:T(8,128)S(1)}, f32[2,256,128]{2,1,0:T(8,128)S(1)}, u32[]{:S(2)}, u32[]{:S(2)}) collective-permute-start(f32[2,256,128]{2,1,0:T(8,128)S(1)} %copy-done.19), channel_id=1, source_target_pairs={{3,0},{0,1},{1,2},{2,3},{7,4},{4,5},{5,6},{6,7},{11,8},{8,9},{9,10... | collective-permute-start | bytes 786440 | tf_op jit(solution)/shard_map/ppermute | solution.py:18
  82.4 0.1 collective-permute-start.14
  82.5 0.4 collective-permute-start.15
  82.9 0.1 copy-done.12
  83.1 0.1 copy-done.13
  83.2 2.0 %shard_map.82 = (f32[2,2,64,256]{3,2,1,0:T(8,128)}, f32[2,2,64,256]{3,2,1,0:T(8,128)}) custom-call(f32[2,2,128,256]{3,2,1,0:T(8,128)} %get-tuple-element.39.edges, f32[2,128,128]{2,1,0:T(8,128)} %copy-done.12, f32[2,128,128]{2,1,0:T(8,128)} %copy-done.13), custom_call_target="tpu_custom_call" | custom-call | bytes 1310720 | tf_op jit(solution)/shard_map/pallas_call | solution.py:386
  85.2 7.5 %collective-permute-done.14.from_left = f32[2,128,128]{2,1,0:T(8,128)S(1)} collective-permute-done((f32[2,128,128]{2,1,0:T(8,128)}, f32[2,128,128]{2,1,0:T(8,128)S(1)}, u32[]{:S(2)}, u32[]{:S(2)}) %collective-permute-start.14) | collective-permute-done | bytes 131104 | tf_op jit(solution)/shard_map/ppermute | solution.py:18
  92.7 2.3 %collective-permute-start.19 = (f32[2,256,128]{2,1,0:T(8,128)S(1)}, f32[2,256,128]{2,1,0:T(8,128)S(1)}, u32[]{:S(2)}, u32[]{:S(2)}) collective-permute-start(f32[2,256,128]{2,1,0:T(8,128)S(1)} %copy-done.18), channel_id=1, source_target_pairs={{1,0},{2,1},{3,2},{0,3},{5,4},{6,5},{7,6},{4,7},{9,8},{10,9},{11,1... | collective-permute-start | bytes 786440 | tf_op jit(solution)/shard_map/ppermute | solution.py:18
  95.0 2.4 %collective-permute-start.22 = (f32[2,2,64,256]{3,2,1,0:T(8,128)}, f32[2,2,64,256]{3,2,1,0:T(8,128)S(1)}, u32[]{:S(2)}, u32[]{:S(2)}) collective-permute-start(f32[2,2,64,256]{3,2,1,0:T(8,128)} %get-tuple-element.42), channel_id=1, source_target_pairs={{28,0},{0,4},{4,8},{8,12},{12,16},{16,20},{20,24},{24,28},{29,1},{... | collective-permute-start | bytes 786440 | tf_op jit(solution)/shard_map/ppermute | solution.py:18
  97.4 2.0 %shard_map.81 = (f32[2,2,64,256]{3,2,1,0:T(8,128)}, f32[2,2,64,256]{3,2,1,0:T(8,128)}) custom-call(f32[2,2,128,256]{3,2,1,0:T(8,128)} %get-tuple-element.31.edges, f32[2,128,128]{2,1,0:T(8,128)} %copy-done.14, f32[2,128,128]{2,1,0:T(8,128)} %copy-done.15), custom_call_target="tpu_custom_call" | custom-call | bytes 1310720 | tf_op jit(solution)/shard_map/pallas_call | solution.py:386
  99.4 3.0 %collective-permute-start.23 = (f32[2,2,64,256]{3,2,1,0:T(8,128)}, f32[2,2,64,256]{3,2,1,0:T(8,128)S(1)}, u32[]{:S(2)}, u32[]{:S(2)}) collective-permute-start(f32[2,2,64,256]{3,2,1,0:T(8,128)} %get-tuple-element.43), channel_id=1, source_target_pairs={{4,0},{8,4},{12,8},{16,12},{20,16},{24,20},{28,24},{0,28},{5,1},{9... | collective-permute-start | bytes 786440 | tf_op jit(solution)/shard_map/ppermute | solution.py:18
  102.5 4.1 %collective-permute-start.17 = (f32[2,2,64,256]{3,2,1,0:T(8,128)}, f32[2,2,64,256]{3,2,1,0:T(8,128)S(1)}, u32[]{:S(2)}, u32[]{:S(2)}) collective-permute-start(f32[2,2,64,256]{3,2,1,0:T(8,128)} %get-tuple-element.35), channel_id=1, source_target_pairs={{4,0},{8,4},{12,8},{16,12},{20,16},{24,20},{28,24},{0,28},{5,1},{9... | collective-permute-start | bytes 786440 | tf_op jit(solution)/shard_map/ppermute | solution.py:18
  106.6 7.9 %collective-permute-done.22.refs_8_ = f32[2,2,64,256]{3,2,1,0:T(8,128)S(1)} collective-permute-done((f32[2,2,64,256]{3,2,1,0:T(8,128)}, f32[2,2,64,256]{3,2,1,0:T(8,128)S(1)}, u32[]{:S(2)}, u32[]{:S(2)}) %collective-permute-start.22) | collective-permute-done | bytes 262176 | tf_op jit(solution)/shard_map/ppermute | solution.py:18
  114.5 3.5 %collective-permute-done.23.refs_9_ = f32[2,2,64,256]{3,2,1,0:T(8,128)S(1)} collective-permute-done((f32[2,2,64,256]{3,2,1,0:T(8,128)}, f32[2,2,64,256]{3,2,1,0:T(8,128)S(1)}, u32[]{:S(2)}, u32[]{:S(2)}) %collective-permute-start.23) | collective-permute-done | bytes 262176 | tf_op jit(solution)/shard_map/ppermute | solution.py:18
  118.0 2.2 %collective-permute-done.16.refs_3_ = f32[2,2,64,256]{3,2,1,0:T(8,128)S(1)} collective-permute-done((f32[2,2,64,256]{3,2,1,0:T(8,128)}, f32[2,2,64,256]{3,2,1,0:T(8,128)S(1)}, u32[]{:S(2)}, u32[]{:S(2)}) %collective-permute-start.16) | collective-permute-done | bytes 262176 | tf_op jit(solution)/shard_map/ppermute | solution.py:18
  120.2 3.5 %collective-permute-done.17.refs_4_ = f32[2,2,64,256]{3,2,1,0:T(8,128)S(1)} collective-permute-done((f32[2,2,64,256]{3,2,1,0:T(8,128)}, f32[2,2,64,256]{3,2,1,0:T(8,128)S(1)}, u32[]{:S(2)}, u32[]{:S(2)}) %collective-permute-start.17) | collective-permute-done | bytes 262176 | tf_op jit(solution)/shard_map/ppermute | solution.py:18
  123.7 0.7 copy-done.11
  124.3 5.3 %shard_map.83 = (f32[2,4,256,256]{3,2,1,0:T(8,128)}, f32[2,4,256,256]{3,2,1,0:T(8,128)}) custom-call(f32[2,2,256,256]{3,2,1,0:T(8,128)} %get-tuple-element.28.refs_0_, f32[2,256,128]{2,1,0:T(8,128)} %copy-done.4, f32[2,256,128]{2,1,0:T(8,128)} %copy-done.5, f32[2,2,64,256]{3,2,1,0:T(8,128)} %copy-done.10, f32[2,2,64,256]{3,2,1,0:T(8,128)} %copy-done.11, ...), custom_call_target="tpu_custom_call" | custom-call | bytes 10485760 | tf_op jit(solution)/shard_map/pallas_call | solution.py:386
  (62 shorter events, 0.2 us)
Async XLA Ops:
  0.6 10.7 %copy-start = (f32[2,4,256,256]{3,2,1,0:T(8,128)S(1)}, f32[2,4,256,256]{3,2,1,0:T(8,128)}, u32[]{:S(2)}) copy-start(f32[2,4,256,256]{3,2,1,0:T(8,128)} %refs_10_.1) | copy-start | bytes 6291460
  2.1 28.7 %collective-permute-start.7 = (f32[2,2,64,256]{3,2,1,0:T(8,128)S(1)}, f32[2,2,64,256]{3,2,1,0:T(8,128)S(1)}, u32[]{:S(2)}, u32[]{:S(2)}) collective-permute-start(f32[2,2,64,256]{3,2,1,0:T(8,128)S(1)} %get-tuple-element.52), channel_id=1, source_target_pairs={{4,0},{8,4},{12,8},{16,12},{20,16},{24,20},{28,24},{0,28},{5,1},{9... | collective-permute-start | bytes 786440 | tf_op jit(solution)/shard_map/ppermute | solution.py:18
  7.2 22.8 %collective-permute-start.6 = (f32[2,2,64,256]{3,2,1,0:T(8,128)S(1)}, f32[2,2,64,256]{3,2,1,0:T(8,128)S(1)}, u32[]{:S(2)}, u32[]{:S(2)}) collective-permute-start(f32[2,2,64,256]{3,2,1,0:T(8,128)S(1)} %get-tuple-element.53), channel_id=1, source_target_pairs={{28,0},{0,4},{4,8},{8,12},{12,16},{16,20},{20,24},{24,28},{29,1},{... | collective-permute-start | bytes 786440 | tf_op jit(solution)/shard_map/ppermute | solution.py:18
  7.2 22.4 %collective-permute-start.1 = (f32[2,2,64,256]{3,2,1,0:T(8,128)S(1)}, f32[2,2,64,256]{3,2,1,0:T(8,128)S(1)}, u32[]{:S(2)}, u32[]{:S(2)}) collective-permute-start(f32[2,2,64,256]{3,2,1,0:T(8,128)S(1)} %get-tuple-element.54), channel_id=1, source_target_pairs={{4,0},{8,4},{12,8},{16,12},{20,16},{24,20},{28,24},{0,28},{5,1},{9... | collective-permute-start | bytes 786440 | tf_op jit(solution)/shard_map/ppermute | solution.py:18
  11.4 16.6 %collective-permute-start = (f32[2,2,64,256]{3,2,1,0:T(8,128)S(1)}, f32[2,2,64,256]{3,2,1,0:T(8,128)S(1)}, u32[]{:S(2)}, u32[]{:S(2)}) collective-permute-start(f32[2,2,64,256]{3,2,1,0:T(8,128)S(1)} %get-tuple-element.55), channel_id=1, source_target_pairs={{28,0},{0,4},{4,8},{8,12},{12,16},{16,20},{20,24},{24,28},{29,1},{... | collective-permute-start | bytes 786440 | tf_op jit(solution)/shard_map/ppermute | solution.py:18
  11.9 3.0 %copy-start.3 = (f32[256,256]{1,0:T(8,128)S(1)}, f32[256,256]{1,0:T(8,128)}, u32[]{:S(2)}) copy-start(f32[256,256]{1,0:T(8,128)} %param.10) | copy-start | bytes 786436
  11.9 20.5 %collective-permute-start.2 = (f32[2,256,128]{2,1,0:T(8,128)S(1)}, f32[2,256,128]{2,1,0:T(8,128)S(1)}, u32[]{:S(2)}, u32[]{:S(2)}) collective-permute-start(f32[2,256,128]{2,1,0:T(8,128)S(1)} %pad_maximum_fusion.1), channel_id=1, source_target_pairs={{1,0},{2,1},{3,2},{0,3},{5,4},{6,5},{7,6},{4,7},{9,8},{10,9},{11,1... | collective-permute-start | bytes 786440 | tf_op jit(solution)/shard_map/ppermute | solution.py:18
  27.9 6.9 %collective-permute-start.3 = (f32[2,256,128]{2,1,0:T(8,128)S(1)}, f32[2,256,128]{2,1,0:T(8,128)S(1)}, u32[]{:S(2)}, u32[]{:S(2)}) collective-permute-start(f32[2,256,128]{2,1,0:T(8,128)S(1)} %pad_maximum_fusion.2), channel_id=1, source_target_pairs={{3,0},{0,1},{1,2},{2,3},{7,4},{4,5},{5,6},{6,7},{11,8},{8,9},{9,10... | collective-permute-start | bytes 786440 | tf_op jit(solution)/shard_map/ppermute | solution.py:18
  29.6 22.7 %collective-permute-start.8 = (f32[2,256,128]{2,1,0:T(8,128)S(1)}, f32[2,256,128]{2,1,0:T(8,128)S(1)}, u32[]{:S(2)}, u32[]{:S(2)}) collective-permute-start(f32[2,256,128]{2,1,0:T(8,128)S(1)} %pad_maximum_fusion.3), channel_id=1, source_target_pairs={{1,0},{2,1},{3,2},{0,3},{5,4},{6,5},{7,6},{4,7},{9,8},{10,9},{11,1... | collective-permute-start | bytes 786440 | tf_op jit(solution)/shard_map/ppermute | solution.py:18
  29.7 2.5 %copy-start.1 = (f32[2,2,128,256]{3,2,1,0:T(8,128)}, f32[2,2,128,256]{3,2,1,0:T(8,128)S(1)}, u32[]{:S(2)}) copy-start(f32[2,2,128,256]{3,2,1,0:T(8,128)S(1)} %constant_dynamic-update-slice_fusion.refs_1_) | copy-start | bytes 1572868
  30.1 11.3 %collective-permute-start.4 = (f32[2,128,128]{2,1,0:T(8,128)S(1)}, f32[2,128,128]{2,1,0:T(8,128)S(1)}, u32[]{:S(2)}, u32[]{:S(2)}) collective-permute-start(f32[2,128,128]{2,1,0:T(8,128)S(1)} %pad_maximum_fusion.5), channel_id=1, source_target_pairs={{1,0},{2,1},{3,2},{0,3},{5,4},{6,5},{7,6},{4,7},{9,8},{10,9},{11,1... | collective-permute-start | bytes 393224 | tf_op jit(solution)/shard_map/ppermute | solution.py:18
  30.7 10.6 %collective-permute-start.5 = (f32[2,128,128]{2,1,0:T(8,128)S(1)}, f32[2,128,128]{2,1,0:T(8,128)S(1)}, u32[]{:S(2)}, u32[]{:S(2)}) collective-permute-start(f32[2,128,128]{2,1,0:T(8,128)S(1)} %pad_maximum_fusion.6), channel_id=1, source_target_pairs={{3,0},{0,1},{1,2},{2,3},{7,4},{4,5},{5,6},{6,7},{11,8},{8,9},{9,10... | collective-permute-start | bytes 393224 | tf_op jit(solution)/shard_map/ppermute | solution.py:18
  32.0 20.3 %copy-start.2 = (f32[2,2,128,256]{3,2,1,0:T(8,128)}, f32[2,2,128,256]{3,2,1,0:T(8,128)S(1)}, u32[]{:S(2)}) copy-start(f32[2,2,128,256]{3,2,1,0:T(8,128)S(1)} %constant_dynamic-update-slice_fusion.2.refs_1_) | copy-start | bytes 1572868
  32.3 9.0 %copy-start.16 = (f32[2,256,128]{2,1,0:T(8,128)}, f32[2,256,128]{2,1,0:T(8,128)S(1)}, u32[]{:S(2)}) copy-start(f32[2,256,128]{2,1,0:T(8,128)S(1)} %collective-permute-done.2.refs_2_) | copy-start | bytes 786436
  32.4 19.9 %collective-permute-start.9 = (f32[2,256,128]{2,1,0:T(8,128)S(1)}, f32[2,256,128]{2,1,0:T(8,128)S(1)}, u32[]{:S(2)}, u32[]{:S(2)}) collective-permute-start(f32[2,256,128]{2,1,0:T(8,128)S(1)} %pad_maximum_fusion.4), channel_id=1, source_target_pairs={{3,0},{0,1},{1,2},{2,3},{7,4},{4,5},{5,6},{6,7},{11,8},{8,9},{9,10... | collective-permute-start | bytes 786440 | tf_op jit(solution)/shard_map/ppermute | solution.py:18
  34.8 6.6 %copy-start.20 = (f32[2,256,128]{2,1,0:T(8,128)}, f32[2,256,128]{2,1,0:T(8,128)S(1)}, u32[]{:S(2)}) copy-start(f32[2,256,128]{2,1,0:T(8,128)S(1)} %collective-permute-done.3.refs_3_) | copy-start | bytes 786436
  34.8 17.5 %collective-permute-start.10 = (f32[2,128,128]{2,1,0:T(8,128)S(1)}, f32[2,128,128]{2,1,0:T(8,128)S(1)}, u32[]{:S(2)}, u32[]{:S(2)}) collective-permute-start(f32[2,128,128]{2,1,0:T(8,128)S(1)} %pad_maximum_fusion.7), channel_id=1, source_target_pairs={{1,0},{2,1},{3,2},{0,3},{5,4},{6,5},{7,6},{4,7},{9,8},{10,9},{11,1... | collective-permute-start | bytes 393224 | tf_op jit(solution)/shard_map/ppermute | solution.py:18
  41.4 0.6 copy-start.22
  41.4 11.0 %collective-permute-start.11 = (f32[2,128,128]{2,1,0:T(8,128)S(1)}, f32[2,128,128]{2,1,0:T(8,128)S(1)}, u32[]{:S(2)}, u32[]{:S(2)}) collective-permute-start(f32[2,128,128]{2,1,0:T(8,128)S(1)} %pad_maximum_fusion.8), channel_id=1, source_target_pairs={{3,0},{0,1},{1,2},{2,3},{7,4},{4,5},{5,6},{6,7},{11,8},{8,9},{9,10... | collective-permute-start | bytes 393224 | tf_op jit(solution)/shard_map/ppermute | solution.py:18
  41.4 0.7 copy-start.24
  52.3 0.7 copy-start.17
  52.3 0.8 copy-start.21
  52.3 0.8 copy-start.23
  52.3 0.8 copy-start.25
  67.6 14.8 %collective-permute-start.20 = (f32[2,128,128]{2,1,0:T(8,128)}, f32[2,128,128]{2,1,0:T(8,128)S(1)}, u32[]{:S(2)}, u32[]{:S(2)}) collective-permute-start(f32[2,128,128]{2,1,0:T(8,128)} %get-tuple-element.40), channel_id=1, source_target_pairs={{3,0},{0,1},{1,2},{2,3},{7,4},{4,5},{5,6},{6,7},{11,8},{8,9},{9,10... | collective-permute-start | bytes 393224 | tf_op jit(solution)/shard_map/ppermute | solution.py:18
  68.1 14.4 %collective-permute-start.21 = (f32[2,128,128]{2,1,0:T(8,128)}, f32[2,128,128]{2,1,0:T(8,128)S(1)}, u32[]{:S(2)}, u32[]{:S(2)}) collective-permute-start(f32[2,128,128]{2,1,0:T(8,128)} %get-tuple-element.41), channel_id=1, source_target_pairs={{1,0},{2,1},{3,2},{0,3},{5,4},{6,5},{7,6},{4,7},{9,8},{10,9},{11,1... | collective-permute-start | bytes 393224 | tf_op jit(solution)/shard_map/ppermute | solution.py:18
  68.3 12.4 %copy-start.19 = (f32[2,256,128]{2,1,0:T(8,128)S(1)}, f32[2,256,128]{2,1,0:T(8,128)}, u32[]{:S(2)}) copy-start(f32[2,256,128]{2,1,0:T(8,128)} %get-tuple-element.37) | copy-start | bytes 786436
  68.3 24.5 %copy-start.18 = (f32[2,256,128]{2,1,0:T(8,128)S(1)}, f32[2,256,128]{2,1,0:T(8,128)}, u32[]{:S(2)}) copy-start(f32[2,256,128]{2,1,0:T(8,128)} %get-tuple-element.38) | copy-start | bytes 786436
  79.1 20.3 %collective-permute-start.12 = (f32[2,256,128]{2,1,0:T(8,128)}, f32[2,256,128]{2,1,0:T(8,128)S(1)}, u32[]{:S(2)}, u32[]{:S(2)}) collective-permute-start(f32[2,256,128]{2,1,0:T(8,128)} %get-tuple-element.29), channel_id=1, source_target_pairs={{3,0},{0,1},{1,2},{2,3},{7,4},{4,5},{5,6},{6,7},{11,8},{8,9},{9,10... | collective-permute-start | bytes 786440 | tf_op jit(solution)/shard_map/ppermute | solution.py:18
  80.7 21.8 %collective-permute-start.13 = (f32[2,256,128]{2,1,0:T(8,128)}, f32[2,256,128]{2,1,0:T(8,128)S(1)}, u32[]{:S(2)}, u32[]{:S(2)}) collective-permute-start(f32[2,256,128]{2,1,0:T(8,128)} %get-tuple-element.30), channel_id=1, source_target_pairs={{1,0},{2,1},{3,2},{0,3},{5,4},{6,5},{7,6},{4,7},{9,8},{10,9},{11,1... | collective-permute-start | bytes 786440 | tf_op jit(solution)/shard_map/ppermute | solution.py:18
  80.7 21.8 %collective-permute-start.18 = (f32[2,256,128]{2,1,0:T(8,128)S(1)}, f32[2,256,128]{2,1,0:T(8,128)S(1)}, u32[]{:S(2)}, u32[]{:S(2)}) collective-permute-start(f32[2,256,128]{2,1,0:T(8,128)S(1)} %copy-done.19), channel_id=1, source_target_pairs={{3,0},{0,1},{1,2},{2,3},{7,4},{4,5},{5,6},{6,7},{11,8},{8,9},{9,10... | collective-permute-start | bytes 786440 | tf_op jit(solution)/shard_map/ppermute | solution.py:18
  82.4 0.7 copy-start.12
  82.4 10.3 %collective-permute-start.14 = (f32[2,128,128]{2,1,0:T(8,128)}, f32[2,128,128]{2,1,0:T(8,128)S(1)}, u32[]{:S(2)}, u32[]{:S(2)}) collective-permute-start(f32[2,128,128]{2,1,0:T(8,128)} %get-tuple-element.32), channel_id=1, source_target_pairs={{3,0},{0,1},{1,2},{2,3},{7,4},{4,5},{5,6},{6,7},{11,8},{8,9},{9,10... | collective-permute-start | bytes 393224 | tf_op jit(solution)/shard_map/ppermute | solution.py:18
  82.5 0.7 copy-start.13
  82.5 12.5 %collective-permute-start.15 = (f32[2,128,128]{2,1,0:T(8,128)}, f32[2,128,128]{2,1,0:T(8,128)S(1)}, u32[]{:S(2)}, u32[]{:S(2)}) collective-permute-start(f32[2,128,128]{2,1,0:T(8,128)} %get-tuple-element.33), channel_id=1, source_target_pairs={{1,0},{2,1},{3,2},{0,3},{5,4},{6,5},{7,6},{4,7},{9,8},{10,9},{11,1... | collective-permute-start | bytes 393224 | tf_op jit(solution)/shard_map/ppermute | solution.py:18
  92.7 4.7 %copy-start.14 = (f32[2,128,128]{2,1,0:T(8,128)}, f32[2,128,128]{2,1,0:T(8,128)S(1)}, u32[]{:S(2)}) copy-start(f32[2,128,128]{2,1,0:T(8,128)S(1)} %collective-permute-done.14.from_left) | copy-start | bytes 393220
  92.7 13.9 %collective-permute-start.19 = (f32[2,256,128]{2,1,0:T(8,128)S(1)}, f32[2,256,128]{2,1,0:T(8,128)S(1)}, u32[]{:S(2)}, u32[]{:S(2)}) collective-permute-start(f32[2,256,128]{2,1,0:T(8,128)S(1)} %copy-done.18), channel_id=1, source_target_pairs={{1,0},{2,1},{3,2},{0,3},{5,4},{6,5},{7,6},{4,7},{9,8},{10,9},{11,1... | collective-permute-start | bytes 786440 | tf_op jit(solution)/shard_map/ppermute | solution.py:18
  95.0 2.4 %copy-start.15 = (f32[2,128,128]{2,1,0:T(8,128)}, f32[2,128,128]{2,1,0:T(8,128)S(1)}, u32[]{:S(2)}) copy-start(f32[2,128,128]{2,1,0:T(8,128)S(1)} %collective-permute-done.15.from_right) | copy-start | bytes 393220
  95.0 19.5 %collective-permute-start.22 = (f32[2,2,64,256]{3,2,1,0:T(8,128)}, f32[2,2,64,256]{3,2,1,0:T(8,128)S(1)}, u32[]{:S(2)}, u32[]{:S(2)}) collective-permute-start(f32[2,2,64,256]{3,2,1,0:T(8,128)} %get-tuple-element.42), channel_id=1, source_target_pairs={{28,0},{0,4},{4,8},{8,12},{12,16},{16,20},{20,24},{24,28},{29,1},{... | collective-permute-start | bytes 786440 | tf_op jit(solution)/shard_map/ppermute | solution.py:18
  99.4 24.2 %copy-start.4 = (f32[2,256,128]{2,1,0:T(8,128)}, f32[2,256,128]{2,1,0:T(8,128)S(1)}, u32[]{:S(2)}) copy-start(f32[2,256,128]{2,1,0:T(8,128)S(1)} %collective-permute-done.12.refs_1_) | copy-start | bytes 786436
  99.4 18.6 %collective-permute-start.23 = (f32[2,2,64,256]{3,2,1,0:T(8,128)}, f32[2,2,64,256]{3,2,1,0:T(8,128)S(1)}, u32[]{:S(2)}, u32[]{:S(2)}) collective-permute-start(f32[2,2,64,256]{3,2,1,0:T(8,128)} %get-tuple-element.43), channel_id=1, source_target_pairs={{4,0},{8,4},{12,8},{16,12},{20,16},{24,20},{28,24},{0,28},{5,1},{9... | collective-permute-start | bytes 786440 | tf_op jit(solution)/shard_map/ppermute | solution.py:18
  102.5 21.2 %copy-start.5 = (f32[2,256,128]{2,1,0:T(8,128)}, f32[2,256,128]{2,1,0:T(8,128)S(1)}, u32[]{:S(2)}) copy-start(f32[2,256,128]{2,1,0:T(8,128)S(1)} %collective-permute-done.13.refs_2_) | copy-start | bytes 786436
  102.5 17.7 %collective-permute-start.16 = (f32[2,2,64,256]{3,2,1,0:T(8,128)}, f32[2,2,64,256]{3,2,1,0:T(8,128)S(1)}, u32[]{:S(2)}, u32[]{:S(2)}) collective-permute-start(f32[2,2,64,256]{3,2,1,0:T(8,128)} %get-tuple-element.34), channel_id=1, source_target_pairs={{28,0},{0,4},{4,8},{8,12},{12,16},{16,20},{20,24},{24,28},{29,1},{... | collective-permute-start | bytes 786440 | tf_op jit(solution)/shard_map/ppermute | solution.py:18
  102.5 21.1 %copy-start.6 = (f32[2,256,128]{2,1,0:T(8,128)}, f32[2,256,128]{2,1,0:T(8,128)S(1)}, u32[]{:S(2)}) copy-start(f32[2,256,128]{2,1,0:T(8,128)S(1)} %collective-permute-done.18.refs_6_) | copy-start | bytes 786436
  102.5 21.1 %collective-permute-start.17 = (f32[2,2,64,256]{3,2,1,0:T(8,128)}, f32[2,2,64,256]{3,2,1,0:T(8,128)S(1)}, u32[]{:S(2)}, u32[]{:S(2)}) collective-permute-start(f32[2,2,64,256]{3,2,1,0:T(8,128)} %get-tuple-element.35), channel_id=1, source_target_pairs={{4,0},{8,4},{12,8},{16,12},{20,16},{24,20},{28,24},{0,28},{5,1},{9... | collective-permute-start | bytes 786440 | tf_op jit(solution)/shard_map/ppermute | solution.py:18
  106.6 17.0 %copy-start.7 = (f32[2,256,128]{2,1,0:T(8,128)}, f32[2,256,128]{2,1,0:T(8,128)S(1)}, u32[]{:S(2)}) copy-start(f32[2,256,128]{2,1,0:T(8,128)S(1)} %collective-permute-done.19.refs_7_) | copy-start | bytes 786436
  114.5 9.1 %copy-start.8 = (f32[2,2,64,256]{3,2,1,0:T(8,128)}, f32[2,2,64,256]{3,2,1,0:T(8,128)S(1)}, u32[]{:S(2)}) copy-start(f32[2,2,64,256]{3,2,1,0:T(8,128)S(1)} %collective-permute-done.22.refs_8_) | copy-start | bytes 786436
  118.0 5.7 %copy-start.9 = (f32[2,2,64,256]{3,2,1,0:T(8,128)}, f32[2,2,64,256]{3,2,1,0:T(8,128)S(1)}, u32[]{:S(2)}) copy-start(f32[2,2,64,256]{3,2,1,0:T(8,128)S(1)} %collective-permute-done.23.refs_9_) | copy-start | bytes 786436
  120.2 3.5 %copy-start.10 = (f32[2,2,64,256]{3,2,1,0:T(8,128)}, f32[2,2,64,256]{3,2,1,0:T(8,128)S(1)}, u32[]{:S(2)}) copy-start(f32[2,2,64,256]{3,2,1,0:T(8,128)S(1)} %collective-permute-done.16.refs_3_) | copy-start | bytes 786436
  123.6 0.7 copy-start.11

commit v4 on v2

--- a/solution.py
+++ b/solution.py
@@ -133,13 +133,23 @@
     return lax.broadcasted_iota(jnp.int32, value.shape, value.ndim - 1) < HALO
 
 
+def entry_kernel(measured, phase, tables, ordered, phases):
+    def pairs(index):
+        return tables[0, index], tables[1, index]
+
+    for c in range(2):
+        phases[c] = by_parity(phase[c], pairs)
+    for k in range(measured.shape[0]):
+        ordered[k] = by_parity(measured[k], pairs)
+
+
 def step_kernel(
-    offsets, core, edges, right, left, right_ends, left_ends, measured, probe, phase, tables,
+    offsets, core, edges, right, left, right_ends, left_ends, ordered, probe, phases, tables,
     out, out_edges, to_right, to_left, to_right_ends, to_left_ends,
-    ext, total, windows, waves, ordered, phases,
+    ext, total, windows, waves,
 ):
-    count = measured.shape[0]
-    width = measured.shape[-1]
+    count = ordered.shape[0]
+    width = ordered.shape[-1]
     layers = core.shape[1]
     last = layers - 1
     tall = core.shape[2]
@@ -167,11 +177,8 @@
 
     lax.fori_loop(0, layers, gather, 0)
     total[...] = jnp.zeros_like(total)
-    for c in range(2):
-        phases[c] = by_parity(phase[c], pairs)
     for k in range(count):
         waves[k, 0] = probe[...]
-        ordered[k] = by_parity(measured[k], pairs)
 
     def cut_layer(k, layer):
         rows, shift = row_place(offsets[k, 0], whole, width)
@@ -304,6 +311,13 @@
     wide = broad // 128
     tables = jnp.asarray(half_tables(width))
     phase = jnp.stack([jnp.cos(propagator), jnp.sin(propagator)])
+    ordered, phases = pl.pallas_call(
+        entry_kernel,
+        out_shape=[like(measured), like(phase)],
+        in_specs=[pl.BlockSpec(memory_space=pltpu.VMEM)] * 3,
+        out_specs=[pl.BlockSpec(memory_space=pltpu.VMEM)] * 2,
+        cost_estimate=pl.CostEstimate(flops=2**30, bytes_accessed=2**22, transcendentals=0),
+    )(measured, phase, tables)
     above = passed_along(object_slices[:, :, tall - HALO :], "row", 1)
     below = passed_along(object_slices[:, :, :HALO], "row", -1)
     head, tail = packed(object_slices)
@@ -325,13 +339,11 @@
             pltpu.VMEM((2, layers, wide + 1, tall + 2 * HALO, 128), jnp.float32),
             pltpu.VMEM((count, layers, 2, width, width), jnp.float32),
             pltpu.VMEM((count, layers, 2, width, width), jnp.float32),
-            pltpu.VMEM((count, width, width), jnp.float32),
-            pltpu.VMEM((2, width, width), jnp.float32),
         ],
         compiler_params=limit,
     )(
         positions[0, 0], object_slices, edges, right, left, right_ends, left_ends,
-        measured, probe, phase, tables,
+        ordered, probe, phases, tables,
     )
     left_ends = passed_along(to_right_ends, "col", 1)
     right_ends = passed_along(to_left_ends, "col", -1)
@@ -346,12 +358,16 @@
     )(edges, left_ends, right_ends)
     from_above = passed_along(down, "row", 1)
     from_below = passed_along(up, "row", -1)
+    plane = pl.BlockSpec((2, 1, tall, broad), lambda layer: (0, layer, 0, 0))
+    strip = pl.BlockSpec((1, tall, 128), lambda layer: (layer, 0, 0))
+    border = pl.BlockSpec((2, 1, HALO, broad), lambda layer: (0, layer, 0, 0))
     return tuple(
         pl.pallas_call(
             final_kernel,
+            grid=(layers,),
             out_shape=[like(cells), like(cells)],
-            in_specs=[vmem] * 6,
-            out_specs=[vmem] * 2,
+            in_specs=[plane, strip, strip, border, border, plane],
+            out_specs=[plane, plane],
             compiler_params=limit,
         )(cells, left, right, from_above, from_below, object_slices)
     )

time: 115 us -> 114 us (level)
  waiting for transfers between devices: 51.7 us -> 47.7 us
  Pallas kernels: 37.5 us -> 40 us
  other arithmetic: 1.54 us -> 2.98 us
    ppermute x12, waiting for transfers between devices: 51.7 us -> 47.7 us  [passed_along(): return lax.ppermute(block, axis, route)]
    pallas_call x1 -> x2, Pallas kernels: 5.29 us -> 9.08 us  [the longest x1 5.29 us: on_device(): pl.pallas_call(final_kernel, grid=(layers,), out_shape=[like(cells), like...]
    pallas_call x1, Pallas kernels: 29.8 us -> 28.4 us  [on_device(): pl.pallas_call(step_kernel, out_shape=[like(v) for v in (object_slices, e...]
    unnamed x27 -> x25, local copies, waits for them, and re-layouts: 2.28 us -> 2.55 us
  transfers between devices with their start and end apart: 12 -> 12, of which waited for: 9 -> 7; matrix products, arithmetic and copies ran while one was open for 3% -> 4% of each run, Pallas kernels for 2% -> 6%
where the time goes in v4:
time: 114 us; the launch traced here: 113 us
  waiting for transfers between devices  47.7 us (42%)
  Pallas kernels  40 us (35%)
  starting transfers between devices  16.5 us (14%)
  local copies, waits for them, and re-layouts  5.51 us (5%)
  other arithmetic  2.98 us (3%)
    ppermute x12, waiting for transfers between devices, passed_along(): return lax.ppermute(block, axis, route)  47.7 us
    pallas_call x1, Pallas kernels, on_device(): pl.pallas_call(step_kernel, out_shape=[like(v) for v in (object_slices, e...  28.4 us
    ppermute x12, starting transfers between devices, passed_along(): return lax.ppermute(block, axis, route)  16.5 us
    pallas_call x1, Pallas kernels, on_device(): pl.pallas_call(final_kernel, grid=(layers,), out_shape=[like(cells), like...  5.29 us
    pallas_call x1, Pallas kernels, on_device(): pl.pallas_call(entry_kernel, out_shape=[like(measured), like(phase)], in_...  3.78 us
    unnamed x25, local copies, waits for them, and re-layouts  2.55 us
    pallas_call x1, Pallas kernels, on_device(): pl.pallas_call(edges_kernel, out_shape=[like(above), like(below)], in_spe...  2.47 us
  transfers between devices with their start and end apart: 12, of which 7 were waited for; matrix products, arithmetic and copies ran while one was open for 4% of the time, Pallas kernels for 6%

profile of v4, /device:TPU:1, one launch (start us, length us, event | category | flops | bytes accessed | tf_op | source)
XLA Modules:
  0.0 113.4 jit_solution(8822574819137049259)
XLA Ops:
  0.6 0.0 copy-start
  0.6 1.4 %fusion = (f32[2,4,64,256]{3,2,1,0:T(8,128)S(1)}, f32[2,4,64,256]{3,2,1,0:T(8,128)S(1)}) fusion(f32[2,4,256,256]{3,2,1,0:T(8,128)} %objects.1), kind=kLoop, calls=%fused_computation.17 | loop fusion | bytes 2097152 | tf_op jit(solution)/shard_map/slice | solution.py:322
  2.1 5.1 %collective-permute-start.1 = (f32[2,4,64,256]{3,2,1,0:T(8,128)S(1)}, f32[2,4,64,256]{3,2,1,0:T(8,128)S(1)}, u32[]{:S(2)}, u32[]{:S(2)}) collective-permute-start(f32[2,4,64,256]{3,2,1,0:T(8,128)S(1)} %get-tuple-element.26), channel_id=1, source_target_pairs={{4,0},{8,4},{12,8},{16,12},{20,16},{24,20},{28,24},{0,28},{5,1},{9... | collective-permute-start | bytes 1572872 | tf_op jit(solution)/shard_map/ppermute | solution.py:18
  7.2 0.0 collective-permute-start
  7.2 0.0 copy-done
  7.2 0.3 slice_bitcast_fusion.1
  7.5 0.2 pad_maximum_fusion
  7.8 1.0 collective-permute-start.2
  8.8 0.2 pad_maximum_fusion.1
  9.0 1.2 %collective-permute-start.3 = (f32[4,256,128]{2,1,0:T(8,128)S(1)}, f32[4,256,128]{2,1,0:T(8,128)S(1)}, u32[]{:S(2)}, u32[]{:S(2)}) collective-permute-start(f32[4,256,128]{2,1,0:T(8,128)S(1)} %pad_maximum_fusion.1), channel_id=1, source_target_pairs={{3,0},{0,1},{1,2},{2,3},{7,4},{4,5},{5,6},{6,7},{11,8},{8,9},{9,10... | collective-permute-start | bytes 1572872 | tf_op jit(solution)/shard_map/ppermute | solution.py:18
  10.2 17.8 %collective-permute-done = f32[2,4,64,256]{3,2,1,0:T(8,128)S(1)} collective-permute-done((f32[2,4,64,256]{3,2,1,0:T(8,128)S(1)}, f32[2,4,64,256]{3,2,1,0:T(8,128)S(1)}, u32[]{:S(2)}, u32[]{:S(2)}) %collective-permute-start) | collective-permute-done | bytes 524320 | tf_op jit(solution)/shard_map/ppermute | solution.py:18
  28.0 0.0 collective-permute-done.1
  28.0 0.0 copy-start.1
  28.0 0.0 copy-start.8
  28.0 0.2 slice_bitcast_fusion.5
  28.3 0.9 pad_maximum_fusion.3
  29.2 0.5 collective-permute-start.4
  29.6 0.8 pad_maximum_fusion.4
  30.5 1.3 %collective-permute-start.5 = (f32[4,128,128]{2,1,0:T(8,128)}, f32[4,128,128]{2,1,0:T(8,128)}, u32[]{:S(2)}, u32[]{:S(2)}) collective-permute-start(f32[4,128,128]{2,1,0:T(8,128)} %pad_maximum_fusion.4), channel_id=1, source_target_pairs={{3,0},{0,1},{1,2},{2,3},{7,4},{4,5},{5,6},{6,7},{11,8},{8,9},{9,10... | collective-permute-start | bytes 786440 | tf_op jit(solution)/shard_map/ppermute | solution.py:18
  31.7 0.0 copy-done.8
  31.7 0.9 cosine_bitcast_fusion
  32.7 0.0 copy-done.1
  32.7 0.8 pad_maximum_fusion.2.phase
  33.5 3.8 %shard_map.77 = (f32[2,256,256]{2,1,0:T(8,128)}, f32[2,256,256]{2,1,0:T(8,128)}) custom-call(f32[2,256,256]{2,1,0:T(8,128)} %bitcast.23, f32[2,256,256]{2,1,0:T(8,128)} %pad_maximum_fusion.2.phase, bf16[2,6,256,256]{3,2,1,0:T(8,128)(2,1)} %constant.2.clone.tables), custom_call_target="tpu_custom_call" | custom-call | flops 1073741824 | bytes 4194304 | tf_op jit(solution)/shard_map/pallas_call | solution.py:314
  37.3 0.0 collective-permute-done.2.right
  37.3 0.0 copy-start.2
  37.3 0.0 collective-permute-done.3.left
  37.3 0.0 copy-start.3
  37.3 0.0 collective-permute-done.4.right_ends
  37.4 0.0 copy-start.9
  37.4 0.0 collective-permute-done.5.left_ends
  37.4 0.7 copy-done.2
  38.1 0.1 copy-done.3
  38.3 0.1 copy-done.9
  38.4 28.4 %shard_map.78 = (f32[2,4,256,256]{3,2,1,0:T(8,128)}, f32[2,4,128,256]{3,2,1,0:T(8,128)}, f32[4,256,128]{2,1,0:T(8,128)}, f32[4,256,128]{2,1,0:T(8,128)}, f32[4,128,128]{2,1,0:T(8,128)}, /*index=5*/f32[4,128,128]{2,1,0:T(8,128)}) custom-call(s32[2,2]{1,0:T(2,128)} %bitcast.22, f32[2,4,256,256]{3,2,1,0:T(8,128)} %objects.1, f32[2,4,128,256]{3,2,1,0:T(8,128)} %copy-done.1, ...), custom_call_target="tpu_custom_call" | custom-call | tf_op jit(solution)/shard_map/pallas_call | solution.py:332
  66.8 1.5 %collective-permute-start.8 = (f32[4,128,128]{2,1,0:T(8,128)}, f32[4,128,128]{2,1,0:T(8,128)S(1)}, u32[]{:S(2)}, u32[]{:S(2)}) collective-permute-start(f32[4,128,128]{2,1,0:T(8,128)} %get-tuple-element.18), channel_id=1, source_target_pairs={{3,0},{0,1},{1,2},{2,3},{7,4},{4,5},{5,6},{6,7},{11,8},{8,9},{9,10... | collective-permute-start | bytes 786440 | tf_op jit(solution)/shard_map/ppermute | solution.py:18
  68.3 0.0 collective-permute-start.9
  68.3 1.7 %collective-permute-start.6 = (f32[4,256,128]{2,1,0:T(8,128)}, f32[4,256,128]{2,1,0:T(8,128)S(1)}, u32[]{:S(2)}, u32[]{:S(2)}) collective-permute-start(f32[4,256,128]{2,1,0:T(8,128)} %get-tuple-element.15), channel_id=1, source_target_pairs={{3,0},{0,1},{1,2},{2,3},{7,4},{4,5},{5,6},{6,7},{11,8},{8,9},{9,10... | collective-permute-start | bytes 1572872 | tf_op jit(solution)/shard_map/ppermute | solution.py:18
  70.1 0.0 collective-permute-start.7
  70.1 3.7 %collective-permute-done.8.from_left = f32[4,128,128]{2,1,0:T(8,128)S(1)} collective-permute-done((f32[4,128,128]{2,1,0:T(8,128)}, f32[4,128,128]{2,1,0:T(8,128)S(1)}, u32[]{:S(2)}, u32[]{:S(2)}) %collective-permute-start.8) | collective-permute-done | bytes 262176 | tf_op jit(solution)/shard_map/ppermute | solution.py:18
  73.8 0.0 copy-start.10
  73.8 3.7 %collective-permute-done.9.from_right = f32[4,128,128]{2,1,0:T(8,128)S(1)} collective-permute-done((f32[4,128,128]{2,1,0:T(8,128)}, f32[4,128,128]{2,1,0:T(8,128)S(1)}, u32[]{:S(2)}, u32[]{:S(2)}) %collective-permute-start.9) | collective-permute-done | bytes 262176 | tf_op jit(solution)/shard_map/ppermute | solution.py:18
  77.4 0.0 copy-start.11
  77.4 0.0 copy-done.10
  77.4 0.7 copy-done.11
  78.1 2.5 %shard_map.79 = (f32[2,4,64,256]{3,2,1,0:T(8,128)}, f32[2,4,64,256]{3,2,1,0:T(8,128)}) custom-call(f32[2,4,128,256]{3,2,1,0:T(8,128)} %get-tuple-element.17.edges, f32[4,128,128]{2,1,0:T(8,128)} %copy-done.10, f32[4,128,128]{2,1,0:T(8,128)} %copy-done.11), custom_call_target="tpu_custom_call" | custom-call | tf_op jit(solution)/shard_map/pallas_call | solution.py:352
  80.6 2.2 %collective-permute-start.10 = (f32[2,4,64,256]{3,2,1,0:T(8,128)}, f32[2,4,64,256]{3,2,1,0:T(8,128)S(1)}, u32[]{:S(2)}, u32[]{:S(2)}) collective-permute-start(f32[2,4,64,256]{3,2,1,0:T(8,128)} %get-tuple-element.20), channel_id=1, source_target_pairs={{28,0},{0,4},{4,8},{8,12},{12,16},{16,20},{20,24},{24,28},{29,1},{... | collective-permute-start | bytes 1572872 | tf_op jit(solution)/shard_map/ppermute | solution.py:18
  82.8 1.9 %collective-permute-start.11 = (f32[2,4,64,256]{3,2,1,0:T(8,128)}, f32[2,4,64,256]{3,2,1,0:T(8,128)S(1)}, u32[]{:S(2)}, u32[]{:S(2)}) collective-permute-start(f32[2,4,64,256]{3,2,1,0:T(8,128)} %get-tuple-element.21), channel_id=1, source_target_pairs={{4,0},{8,4},{12,8},{16,12},{20,16},{24,20},{28,24},{0,28},{5,1},{9... | collective-permute-start | bytes 1572872 | tf_op jit(solution)/shard_map/ppermute | solution.py:18
  84.8 0.2 collective-permute-done.6.from_left
  85.0 0.0 copy-start.4
  85.0 2.0 %collective-permute-done.7.from_right = f32[4,256,128]{2,1,0:T(8,128)S(1)} collective-permute-done((f32[4,256,128]{2,1,0:T(8,128)}, f32[4,256,128]{2,1,0:T(8,128)S(1)}, u32[]{:S(2)}, u32[]{:S(2)}) %collective-permute-start.7) | collective-permute-done | bytes 524320 | tf_op jit(solution)/shard_map/ppermute | solution.py:18
  87.0 0.0 copy-start.5
  87.1 18.1 %collective-permute-done.10.from_above = f32[2,4,64,256]{3,2,1,0:T(8,128)S(1)} collective-permute-done((f32[2,4,64,256]{3,2,1,0:T(8,128)}, f32[2,4,64,256]{3,2,1,0:T(8,128)S(1)}, u32[]{:S(2)}, u32[]{:S(2)}) %collective-permute-start.10) | collective-permute-done | bytes 524320 | tf_op jit(solution)/shard_map/ppermute | solution.py:18
  105.2 0.0 copy-start.6
  105.2 2.1 %collective-permute-done.11.from_below = f32[2,4,64,256]{3,2,1,0:T(8,128)S(1)} collective-permute-done((f32[2,4,64,256]{3,2,1,0:T(8,128)}, f32[2,4,64,256]{3,2,1,0:T(8,128)S(1)}, u32[]{:S(2)}, u32[]{:S(2)}) %collective-permute-start.11) | collective-permute-done | bytes 524320 | tf_op jit(solution)/shard_map/ppermute | solution.py:18
  107.3 0.0 copy-start.7
  107.3 0.0 copy-done.4
  107.3 0.0 copy-done.5
  107.3 0.0 copy-done.6
  107.3 0.8 copy-done.7
  108.1 5.3 %shard_map.80 = (f32[2,4,256,256]{3,2,1,0:T(8,128)}, f32[2,4,256,256]{3,2,1,0:T(8,128)}) custom-call(f32[2,4,256,256]{3,2,1,0:T(8,128)} %get-tuple-element.14.cells, f32[4,256,128]{2,1,0:T(8,128)} %copy-done.4, f32[4,256,128]{2,1,0:T(8,128)} %copy-done.5, f32[2,4,64,256]{3,2,1,0:T(8,128)} %copy-done.6, f32[2,4,64,256]{3,2,1,0:T(8,128)} %copy-done.7, ...), custom_call_target="tpu_custom_call" | custom-call | tf_op jit(solution)/shard_map/pallas_call | solution.py:365
  (2 shorter events, 0.1 us)
Async XLA Ops:
  0.6 6.6 %copy-start = (f32[2,4,256,256]{3,2,1,0:T(8,128)S(1)}, f32[2,4,256,256]{3,2,1,0:T(8,128)}, u32[]{:S(2)}) copy-start(f32[2,4,256,256]{3,2,1,0:T(8,128)} %objects.1) | copy-start | bytes 6291460
  2.1 25.9 %collective-permute-start.1 = (f32[2,4,64,256]{3,2,1,0:T(8,128)S(1)}, f32[2,4,64,256]{3,2,1,0:T(8,128)S(1)}, u32[]{:S(2)}, u32[]{:S(2)}) collective-permute-start(f32[2,4,64,256]{3,2,1,0:T(8,128)S(1)} %get-tuple-element.26), channel_id=1, source_target_pairs={{4,0},{8,4},{12,8},{16,12},{20,16},{24,20},{28,24},{0,28},{5,1},{9... | collective-permute-start | bytes 1572872 | tf_op jit(solution)/shard_map/ppermute | solution.py:18
  7.2 20.7 %collective-permute-start = (f32[2,4,64,256]{3,2,1,0:T(8,128)S(1)}, f32[2,4,64,256]{3,2,1,0:T(8,128)S(1)}, u32[]{:S(2)}, u32[]{:S(2)}) collective-permute-start(f32[2,4,64,256]{3,2,1,0:T(8,128)S(1)} %get-tuple-element.27), channel_id=1, source_target_pairs={{28,0},{0,4},{4,8},{8,12},{12,16},{16,20},{20,24},{24,28},{29,1},{... | collective-permute-start | bytes 1572872 | tf_op jit(solution)/shard_map/ppermute | solution.py:18
  7.8 29.6 %collective-permute-start.2 = (f32[4,256,128]{2,1,0:T(8,128)S(1)}, f32[4,256,128]{2,1,0:T(8,128)S(1)}, u32[]{:S(2)}, u32[]{:S(2)}) collective-permute-start(f32[4,256,128]{2,1,0:T(8,128)S(1)} %pad_maximum_fusion), channel_id=1, source_target_pairs={{1,0},{2,1},{3,2},{0,3},{5,4},{6,5},{7,6},{4,7},{9,8},{10,9},{11,1... | collective-permute-start | bytes 1572872 | tf_op jit(solution)/shard_map/ppermute | solution.py:18
  9.0 28.4 %collective-permute-start.3 = (f32[4,256,128]{2,1,0:T(8,128)S(1)}, f32[4,256,128]{2,1,0:T(8,128)S(1)}, u32[]{:S(2)}, u32[]{:S(2)}) collective-permute-start(f32[4,256,128]{2,1,0:T(8,128)S(1)} %pad_maximum_fusion.1), channel_id=1, source_target_pairs={{3,0},{0,1},{1,2},{2,3},{7,4},{4,5},{5,6},{6,7},{11,8},{8,9},{9,10... | collective-permute-start | bytes 1572872 | tf_op jit(solution)/shard_map/ppermute | solution.py:18
  28.0 4.7 %copy-start.1 = (f32[2,4,128,256]{3,2,1,0:T(8,128)}, f32[2,4,128,256]{3,2,1,0:T(8,128)S(1)}, u32[]{:S(2)}) copy-start(f32[2,4,128,256]{3,2,1,0:T(8,128)S(1)} %constant_dynamic-update-slice_fusion.edges) | copy-start | bytes 3145732
  28.0 3.7 %copy-start.8 = (f32[256,256]{1,0:T(8,128)S(1)}, f32[256,256]{1,0:T(8,128)}, u32[]{:S(2)}) copy-start(f32[256,256]{1,0:T(8,128)} %param.10) | copy-start | bytes 786436
  29.2 8.2 %collective-permute-start.4 = (f32[4,128,128]{2,1,0:T(8,128)}, f32[4,128,128]{2,1,0:T(8,128)S(1)}, u32[]{:S(2)}, u32[]{:S(2)}) collective-permute-start(f32[4,128,128]{2,1,0:T(8,128)} %pad_maximum_fusion.3), channel_id=1, source_target_pairs={{1,0},{2,1},{3,2},{0,3},{5,4},{6,5},{7,6},{4,7},{9,8},{10,9},{11,1... | collective-permute-start | bytes 786440 | tf_op jit(solution)/shard_map/ppermute | solution.py:18
  30.5 6.9 %collective-permute-start.5 = (f32[4,128,128]{2,1,0:T(8,128)}, f32[4,128,128]{2,1,0:T(8,128)}, u32[]{:S(2)}, u32[]{:S(2)}) collective-permute-start(f32[4,128,128]{2,1,0:T(8,128)} %pad_maximum_fusion.4), channel_id=1, source_target_pairs={{3,0},{0,1},{1,2},{2,3},{7,4},{4,5},{5,6},{6,7},{11,8},{8,9},{9,10... | collective-permute-start | bytes 786440 | tf_op jit(solution)/shard_map/ppermute | solution.py:18
  37.3 0.8 copy-start.2
  37.3 1.0 copy-start.3
  37.4 1.0 copy-start.9
  66.8 7.0 %collective-permute-start.8 = (f32[4,128,128]{2,1,0:T(8,128)}, f32[4,128,128]{2,1,0:T(8,128)S(1)}, u32[]{:S(2)}, u32[]{:S(2)}) collective-permute-start(f32[4,128,128]{2,1,0:T(8,128)} %get-tuple-element.18), channel_id=1, source_target_pairs={{3,0},{0,1},{1,2},{2,3},{7,4},{4,5},{5,6},{6,7},{11,8},{8,9},{9,10... | collective-permute-start | bytes 786440 | tf_op jit(solution)/shard_map/ppermute | solution.py:18
  68.3 9.1 %collective-permute-start.9 = (f32[4,128,128]{2,1,0:T(8,128)}, f32[4,128,128]{2,1,0:T(8,128)S(1)}, u32[]{:S(2)}, u32[]{:S(2)}) collective-permute-start(f32[4,128,128]{2,1,0:T(8,128)} %get-tuple-element.19), channel_id=1, source_target_pairs={{1,0},{2,1},{3,2},{0,3},{5,4},{6,5},{7,6},{4,7},{9,8},{10,9},{11,1... | collective-permute-start | bytes 786440 | tf_op jit(solution)/shard_map/ppermute | solution.py:18
  68.3 16.7 %collective-permute-start.6 = (f32[4,256,128]{2,1,0:T(8,128)}, f32[4,256,128]{2,1,0:T(8,128)S(1)}, u32[]{:S(2)}, u32[]{:S(2)}) collective-permute-start(f32[4,256,128]{2,1,0:T(8,128)} %get-tuple-element.15), channel_id=1, source_target_pairs={{3,0},{0,1},{1,2},{2,3},{7,4},{4,5},{5,6},{6,7},{11,8},{8,9},{9,10... | collective-permute-start | bytes 1572872 | tf_op jit(solution)/shard_map/ppermute | solution.py:18
  70.1 17.0 %collective-permute-start.7 = (f32[4,256,128]{2,1,0:T(8,128)}, f32[4,256,128]{2,1,0:T(8,128)S(1)}, u32[]{:S(2)}, u32[]{:S(2)}) collective-permute-start(f32[4,256,128]{2,1,0:T(8,128)} %get-tuple-element.16), channel_id=1, source_target_pairs={{1,0},{2,1},{3,2},{0,3},{5,4},{6,5},{7,6},{4,7},{9,8},{10,9},{11,1... | collective-permute-start | bytes 1572872 | tf_op jit(solution)/shard_map/ppermute | solution.py:18
  73.8 3.7 %copy-start.10 = (f32[4,128,128]{2,1,0:T(8,128)}, f32[4,128,128]{2,1,0:T(8,128)S(1)}, u32[]{:S(2)}) copy-start(f32[4,128,128]{2,1,0:T(8,128)S(1)} %collective-permute-done.8.from_left) | copy-start | bytes 786436
  77.4 0.7 copy-start.11
  80.6 24.6 %collective-permute-start.10 = (f32[2,4,64,256]{3,2,1,0:T(8,128)}, f32[2,4,64,256]{3,2,1,0:T(8,128)S(1)}, u32[]{:S(2)}, u32[]{:S(2)}) collective-permute-start(f32[2,4,64,256]{3,2,1,0:T(8,128)} %get-tuple-element.20), channel_id=1, source_target_pairs={{28,0},{0,4},{4,8},{8,12},{12,16},{16,20},{20,24},{24,28},{29,1},{... | collective-permute-start | bytes 1572872 | tf_op jit(solution)/shard_map/ppermute | solution.py:18
  82.8 24.4 %collective-permute-start.11 = (f32[2,4,64,256]{3,2,1,0:T(8,128)}, f32[2,4,64,256]{3,2,1,0:T(8,128)S(1)}, u32[]{:S(2)}, u32[]{:S(2)}) collective-permute-start(f32[2,4,64,256]{3,2,1,0:T(8,128)} %get-tuple-element.21), channel_id=1, source_target_pairs={{4,0},{8,4},{12,8},{16,12},{20,16},{24,20},{28,24},{0,28},{5,1},{9... | collective-permute-start | bytes 1572872 | tf_op jit(solution)/shard_map/ppermute | solution.py:18
  85.0 22.3 %copy-start.4 = (f32[4,256,128]{2,1,0:T(8,128)}, f32[4,256,128]{2,1,0:T(8,128)S(1)}, u32[]{:S(2)}) copy-start(f32[4,256,128]{2,1,0:T(8,128)S(1)} %collective-permute-done.6.from_left) | copy-start | bytes 1572868
  87.0 20.2 %copy-start.5 = (f32[4,256,128]{2,1,0:T(8,128)}, f32[4,256,128]{2,1,0:T(8,128)S(1)}, u32[]{:S(2)}) copy-start(f32[4,256,128]{2,1,0:T(8,128)S(1)} %collective-permute-done.7.from_right) | copy-start | bytes 1572868
  105.2 2.1 %copy-start.6 = (f32[2,4,64,256]{3,2,1,0:T(8,128)}, f32[2,4,64,256]{3,2,1,0:T(8,128)S(1)}, u32[]{:S(2)}) copy-start(f32[2,4,64,256]{3,2,1,0:T(8,128)S(1)} %collective-permute-done.10.from_above) | copy-start | bytes 1572868
  107.3 0.8 copy-start.7

commit v5 on v4

--- a/solution.py
+++ b/solution.py
@@ -82,14 +82,32 @@
     return dot_left(pair, value)
 
 
+def turned_over(value, width, source, target):
+    parts = [lax.slice_in_dim(value, at, at + width, axis=source) for at in range(0, value.shape[source], width)]
+    return jnp.concatenate(parts, target)
+
+
 def forward(re, im, pairs):
+    width = re.shape[0]
     re, im = forward_axis(re, im, 0, left_dot, pairs(0), pairs(1))
+    re, im = (turned_over(v, width, 1, 0) for v in (re, im))
     return forward_axis(re, im, 1, dot_right, pairs(2), pairs(3))
 
 
 def inverse(re, im, pairs):
+    width = re.shape[1]
     re, im = inverse_axis(re, im, 1, dot_right, pairs(0), pairs(1))
+    re, im = (turned_over(v, width, 0, 1) for v in (re, im))
     return inverse_axis(re, im, 0, left_dot, pairs(2), pairs(3))
+
+
+def hop(fields, phase_re, phase_im, pairs):
+    width = fields[0][0].shape[0]
+    re, im = forward(*(jnp.concatenate([f[c] for f in fields], 1) for c in range(2)), pairs)
+    re, im = complex_product(re, im, *(jnp.concatenate([p] * len(fields), 0) for p in (phase_re, phase_im)))
+    re, im = inverse(re, im, pairs)
+    spans = [slice(at, at + width) for at in range(0, re.shape[1], width)]
+    return [(re[:, span], im[:, span]) for span in spans]
 
 
 def by_parity(value, pairs):
@@ -200,9 +218,8 @@
     def onward(layer, carry):
         for k in range(count):
             cut_layer(k, layer)
-            re, im = forward(*leave(k, layer), pairs)
-            re, im = complex_product(re, im, phases[0], phases[1])
-            re, im = inverse(re, im, pairs)
+        fields = [leave(k, layer) for k in range(count)]
+        for k, (re, im) in enumerate(hop(fields, phases[0], phases[1], pairs)):
             waves[k, layer + 1, 0] = re
             waves[k, layer + 1, 1] = im
         return carry
@@ -232,13 +249,12 @@
 
     def backward(step, carry):
         layer = last - step
+        fields = []
         for k in range(count):
             back_re, back_im = waves[k, layer, 0], waves[k, layer, 1]
             slab_re, slab_im = windows[k, layer, 0], windows[k, layer, 1]
-            re, im = complex_product(back_re, back_im, slab_re, -slab_im)
-            re, im = forward(re, im, pairs)
-            re, im = complex_product(re, im, phases[0], -phases[1])
-            re, im = inverse(re, im, pairs)
+            fields.append(complex_product(back_re, back_im, slab_re, -slab_im))
+        for k, (re, im) in enumerate(hop(fields, phases[0], -phases[1], pairs)):
             record(k, layer - 1, re, im)
             waves[k, layer - 1, 0] = re
             waves[k, layer - 1, 1] = im

time: 114 us -> 111 us (0.974)
  Pallas kernels: 40 us -> 37.7 us
    pallas_call x1, Pallas kernels: 28.4 us -> 26.2 us  [on_device(): pl.pallas_call(step_kernel, out_shape=[like(v) for v in (object_slices, e...]
where the time goes in v5:
time: 111 us
  waiting for transfers between devices  47.6 us (43%)
  Pallas kernels  37.7 us (34%)
  starting transfers between devices  16.4 us (15%)
  local copies, waits for them, and re-layouts  5.51 us (5%)
  other arithmetic  2.98 us (3%)
    ppermute x12, waiting for transfers between devices, passed_along(): return lax.ppermute(block, axis, route)  47.6 us
    pallas_call x1, Pallas kernels, on_device(): pl.pallas_call(step_kernel, out_shape=[like(v) for v in (object_slices, e...  26.2 us
    ppermute x12, starting transfers between devices, passed_along(): return lax.ppermute(block, axis, route)  16.4 us
    pallas_call x1, Pallas kernels, on_device(): pl.pallas_call(final_kernel, grid=(layers,), out_shape=[like(cells), like...  5.29 us
    pallas_call x1, Pallas kernels, on_device(): pl.pallas_call(entry_kernel, out_shape=[like(measured), like(phase)], in_...  3.78 us
    unnamed x25, local copies, waits for them, and re-layouts  2.55 us
    pallas_call x1, Pallas kernels, on_device(): pl.pallas_call(edges_kernel, out_shape=[like(above), like(below)], in_spe...  2.47 us
  transfers between devices with their start and end apart: 12, of which 7 were waited for; matrix products, arithmetic and copies ran while one was open for 4% of the time, Pallas kernels for 6%

profile of v5, /device:TPU:1, one launch (start us, length us, event | category | flops | bytes accessed | tf_op | source)
XLA Modules:
  0.0 110.9 jit_solution(434427363219634772)
XLA Ops:
  0.6 0.0 copy-start
  0.6 1.4 %fusion = (f32[2,4,64,256]{3,2,1,0:T(8,128)S(1)}, f32[2,4,64,256]{3,2,1,0:T(8,128)S(1)}) fusion(f32[2,4,256,256]{3,2,1,0:T(8,128)} %objects.1), kind=kLoop, calls=%fused_computation.17 | loop fusion | bytes 2097152 | tf_op jit(solution)/shard_map/slice | solution.py:338
  2.1 5.1 %collective-permute-start.1 = (f32[2,4,64,256]{3,2,1,0:T(8,128)S(1)}, f32[2,4,64,256]{3,2,1,0:T(8,128)S(1)}, u32[]{:S(2)}, u32[]{:S(2)}) collective-permute-start(f32[2,4,64,256]{3,2,1,0:T(8,128)S(1)} %get-tuple-element.26), channel_id=1, source_target_pairs={{4,0},{8,4},{12,8},{16,12},{20,16},{24,20},{28,24},{0,28},{5,1},{9... | collective-permute-start | bytes 1572872 | tf_op jit(solution)/shard_map/ppermute | solution.py:18
  7.2 0.0 collective-permute-start
  7.2 0.0 copy-done
  7.2 0.3 slice_bitcast_fusion.1
  7.5 0.2 pad_maximum_fusion
  7.8 1.0 collective-permute-start.2
  8.8 0.2 pad_maximum_fusion.1
  9.0 1.2 %collective-permute-start.3 = (f32[4,256,128]{2,1,0:T(8,128)S(1)}, f32[4,256,128]{2,1,0:T(8,128)S(1)}, u32[]{:S(2)}, u32[]{:S(2)}) collective-permute-start(f32[4,256,128]{2,1,0:T(8,128)S(1)} %pad_maximum_fusion.1), channel_id=1, source_target_pairs={{3,0},{0,1},{1,2},{2,3},{7,4},{4,5},{5,6},{6,7},{11,8},{8,9},{9,10... | collective-permute-start | bytes 1572872 | tf_op jit(solution)/shard_map/ppermute | solution.py:18
  10.2 17.8 %collective-permute-done = f32[2,4,64,256]{3,2,1,0:T(8,128)S(1)} collective-permute-done((f32[2,4,64,256]{3,2,1,0:T(8,128)S(1)}, f32[2,4,64,256]{3,2,1,0:T(8,128)S(1)}, u32[]{:S(2)}, u32[]{:S(2)}) %collective-permute-start) | collective-permute-done | bytes 524320 | tf_op jit(solution)/shard_map/ppermute | solution.py:18
  28.0 0.0 collective-permute-done.1
  28.0 0.0 copy-start.1
  28.0 0.0 copy-start.8
  28.0 0.2 slice_bitcast_fusion.5
  28.3 0.9 pad_maximum_fusion.3
  29.2 0.5 collective-permute-start.4
  29.6 0.8 pad_maximum_fusion.4
  30.5 1.3 %collective-permute-start.5 = (f32[4,128,128]{2,1,0:T(8,128)}, f32[4,128,128]{2,1,0:T(8,128)}, u32[]{:S(2)}, u32[]{:S(2)}) collective-permute-start(f32[4,128,128]{2,1,0:T(8,128)} %pad_maximum_fusion.4), channel_id=1, source_target_pairs={{3,0},{0,1},{1,2},{2,3},{7,4},{4,5},{5,6},{6,7},{11,8},{8,9},{9,10... | collective-permute-start | bytes 786440 | tf_op jit(solution)/shard_map/ppermute | solution.py:18
  31.7 0.0 copy-done.8
  31.7 0.9 cosine_bitcast_fusion
  32.7 0.0 copy-done.1
  32.7 0.8 pad_maximum_fusion.2.phase
  33.5 3.8 %shard_map.77 = (f32[2,256,256]{2,1,0:T(8,128)}, f32[2,256,256]{2,1,0:T(8,128)}) custom-call(f32[2,256,256]{2,1,0:T(8,128)} %bitcast.23, f32[2,256,256]{2,1,0:T(8,128)} %pad_maximum_fusion.2.phase, bf16[2,6,256,256]{3,2,1,0:T(8,128)(2,1)} %constant.2.clone.tables), custom_call_target="tpu_custom_call" | custom-call | flops 1073741824 | bytes 4194304 | tf_op jit(solution)/shard_map/pallas_call | solution.py:330
  37.3 0.0 collective-permute-done.2.right
  37.3 0.0 copy-start.2
  37.3 0.0 collective-permute-done.3.left
  37.3 0.0 copy-start.3
  37.3 0.0 collective-permute-done.4.right_ends
  37.4 0.0 copy-start.9
  37.4 0.0 collective-permute-done.5.left_ends
  37.4 0.7 copy-done.2
  38.1 0.1 copy-done.3
  38.3 0.1 copy-done.9
  38.4 26.2 %shard_map.78 = (f32[2,4,256,256]{3,2,1,0:T(8,128)}, f32[2,4,128,256]{3,2,1,0:T(8,128)}, f32[4,256,128]{2,1,0:T(8,128)}, f32[4,256,128]{2,1,0:T(8,128)}, f32[4,128,128]{2,1,0:T(8,128)}, /*index=5*/f32[4,128,128]{2,1,0:T(8,128)}) custom-call(s32[2,2]{1,0:T(2,128)} %bitcast.22, f32[2,4,256,256]{3,2,1,0:T(8,128)} %objects.1, f32[2,4,128,256]{3,2,1,0:T(8,128)} %copy-done.1, ...), custom_call_target="tpu_custom_call" | custom-call | tf_op jit(solution)/shard_map/pallas_call | solution.py:348
  64.5 1.4 %collective-permute-start.8 = (f32[4,128,128]{2,1,0:T(8,128)}, f32[4,128,128]{2,1,0:T(8,128)S(1)}, u32[]{:S(2)}, u32[]{:S(2)}) collective-permute-start(f32[4,128,128]{2,1,0:T(8,128)} %get-tuple-element.18), channel_id=1, source_target_pairs={{3,0},{0,1},{1,2},{2,3},{7,4},{4,5},{5,6},{6,7},{11,8},{8,9},{9,10... | collective-permute-start | bytes 786440 | tf_op jit(solution)/shard_map/ppermute | solution.py:18
  66.0 0.0 collective-permute-start.9
  66.0 1.7 %collective-permute-start.6 = (f32[4,256,128]{2,1,0:T(8,128)}, f32[4,256,128]{2,1,0:T(8,128)S(1)}, u32[]{:S(2)}, u32[]{:S(2)}) collective-permute-start(f32[4,256,128]{2,1,0:T(8,128)} %get-tuple-element.15), channel_id=1, source_target_pairs={{3,0},{0,1},{1,2},{2,3},{7,4},{4,5},{5,6},{6,7},{11,8},{8,9},{9,10... | collective-permute-start | bytes 1572872 | tf_op jit(solution)/shard_map/ppermute | solution.py:18
  67.7 0.0 collective-permute-start.7
  67.7 3.8 %collective-permute-done.8.from_left = f32[4,128,128]{2,1,0:T(8,128)S(1)} collective-permute-done((f32[4,128,128]{2,1,0:T(8,128)}, f32[4,128,128]{2,1,0:T(8,128)S(1)}, u32[]{:S(2)}, u32[]{:S(2)}) %collective-permute-start.8) | collective-permute-done | bytes 262176 | tf_op jit(solution)/shard_map/ppermute | solution.py:18
  71.5 0.0 copy-start.10
  71.5 3.6 %collective-permute-done.9.from_right = f32[4,128,128]{2,1,0:T(8,128)S(1)} collective-permute-done((f32[4,128,128]{2,1,0:T(8,128)}, f32[4,128,128]{2,1,0:T(8,128)S(1)}, u32[]{:S(2)}, u32[]{:S(2)}) %collective-permute-start.9) | collective-permute-done | bytes 262176 | tf_op jit(solution)/shard_map/ppermute | solution.py:18
  75.1 0.0 copy-start.11
  75.1 0.0 copy-done.10
  75.1 0.7 copy-done.11
  75.8 2.5 %shard_map.79 = (f32[2,4,64,256]{3,2,1,0:T(8,128)}, f32[2,4,64,256]{3,2,1,0:T(8,128)}) custom-call(f32[2,4,128,256]{3,2,1,0:T(8,128)} %get-tuple-element.17.edges, f32[4,128,128]{2,1,0:T(8,128)} %copy-done.10, f32[4,128,128]{2,1,0:T(8,128)} %copy-done.11), custom_call_target="tpu_custom_call" | custom-call | tf_op jit(solution)/shard_map/pallas_call | solution.py:368
  78.2 2.3 %collective-permute-start.10 = (f32[2,4,64,256]{3,2,1,0:T(8,128)}, f32[2,4,64,256]{3,2,1,0:T(8,128)S(1)}, u32[]{:S(2)}, u32[]{:S(2)}) collective-permute-start(f32[2,4,64,256]{3,2,1,0:T(8,128)} %get-tuple-element.20), channel_id=1, source_target_pairs={{28,0},{0,4},{4,8},{8,12},{12,16},{16,20},{20,24},{24,28},{29,1},{... | collective-permute-start | bytes 1572872 | tf_op jit(solution)/shard_map/ppermute | solution.py:18
  80.5 1.9 %collective-permute-start.11 = (f32[2,4,64,256]{3,2,1,0:T(8,128)}, f32[2,4,64,256]{3,2,1,0:T(8,128)S(1)}, u32[]{:S(2)}, u32[]{:S(2)}) collective-permute-start(f32[2,4,64,256]{3,2,1,0:T(8,128)} %get-tuple-element.21), channel_id=1, source_target_pairs={{4,0},{8,4},{12,8},{16,12},{20,16},{24,20},{28,24},{0,28},{5,1},{9... | collective-permute-start | bytes 1572872 | tf_op jit(solution)/shard_map/ppermute | solution.py:18
  82.4 0.3 collective-permute-done.6.from_left
  82.7 0.0 copy-start.4
  82.7 1.9 %collective-permute-done.7.from_right = f32[4,256,128]{2,1,0:T(8,128)S(1)} collective-permute-done((f32[4,256,128]{2,1,0:T(8,128)}, f32[4,256,128]{2,1,0:T(8,128)S(1)}, u32[]{:S(2)}, u32[]{:S(2)}) %collective-permute-start.7) | collective-permute-done | bytes 524320 | tf_op jit(solution)/shard_map/ppermute | solution.py:18
  84.6 0.0 copy-start.5
  84.6 18.1 %collective-permute-done.10.from_above = f32[2,4,64,256]{3,2,1,0:T(8,128)S(1)} collective-permute-done((f32[2,4,64,256]{3,2,1,0:T(8,128)}, f32[2,4,64,256]{3,2,1,0:T(8,128)S(1)}, u32[]{:S(2)}, u32[]{:S(2)}) %collective-permute-start.10) | collective-permute-done | bytes 524320 | tf_op jit(solution)/shard_map/ppermute | solution.py:18
  102.7 0.0 copy-start.6
  102.7 2.1 %collective-permute-done.11.from_below = f32[2,4,64,256]{3,2,1,0:T(8,128)S(1)} collective-permute-done((f32[2,4,64,256]{3,2,1,0:T(8,128)}, f32[2,4,64,256]{3,2,1,0:T(8,128)S(1)}, u32[]{:S(2)}, u32[]{:S(2)}) %collective-permute-start.11) | collective-permute-done | bytes 524320 | tf_op jit(solution)/shard_map/ppermute | solution.py:18
  104.8 0.0 copy-start.7
  104.8 0.0 copy-done.4
  104.8 0.0 copy-done.5
  104.8 0.0 copy-done.6
  104.8 0.8 copy-done.7
  105.6 5.3 %shard_map.80 = (f32[2,4,256,256]{3,2,1,0:T(8,128)}, f32[2,4,256,256]{3,2,1,0:T(8,128)}) custom-call(f32[2,4,256,256]{3,2,1,0:T(8,128)} %get-tuple-element.14.cells, f32[4,256,128]{2,1,0:T(8,128)} %copy-done.4, f32[4,256,128]{2,1,0:T(8,128)} %copy-done.5, f32[2,4,64,256]{3,2,1,0:T(8,128)} %copy-done.6, f32[2,4,64,256]{3,2,1,0:T(8,128)} %copy-done.7, ...), custom_call_target="tpu_custom_call" | custom-call | tf_op jit(solution)/shard_map/pallas_call | solution.py:381
  (2 shorter events, 0.1 us)
Async XLA Ops:
  0.6 6.6 %copy-start = (f32[2,4,256,256]{3,2,1,0:T(8,128)S(1)}, f32[2,4,256,256]{3,2,1,0:T(8,128)}, u32[]{:S(2)}) copy-start(f32[2,4,256,256]{3,2,1,0:T(8,128)} %objects.1) | copy-start | bytes 6291460
  2.1 25.9 %collective-permute-start.1 = (f32[2,4,64,256]{3,2,1,0:T(8,128)S(1)}, f32[2,4,64,256]{3,2,1,0:T(8,128)S(1)}, u32[]{:S(2)}, u32[]{:S(2)}) collective-permute-start(f32[2,4,64,256]{3,2,1,0:T(8,128)S(1)} %get-tuple-element.26), channel_id=1, source_target_pairs={{4,0},{8,4},{12,8},{16,12},{20,16},{24,20},{28,24},{0,28},{5,1},{9... | collective-permute-start | bytes 1572872 | tf_op jit(solution)/shard_map/ppermute | solution.py:18
  7.2 20.7 %collective-permute-start = (f32[2,4,64,256]{3,2,1,0:T(8,128)S(1)}, f32[2,4,64,256]{3,2,1,0:T(8,128)S(1)}, u32[]{:S(2)}, u32[]{:S(2)}) collective-permute-start(f32[2,4,64,256]{3,2,1,0:T(8,128)S(1)} %get-tuple-element.27), channel_id=1, source_target_pairs={{28,0},{0,4},{4,8},{8,12},{12,16},{16,20},{20,24},{24,28},{29,1},{... | collective-permute-start | bytes 1572872 | tf_op jit(solution)/shard_map/ppermute | solution.py:18
  7.8 29.6 %collective-permute-start.2 = (f32[4,256,128]{2,1,0:T(8,128)S(1)}, f32[4,256,128]{2,1,0:T(8,128)S(1)}, u32[]{:S(2)}, u32[]{:S(2)}) collective-permute-start(f32[4,256,128]{2,1,0:T(8,128)S(1)} %pad_maximum_fusion), channel_id=1, source_target_pairs={{1,0},{2,1},{3,2},{0,3},{5,4},{6,5},{7,6},{4,7},{9,8},{10,9},{11,1... | collective-permute-start | bytes 1572872 | tf_op jit(solution)/shard_map/ppermute | solution.py:18
  9.0 28.4 %collective-permute-start.3 = (f32[4,256,128]{2,1,0:T(8,128)S(1)}, f32[4,256,128]{2,1,0:T(8,128)S(1)}, u32[]{:S(2)}, u32[]{:S(2)}) collective-permute-start(f32[4,256,128]{2,1,0:T(8,128)S(1)} %pad_maximum_fusion.1), channel_id=1, source_target_pairs={{3,0},{0,1},{1,2},{2,3},{7,4},{4,5},{5,6},{6,7},{11,8},{8,9},{9,10... | collective-permute-start | bytes 1572872 | tf_op jit(solution)/shard_map/ppermute | solution.py:18
  28.0 4.7 %copy-start.1 = (f32[2,4,128,256]{3,2,1,0:T(8,128)}, f32[2,4,128,256]{3,2,1,0:T(8,128)S(1)}, u32[]{:S(2)}) copy-start(f32[2,4,128,256]{3,2,1,0:T(8,128)S(1)} %constant_dynamic-update-slice_fusion.edges) | copy-start | bytes 3145732
  28.0 3.7 %copy-start.8 = (f32[256,256]{1,0:T(8,128)S(1)}, f32[256,256]{1,0:T(8,128)}, u32[]{:S(2)}) copy-start(f32[256,256]{1,0:T(8,128)} %param.10) | copy-start | bytes 786436
  29.2 8.2 %collective-permute-start.4 = (f32[4,128,128]{2,1,0:T(8,128)}, f32[4,128,128]{2,1,0:T(8,128)S(1)}, u32[]{:S(2)}, u32[]{:S(2)}) collective-permute-start(f32[4,128,128]{2,1,0:T(8,128)} %pad_maximum_fusion.3), channel_id=1, source_target_pairs={{1,0},{2,1},{3,2},{0,3},{5,4},{6,5},{7,6},{4,7},{9,8},{10,9},{11,1... | collective-permute-start | bytes 786440 | tf_op jit(solution)/shard_map/ppermute | solution.py:18
  30.5 6.9 %collective-permute-start.5 = (f32[4,128,128]{2,1,0:T(8,128)}, f32[4,128,128]{2,1,0:T(8,128)}, u32[]{:S(2)}, u32[]{:S(2)}) collective-permute-start(f32[4,128,128]{2,1,0:T(8,128)} %pad_maximum_fusion.4), channel_id=1, source_target_pairs={{3,0},{0,1},{1,2},{2,3},{7,4},{4,5},{5,6},{6,7},{11,8},{8,9},{9,10... | collective-permute-start | bytes 786440 | tf_op jit(solution)/shard_map/ppermute | solution.py:18
  37.3 0.8 copy-start.2
  37.3 1.0 copy-start.3
  37.4 1.0 copy-start.9
  64.5 7.0 %collective-permute-start.8 = (f32[4,128,128]{2,1,0:T(8,128)}, f32[4,128,128]{2,1,0:T(8,128)S(1)}, u32[]{:S(2)}, u32[]{:S(2)}) collective-permute-start(f32[4,128,128]{2,1,0:T(8,128)} %get-tuple-element.18), channel_id=1, source_target_pairs={{3,0},{0,1},{1,2},{2,3},{7,4},{4,5},{5,6},{6,7},{11,8},{8,9},{9,10... | collective-permute-start | bytes 786440 | tf_op jit(solution)/shard_map/ppermute | solution.py:18
  66.0 9.1 %collective-permute-start.9 = (f32[4,128,128]{2,1,0:T(8,128)}, f32[4,128,128]{2,1,0:T(8,128)S(1)}, u32[]{:S(2)}, u32[]{:S(2)}) collective-permute-start(f32[4,128,128]{2,1,0:T(8,128)} %get-tuple-element.19), channel_id=1, source_target_pairs={{1,0},{2,1},{3,2},{0,3},{5,4},{6,5},{7,6},{4,7},{9,8},{10,9},{11,1... | collective-permute-start | bytes 786440 | tf_op jit(solution)/shard_map/ppermute | solution.py:18
  66.0 16.8 %collective-permute-start.6 = (f32[4,256,128]{2,1,0:T(8,128)}, f32[4,256,128]{2,1,0:T(8,128)S(1)}, u32[]{:S(2)}, u32[]{:S(2)}) collective-permute-start(f32[4,256,128]{2,1,0:T(8,128)} %get-tuple-element.15), channel_id=1, source_target_pairs={{3,0},{0,1},{1,2},{2,3},{7,4},{4,5},{5,6},{6,7},{11,8},{8,9},{9,10... | collective-permute-start | bytes 1572872 | tf_op jit(solution)/shard_map/ppermute | solution.py:18
  67.7 16.9 %collective-permute-start.7 = (f32[4,256,128]{2,1,0:T(8,128)}, f32[4,256,128]{2,1,0:T(8,128)S(1)}, u32[]{:S(2)}, u32[]{:S(2)}) collective-permute-start(f32[4,256,128]{2,1,0:T(8,128)} %get-tuple-element.16), channel_id=1, source_target_pairs={{1,0},{2,1},{3,2},{0,3},{5,4},{6,5},{7,6},{4,7},{9,8},{10,9},{11,1... | collective-permute-start | bytes 1572872 | tf_op jit(solution)/shard_map/ppermute | solution.py:18
  71.5 3.6 %copy-start.10 = (f32[4,128,128]{2,1,0:T(8,128)}, f32[4,128,128]{2,1,0:T(8,128)S(1)}, u32[]{:S(2)}) copy-start(f32[4,128,128]{2,1,0:T(8,128)S(1)} %collective-permute-done.8.from_left) | copy-start | bytes 786436
  75.1 0.7 copy-start.11
  78.2 24.5 %collective-permute-start.10 = (f32[2,4,64,256]{3,2,1,0:T(8,128)}, f32[2,4,64,256]{3,2,1,0:T(8,128)S(1)}, u32[]{:S(2)}, u32[]{:S(2)}) collective-permute-start(f32[2,4,64,256]{3,2,1,0:T(8,128)} %get-tuple-element.20), channel_id=1, source_target_pairs={{28,0},{0,4},{4,8},{8,12},{12,16},{16,20},{20,24},{24,28},{29,1},{... | collective-permute-start | bytes 1572872 | tf_op jit(solution)/shard_map/ppermute | solution.py:18
  80.5 24.3 %collective-permute-start.11 = (f32[2,4,64,256]{3,2,1,0:T(8,128)}, f32[2,4,64,256]{3,2,1,0:T(8,128)S(1)}, u32[]{:S(2)}, u32[]{:S(2)}) collective-permute-start(f32[2,4,64,256]{3,2,1,0:T(8,128)} %get-tuple-element.21), channel_id=1, source_target_pairs={{4,0},{8,4},{12,8},{16,12},{20,16},{24,20},{28,24},{0,28},{5,1},{9... | collective-permute-start | bytes 1572872 | tf_op jit(solution)/shard_map/ppermute | solution.py:18
  82.7 22.1 %copy-start.4 = (f32[4,256,128]{2,1,0:T(8,128)}, f32[4,256,128]{2,1,0:T(8,128)S(1)}, u32[]{:S(2)}) copy-start(f32[4,256,128]{2,1,0:T(8,128)S(1)} %collective-permute-done.6.from_left) | copy-start | bytes 1572868
  84.6 20.2 %copy-start.5 = (f32[4,256,128]{2,1,0:T(8,128)}, f32[4,256,128]{2,1,0:T(8,128)S(1)}, u32[]{:S(2)}) copy-start(f32[4,256,128]{2,1,0:T(8,128)S(1)} %collective-permute-done.7.from_right) | copy-start | bytes 1572868
  102.7 2.1 %copy-start.6 = (f32[2,4,64,256]{3,2,1,0:T(8,128)}, f32[2,4,64,256]{3,2,1,0:T(8,128)S(1)}, u32[]{:S(2)}) copy-start(f32[2,4,64,256]{3,2,1,0:T(8,128)S(1)} %collective-permute-done.10.from_above) | copy-start | bytes 1572868
  104.8 0.8 copy-start.7
